TPU v7x, 32 devices: a whole 2x2x4 slice. The times are simulated.
32 devices in a mesh: freq: 4 (over x, core), grid: 8 (over z, y).
Axes of the slice: x: 2, y: 2, z: 4, core: 2. Of those that a mesh axis runs over, the one named last changes fastest.
Arguments:
- series: bfloat16 [128, 1024, 256], P('freq', 'grid'), may hold values from -8 to 8
- bins: int32 [4], replicated, may hold values from 32 to 127
- sensor_coords: int32 [3, 1024], replicated, may hold values from 0 to 63
- grid_coords: int32 [3, 2048], P(None, 'grid'), may hold values from 0 to 63
Outputs:
- bin_power: float32 [4, 2048], P('freq', 'grid')
- power: float32 [2048], P('grid')
All inputs are finite; a program needn't handle non-finite values.
Results may differ from a plain program's by a relative error of at most 0.0015.
Values may be sent and summed in bfloat16 or wider, within the bound.
No kernel may reach another device: no remote copies, remote signals or barrier semaphores. Data moves between devices by JAX's collectives and lax.ppermute only.
A program may use at most 64 MiB of HBM per device.

v0:
```python
import math

import jax
import jax.numpy as jnp
from jax import lax
from jax.sharding import PartitionSpec as P


def on_device(series, bins, sensor_coords, grid_coords):
    snap_local, channel_local, samples = series.shape
    all_bins = bins.shape[0]
    sample_index = jnp.arange(samples, dtype=jnp.int32)
    cycles = bins[:, None] * sample_index[None, :] % samples
    angles = 2.0 * math.pi / samples * cycles.astype(jnp.float32)
    scaling = (samples / 2.0) ** (-0.5)
    transform_table = jnp.stack([jnp.cos(angles) * scaling, -jnp.sin(angles) * scaling], 1)
    transform_table = transform_table.astype(jnp.bfloat16).reshape(2 * all_bins, samples)
    spectra = jnp.einsum("kt,sct->kcs", transform_table, series, preferred_element_type=jnp.float32)
    spectra = spectra.astype(jnp.bfloat16).reshape(all_bins, 2, channel_local, snap_local)
    regrouped = lax.all_to_all(spectra, "freq", split_axis=0, concat_axis=3, tiled=True)
    bin_count = regrouped.shape[0]
    snap_total = regrouped.shape[3]
    gathered = lax.all_gather(regrouped, "grid", axis=2, tiled=True)
    channels = gathered.shape[2]
    local_bins = lax.dynamic_slice_in_dim(bins, lax.axis_index("freq") * bin_count, bin_count)
    squared = jnp.zeros((grid_coords.shape[1], channels), jnp.int32)
    for axis_pos in range(3):
        offsets = grid_coords[axis_pos][:, None] - sensor_coords[axis_pos][None, :]
        squared = squared + offsets * offsets
    distance = jnp.sqrt(squared.astype(jnp.float32))
    phases = (
        4.0 * math.pi / samples * local_bins.astype(jnp.float32)[:, None, None] * distance[None]
    )
    amplitude = channels ** (-0.5)
    beam_real = (jnp.cos(phases) * amplitude).astype(jnp.bfloat16)
    beam_imag = (-jnp.sin(phases) * amplitude).astype(jnp.bfloat16)
    spec_real = gathered[:, 0]
    spec_imag = gathered[:, 1]

    def product(left, right):
        return jnp.einsum("fgc,fcs->fgs", left, right, preferred_element_type=jnp.float32)

    out_real = product(beam_real, spec_real) + product(beam_imag, spec_imag)
    out_imag = product(beam_real, spec_imag) - product(beam_imag, spec_real)
    bin_power = jnp.sum(out_real * out_real + out_imag * out_imag, 2) / snap_total
    summed = lax.psum(jnp.sum(bin_power, 0), "freq")
    power = summed / (bin_count * lax.axis_size("freq"))
    return (bin_power, power)


def solution(mesh):
    return jax.shard_map(
        on_device,
        mesh=mesh,
        in_specs=(P("freq", "grid", None), P(), P(), P(None, "grid")),
        out_specs=(P("freq", "grid"), P("grid")),
        check_vma=False,
    )
```

profile of v0, /device:TPU:0, one launch (start us, length us, event | category | flops | bytes accessed | tf_op | source)
XLA Modules:
  0.0 64.2 jit_solution(2394044324553024529)
XLA Ops:
  0.6 0.0 copy-start
  0.6 0.0 copy-start.4
  0.7 0.0 copy-start.1
  0.7 0.0 copy-start.3
  0.7 0.9 %multiply_convert_fusion.3 = (bf16[4,1,256]{2,0,1:T(4,128)(2,1)S(1)}, bf16[4,1,256]{2,0,1:T(4,128)(2,1)S(1)}) fusion(s32[4]{0:T(128)} %param.5), kind=kLoop, calls=%fused_computation.24 | loop fusion | flops 19456 | bytes 4112 | tf_op jit(solution)/shard_map/convert
  1.6 0.6 copy-done
  2.3 0.6 convolution_convert_fusion
  2.9 0.6 %copy.12 = bf16[4,2,128,32]{2,3,1,0:T(8,128)(2,1)} copy(bf16[4,2,128,32]{2,1,0,3:T(2,128)(2,1)S(1)} %bitcast.34) | data formatting | bytes 131072 | tf_op jit(solution)/shard_map/reshape | solution.py:19
  3.6 4.2 %all-to-all-start = ((bf16[4,2,128,32]{2,3,1,0:T(8,128)(2,1)}), bf16[4,2,128,32]{2,3,1,0:T(8,128)(2,1)S(1)}, u32[]{:S(2)}, u32[]{:S(2)}) async-start(bf16[4,2,128,32]{2,3,1,0:T(8,128)(2,1)} %copy.12), calls=%async_computation | async-start | bytes 131072 | tf_op jit(solution)/shard_map/all_to_all | solution.py:20
  7.8 0.0 copy-done.1
  7.8 0.0 copy-done.3
  7.8 0.0 copy-done.4
  7.9 0.6 dynamic_slice.3
  9.1 2.8 %all-to-all-done = bf16[4,2,128,32]{2,3,1,0:T(8,128)(2,1)S(1)} async-done(((bf16[4,2,128,32]{2,3,1,0:T(8,128)(2,1)}), bf16[4,2,128,32]{2,3,1,0:T(8,128)(2,1)S(1)}, u32[]{:S(2)}, u32[]{:S(2)}) %all-to-all-start) | async-done | bytes 65568 | tf_op jit(solution)/shard_map/all_to_all | solution.py:20
  11.9 28.8 %all_gather.3 = bf16[1,2,1024,128]{2,3,1,0:T(8,128)(2,1)S(1)} all-gather(bf16[1,2,128,128]{2,3,1,0:T(8,128)(2,1)S(1)} %bitcast.35), channel_id=1, replica_groups=mesh['freq'=4,'grid'=8] {'grid'}, dimensions={2}, use_global_device_ids=true | all-gather | bytes 589824 | tf_op jit(solution)/shard_map/all_gather | solution.py:23
  40.7 4.2 %fusion.8 = f32[256,128]{0,1:T(8,128)S(1)} fusion(s32[1024]{0:T(1024)S(1)} %bitcast.41, s32[256]{0:T(256)S(1)} %bitcast.53, s32[1024]{0:T(1024)S(1)} %bitcast.45, s32[256]{0:T(256)S(1)} %bitcast.57, s32[1024]{0:T(1024)S(1)} %bitcast.37, s32[256]{0:T(256)S(1)} %bitcast.49, f32[]{:T(128)} %bitcast, bf16[1,2,1024,128]{2,3,1,0:T(8,128)(2,1)S(1)} %all_gather.3), kind=kOutput, calls=%fused_computation.12 | convolution fusion | flops 70254592 | bytes 408580 | tf_op jit(solution)/shard_map/fgc,fcs->fgs/dot_general | solution.py:41
  44.9 4.2 %fusion.10 = f32[256,128]{0,1:T(8,128)S(1)} fusion(s32[1024]{0:T(1024)S(1)} %bitcast.42, s32[256]{0:T(256)S(1)} %bitcast.54, s32[1024]{0:T(1024)S(1)} %bitcast.46, s32[256]{0:T(256)S(1)} %bitcast.58, s32[1024]{0:T(1024)S(1)} %bitcast.38, s32[256]{0:T(256)S(1)} %bitcast.50, f32[]{:T(128)} %bitcast, bf16[1,2,1024,128]{2,3,1,0:T(8,128)(2,1)S(1)} %all_gather.3), kind=kOutput, calls=%fused_computation.13 | convolution fusion | flops 70254592 | bytes 408580 | tf_op jit(solution)/shard_map/fgc,fcs->fgs/dot_general | solution.py:41
  49.1 4.4 %fusion.2 = f32[256,128]{0,1:T(8,128)S(1)} fusion(f32[256,128]{0,1:T(8,128)S(1)} %fusion.10, s32[1024]{0:T(1024)S(1)} %bitcast.43, s32[256]{0:T(256)S(1)} %bitcast.55, s32[1024]{0:T(1024)S(1)} %bitcast.47, s32[256]{0:T(256)S(1)} %bitcast.59, s32[1024]{0:T(1024)S(1)} %bitcast.39, s32[256]{0:T(256)S(1)} %bitcast.51, f32[]{:T(128)} %bitcast, ...), kind=kOutput, calls=%fused_computation.4 | convolution fusion | flops 70582272 | bytes 539652 | tf_op jit(solution)/shard_map/fgc,fcs->fgs/dot_general | solution.py:41
  53.6 4.3 %fusion.3 = f32[256]{0:T(256)S(1)} fusion(f32[256,128]{0,1:T(8,128)S(1)} %fusion.2, f32[256,128]{0,1:T(8,128)S(1)} %fusion.8, s32[1024]{0:T(1024)S(1)} %bitcast.44, s32[256]{0:T(256)S(1)} %bitcast.56, s32[1024]{0:T(1024)S(1)} %bitcast.48, s32[256]{0:T(256)S(1)} %bitcast.60, s32[1024]{0:T(1024)S(1)} %bitcast.40, s32[256]{0:T(256)S(1)} %bitcast.52, f32[]{:T(128)} %bitcast, ...), kind=kOutput, calls=%fused_computation.6 | convolution fusion | flops 70647552 | bytes 540676 | tf_op jit(solution)/shard_map/fgc,fcs->fgs/dot_general | solution.py:41
  57.8 0.0 copy-start.2
  57.9 5.8 %psum.7 = f32[256]{0:T(256)S(1)} all-reduce(f32[256]{0:T(256)S(1)} %broadcast_multiply_fusion.1), channel_id=1, replica_groups=mesh['freq'=4,'grid'=8] {'freq'}, use_global_device_ids=true, to_apply=%region_1.2 | all-reduce | flops 256 | bytes 2048 | tf_op jit(solution)/shard_map/psum | solution.py:46
  63.6 0.6 broadcast_multiply_fusion
  64.2 0.0 copy-done.2
  (7 shorter events, 0.1 us)
Async XLA Ops:
  0.6 1.6 %copy-start = (bf16[32,128,256]{2,1,0:T(8,128)(2,1)S(1)}, bf16[32,128,256]{2,1,0:T(8,128)(2,1)}, u32[]{:S(2)}) copy-start(bf16[32,128,256]{2,1,0:T(8,128)(2,1)} %param.4) | copy-start | bytes 6291460
  0.6 7.2 %copy-start.4 = (s32[4]{0:T(128)S(1)}, s32[4]{0:T(128)}, u32[]{:S(2)}) copy-start(s32[4]{0:T(128)} %param.5) | copy-start | bytes 52
  0.7 7.1 %copy-start.1 = (s32[3,1024]{1,0:T(4,128)S(1)}, s32[3,1024]{1,0:T(4,128)}, u32[]{:S(2)}) copy-start(s32[3,1024]{1,0:T(4,128)} %param.6) | copy-start | bytes 36868
  0.7 7.2 %copy-start.3 = (s32[3,256]{1,0:T(4,128)S(1)}, s32[3,256]{1,0:T(4,128)}, u32[]{:S(2)}) copy-start(s32[3,256]{1,0:T(4,128)} %param.7) | copy-start | bytes 9220
  3.6 8.4 %all-to-all-start = ((bf16[4,2,128,32]{2,3,1,0:T(8,128)(2,1)}), bf16[4,2,128,32]{2,3,1,0:T(8,128)(2,1)S(1)}, u32[]{:S(2)}, u32[]{:S(2)}) async-start(bf16[4,2,128,32]{2,3,1,0:T(8,128)(2,1)} %copy.12), calls=%async_computation | async-start | bytes 131072 | tf_op jit(solution)/shard_map/all_to_all | solution.py:20
  57.8 6.3 %copy-start.2 = (f32[256]{0:T(256)}, f32[256]{0:T(256)S(1)}, u32[]{:S(2)}) copy-start(f32[256]{0:T(256)S(1)} %broadcast_multiply_fusion.1) | copy-start | bytes 3076
where the time goes:
time: 64.5 us; the launch traced here: 64.2 us
  blocking collectives  34.5 us (53%)
  matrix products  17.7 us (27%)
  starting transfers between devices  4.24 us (7%)
  waiting for transfers between devices  2.83 us (4%)
  local copies, waits for them, and re-layouts  1.93 us (3%)
  other arithmetic  1.51 us (2%)
  between operations  1.41 us (2%)
    all_gather x1, blocking collectives, on_device(): gathered = lax.all_gather(regrouped, 'grid', axis=2, tiled=True)  28.8 us
    dot_general x4, matrix products, product(): jnp.einsum('fgc,fcs->fgs', left, right, preferred_element_type=jnp.float32)  17.1 us
    psum x1, blocking collectives, on_device(): summed = lax.psum(jnp.sum(bin_power, 0), 'freq')  5.76 us
    all_to_all x1, starting transfers between devices, on_device(): lax.all_to_all(spectra, 'freq', split_axis=0, concat_axis=3, tiled=True)  4.24 us
    all_to_all x1, waiting for transfers between devices, on_device(): lax.all_to_all(spectra, 'freq', split_axis=0, concat_axis=3, tiled=True)  2.83 us
  transfers between devices with their start and end apart: 1, of which 1 were waited for; matrix products, arithmetic and copies ran while one was open for 1% of the time, Pallas kernels for 0%

commit v1 on v0

v1 whole, which is shorter than its diff:
```python
import math

import jax
import jax.numpy as jnp
from jax import lax
from jax.sharding import PartitionSpec as P


def turns_cos_sin(turns):
    rest = turns - jnp.round(turns)
    x = rest * math.pi
    z = x * x
    s = x * (1.0 + z * (-1 / 6 + z * (1 / 120 + z * (-1 / 5040 + z * (1 / 362880 - z / 39916800)))))
    c = 1.0 + z * (-0.5 + z * (1 / 24 + z * (-1 / 720 + z * (1 / 40320 + z * (-1 / 3628800 + z / 479001600)))))
    return 1.0 - 2.0 * s * s, 2.0 * s * c


def on_device(series, bins, sensor_coords, grid_coords):
    snap_local, channel_local, samples = series.shape
    all_bins = bins.shape[0]
    channels = sensor_coords.shape[1]
    grid_local = grid_coords.shape[1]
    freq_size = lax.axis_size("freq")
    grid_size = lax.axis_size("grid")
    snap_total = snap_local * freq_size
    half = all_bins // 2
    place = lax.axis_index("grid")
    side = place % 2

    def swap(value, axis, mask):
        size = lax.axis_size(axis)
        return lax.ppermute(value, axis, [(i, i ^ mask) for i in range(size)])

    ordered = jnp.where(side == 0, bins, jnp.roll(bins, half))
    sample_index = jnp.arange(samples, dtype=jnp.int32)
    cycles = ordered[:, None] * sample_index[None, :] % samples
    angles = 2.0 * math.pi / samples * cycles.astype(jnp.float32)
    scaling = (samples / 2.0) ** (-0.5)
    table = jnp.stack([jnp.cos(angles) * scaling, -jnp.sin(angles) * scaling], 1)
    table = table.astype(jnp.bfloat16).reshape(2 * all_bins, samples)
    spectra = jnp.einsum("kt,sct->ksc", table, series, preferred_element_type=jnp.float32)
    spectra = spectra.astype(jnp.bfloat16).reshape(2 * all_bins * snap_local, channel_local)
    rows = all_bins * snap_local
    keep, send = spectra[:rows], spectra[rows:]
    points = grid_coords.astype(jnp.bfloat16).reshape(-1, channel_local)
    received = swap(jnp.concatenate([send, points], 0), "grid", 1)
    other_points = received[rows:].reshape(grid_coords.shape).astype(jnp.int32)
    pair = jnp.stack([keep, received[:rows]], 1)
    blocks = [pair] + [swap(pair, "grid", 2 * k) for k in range(1, grid_size // 2)]

    my_bins = ordered[:half].astype(jnp.float32)
    amplitude = channels ** (-0.5)
    sensors = sensor_coords.reshape(3, grid_size, channel_local)
    picks = jnp.arange(grid_size) ^ place
    sensors = sensors[:, picks].reshape(3, channels)
    beams = []
    for these in (grid_coords, other_points):
        squared = jnp.zeros((channels, grid_local), jnp.int32)
        for axis_pos in range(3):
            offsets = these[axis_pos][None, :] - sensors[axis_pos][:, None]
            squared = squared + offsets * offsets
        distance = jnp.sqrt(squared.astype(jnp.float32))
        turns = (2.0 / samples) * my_bins[:, None, None] * distance[None]
        cosine, sine = turns_cos_sin(turns)
        beam = ((cosine * amplitude).astype(jnp.bfloat16), (-sine * amplitude).astype(jnp.bfloat16))
        beams.append(lax.optimization_barrier(beam))
    partial = []
    for real, imag in beams:
        first = second = 0.0
        for k, block in enumerate(blocks):
            left = block.reshape(half, 2 * snap_local, 2 * channel_local)
            span = slice(2 * k * channel_local, 2 * (k + 1) * channel_local)
            first += jnp.einsum("fsc,fcg->fsg", left, real[:, span], preferred_element_type=jnp.float32)
            second += jnp.einsum("fsc,fcg->fsg", left, imag[:, span], preferred_element_type=jnp.float32)
        out_real = first[:, :snap_local] + second[:, snap_local:]
        out_imag = first[:, snap_local:] - second[:, :snap_local]
        partial.append(jnp.sum(out_real * out_real + out_imag * out_imag, 1))
    total = jnp.concatenate([partial[0], swap(partial[1], "grid", 1)], 0)
    step = freq_size // 2
    while step:
        total = total + swap(total, "freq", step)
        step //= 2
    total = total / snap_total
    bin_count = all_bins // freq_size
    mine = (lax.axis_index("freq") * bin_count + side * half) % all_bins
    bin_power = lax.dynamic_slice_in_dim(total, mine, bin_count)
    power = jnp.sum(total, 0) / all_bins
    return (bin_power, power)


def solution(mesh):
    return jax.shard_map(
        on_device,
        mesh=mesh,
        in_specs=(P("freq", "grid", None), P(), P(), P(None, "grid")),
        out_specs=(P("freq", "grid"), P("grid")),
        check_vma=False,
    )
```

time: 64.5 us -> 52.9 us (0.82)
  blocking collectives: 34.5 us -> 0 us
  other arithmetic: 1.51 us -> 9.62 us
  starting transfers between devices: 4.24 us -> 10.7 us
  local copies, waits for them, and re-layouts: 1.93 us -> 5.78 us
  waiting for transfers between devices: 2.83 us -> 5.46 us
  matrix products: 17.7 us -> 19.8 us
    all_gather x1 -> x0, blocking collectives: 28.8 us -> none  [on_device(): gathered = lax.all_gather(regrouped, 'grid', axis=2, tiled=True)]
    ppermute x0 -> x7, starting transfers between devices: none -> 10.7 us  [swap(): return lax.ppermute(value, axis, [(i, i ^ mask) for i in range(size)])]
    convert_element_type x0 -> x3, other arithmetic: none -> 6.25 us  [the longest x1 6.24 us: on_device(): (-sine * amplitude).astype(jnp.bfloat16)]
    psum x1 -> x0, blocking collectives: 5.76 us -> none  [on_device(): summed = lax.psum(jnp.sum(bin_power, 0), 'freq')]
    ppermute x0 -> x7, waiting for transfers between devices: none -> 5.46 us  [swap(): return lax.ppermute(value, axis, [(i, i ^ mask) for i in range(size)])]
    all_to_all x1 -> x0, starting transfers between devices: 4.24 us -> none  [on_device(): lax.all_to_all(spectra, 'freq', split_axis=0, concat_axis=3, tiled=True)]
    all_to_all x1 -> x0, waiting for transfers between devices: 2.83 us -> none  [on_device(): lax.all_to_all(spectra, 'freq', split_axis=0, concat_axis=3, tiled=True)]
    dot_general x5 -> x17, matrix products: 17.7 us -> 19.8 us  [the longest x8 11.1 us: on_device(): jnp.einsum('fsc,fcg->fsg', left, real[:, span], preferred_element_type=jn...]
  transfers between devices with their start and end apart: 1 -> 7, of which waited for: 1 -> 4; matrix products, arithmetic and copies ran while one was open for 1% -> 39% of each run, Pallas kernels for 0% -> 0%
where the time goes in v1:
time: 52.9 us; the launch traced here: 52.3 us
  matrix products  19.8 us (37%)
  starting transfers between devices  10.7 us (20%)
  other arithmetic  9.62 us (18%)
  local copies, waits for them, and re-layouts  5.78 us (11%)
  waiting for transfers between devices  5.46 us (10%)
  between operations  0.9 us (2%)
    dot_general x8, matrix products, on_device(): jnp.einsum('fsc,fcg->fsg', left, real[:, span], preferred_element_type=jn...  11.1 us
    ppermute x7, starting transfers between devices, swap(): return lax.ppermute(value, axis, [(i, i ^ mask) for i in range(size)])  10.7 us
    dot_general x8, matrix products, on_device(): jnp.einsum('fsc,fcg->fsg', left, imag[:, span], preferred_element_type=jn...  8.08 us
    convert_element_type x1, other arithmetic, on_device(): (-sine * amplitude).astype(jnp.bfloat16)  6.24 us
    ppermute x7, waiting for transfers between devices, swap(): return lax.ppermute(value, axis, [(i, i ^ mask) for i in range(size)])  5.46 us
    ppermute x3, local copies, waits for them, and re-layouts, swap(): return lax.ppermute(value, axis, [(i, i ^ mask) for i in range(size)])  1.68 us
    sqrt x1, other arithmetic, on_device(): distance = jnp.sqrt(squared.astype(jnp.float32))  1.15 us
  transfers between devices with their start and end apart: 7, of which 4 were waited for; matrix products, arithmetic and copies ran while one was open for 39% of the time, Pallas kernels for 0%

profile of v1, /device:TPU:0, one launch (start us, length us, event | category | flops | bytes accessed | tf_op | source)
XLA Modules:
  0.0 52.3 jit_solution(301030165355842958)
XLA Ops:
  0.6 0.0 copy-start
  0.6 0.0 copy-start.3
  0.7 0.0 copy-start.4
  0.7 0.9 %fusion.65 = (s32[2]{0:T(128)S(1)}, s32[2]{0:T(128)S(1)}) fusion(s32[4]{0:T(128)} %param.5), kind=kLoop, calls=%fused_computation.116 | loop fusion | bytes 32 | tf_op jit(solution)/shard_map/jit(_roll_static)/slice | solution.py:34
  1.6 0.7 %broadcast_select_fusion = s32[4]{0:T(128)S(1)} fusion(s32[4]{0:T(128)} %param.5, pred[]{:T(512)S(6)} %eq.8, s32[2]{0:T(128)S(1)} %get-tuple-element.34, s32[2]{0:T(128)S(1)} %get-tuple-element.33), kind=kLoop, calls=%fused_computation.106 | loop fusion | flops 8 | bytes 49 | tf_op jit(solution)/shard_map/jit(_where)/select_n | solution.py:34
  2.3 0.1 multiply_convert_fusion.1
  2.5 0.0 copy-done
  2.5 0.6 %convolution_convert_fusion = bf16[8,32,128]{2,0,1:T(8,128)(2,1)S(1)} fusion(bf16[8,256,1]{1,0,2:T(8,128)(2,1)S(1)} %reshape.377, bf16[32,128,256]{2,1,0:T(8,128)(2,1)S(1)} %copy-done), kind=kOutput, calls=%fused_computation.47 | convolution fusion | flops 16809984 | bytes 2166784 | tf_op jit(solution)/shard_map/kt,sct->ksc/dot_general | solution.py:41
  3.2 0.0 copy-done.3
  3.2 2.8 %collective-permute-start = (bf16[134,128]{1,0:T(8,128)(2,1)S(1)}, bf16[134,128]{1,0:T(8,128)(2,1)S(1)}, u32[]{:S(2)}, u32[]{:S(2)}) collective-permute-start(bf16[134,128]{1,0:T(8,128)(2,1)S(1)} %pad_maximum_fusion.1), channel_id=1, source_target_pairs={{0,1},{1,0},{2,3},{3,2},{4,5},{5,4},{6,7},{7,6},{8,9},{9,8},{10,11... | collective-permute-start | bytes 102920 | tf_op jit(solution)/shard_map/ppermute | solution.py:32
  6.1 0.0 copy-done.4
  6.1 0.6 %gather_fusion = s32[8,3,128]{2,1,0:T(4,128)S(1)} fusion(s32[3,8,128]{2,0,1:T(4,128)S(1)} %bitcast.44, s32[1024]{0:T(1024)S(1)} %pad_clamp_fusion), kind=kCustom, calls=%fused_computation | custom fusion | bytes 24608 | tf_op jit(solution)/shard_map/gather | solution.py:55
  6.7 1.3 %collective-permute-done = bf16[134,128]{1,0:T(8,128)(2,1)S(1)} collective-permute-done((bf16[134,128]{1,0:T(8,128)(2,1)S(1)}, bf16[134,128]{1,0:T(8,128)(2,1)S(1)}, u32[]{:S(2)}, u32[]{:S(2)}) %collective-permute-start) | collective-permute-done | bytes 34336 | tf_op jit(solution)/shard_map/ppermute | solution.py:32
  8.0 0.6 %pad_maximum_fusion = bf16[128,2,128]{2,0,1:T(8,128)(2,1)} fusion(bf16[128,1,128]{2,0,1:T(8,128)(2,1)S(1)} %slice_bitcast_fusion, bf16[128,1,128]{2,0,1:T(8,128)(2,1)S(1)} %bitcast.39), kind=kLoop, calls=%fused_computation.86 | loop fusion | flops 32768 | bytes 131072 | tf_op jit(solution)/shard_map/stack | solution.py:48
  8.6 0.9 %copy.21 = bf16[128,2,128]{2,1,0:T(2,128)(2,1)S(1)} copy(bf16[128,2,128]{2,0,1:T(8,128)(2,1)} %pad_maximum_fusion) | data formatting | bytes 131072 | tf_op jit(solution)/shard_map/stack | solution.py:48
  9.5 2.4 %collective-permute-start.1 = (bf16[128,2,128]{2,0,1:T(8,128)(2,1)}, bf16[128,2,128]{2,0,1:T(8,128)(2,1)S(1)}, u32[]{:S(2)}, u32[]{:S(2)}) collective-permute-start(bf16[128,2,128]{2,0,1:T(8,128)(2,1)} %pad_maximum_fusion), channel_id=1, source_target_pairs={{0,2},{1,3},{2,0},{3,1},{4,6},{5,7},{6,4},{7,5},{8,10},{9,11},{10,... | collective-permute-start | bytes 196616 | tf_op jit(solution)/shard_map/ppermute | solution.py:32
  11.9 2.5 %collective-permute-start.3 = (bf16[128,2,128]{2,0,1:T(8,128)(2,1)}, bf16[128,2,128]{2,0,1:T(8,128)(2,1)S(1)}, u32[]{:S(2)}, u32[]{:S(2)}) collective-permute-start(bf16[128,2,128]{2,0,1:T(8,128)(2,1)} %pad_maximum_fusion), channel_id=1, source_target_pairs={{0,6},{1,7},{2,4},{3,5},{4,2},{5,3},{6,0},{7,1},{8,14},{9,15},{10,... | collective-permute-start | bytes 196616 | tf_op jit(solution)/shard_map/ppermute | solution.py:32
  14.4 0.1 collective-permute-start.2
  14.5 1.1 %convert_sqrt_fusion.1 = (f32[1024,256]{1,0:T(8,128)S(1)}, f32[1024,256]{1,0:T(8,128)S(1)}) fusion(s32[1024]{0:T(1024)S(1)} %bitcast.43, s32[256]{0:T(256)S(1)} %bitcast.46, s32[1024]{0:T(1024)S(1)} %bitcast.42, s32[256]{0:T(256)S(1)} %bitcast.47, s32[1024]{0:T(1024)S(1)} %bitcast.41, s32[256]{0:T(256)S(1)} %bitcast.45, s32[256]{0:T(256)S(1)} %get-tuple-element.27, ...), kind=kLoop, calls=%fused_computation.49 | loop fusion | flops 4718592 | bytes 2115584 | tf_op jit(solution)/shard_map/sqrt | solution.py:62
  15.7 6.2 %fusion.5 = (bf16[2,1024,256]{2,1,0:T(8,128)(2,1)S(1)}, bf16[2,1024,256]{2,1,0:T(8,128)(2,1)}, bf16[2,1024,256]{2,1,0:T(8,128)(2,1)}, bf16[2,1024,256]{2,1,0:T(8,128)(2,1)}) fusion(f32[1024,256]{1,0:T(8,128)S(1)} %get-tuple-element.21, f32[2]{0:T(128)S(1)} %convert_multiply_fusion, f32[1024,256]{1,0:T(8,128)S(1)} %get-tuple-element.22), kind=kLoop, calls=%fused_computation.12 | loop fusion | flops 38797312 | bytes 6291464 | tf_op jit(solution)/shard_map/convert_element_type | solution.py:65
  22.0 1.8 %fusion.46 = f32[2,64,256]{2,1,0:T(8,128)} fusion(bf16[2,64,256]{2,1,0:T(8,128)(2,1)S(1)} %reshape.364, bf16[2,1024,256]{2,1,0:T(8,128)(2,1)} %get-tuple-element.6), kind=kOutput, calls=%fused_computation.72 | convolution fusion | flops 16777216 | bytes 458752 | tf_op jit(solution)/shard_map/fsc,fcg->fsg/dot_general | solution.py:73
  23.8 0.8 %fusion.40 = f32[2,64,256]{2,1,0:T(8,128)} fusion(bf16[2,64,256]{2,1,0:T(8,128)(2,1)S(1)} %reshape.364, bf16[2,1024,256]{2,1,0:T(8,128)(2,1)S(1)} %get-tuple-element.7), kind=kOutput, calls=%fused_computation.66 | convolution fusion | flops 16777216 | bytes 458752 | tf_op jit(solution)/shard_map/fsc,fcg->fsg/dot_general | solution.py:74
  24.6 1.8 %fusion.34 = f32[2,64,256]{2,1,0:T(8,128)} fusion(bf16[2,64,256]{2,1,0:T(8,128)(2,1)S(1)} %reshape.364, bf16[2,1024,256]{2,1,0:T(8,128)(2,1)} %get-tuple-element.8), kind=kOutput, calls=%fused_computation.60 | convolution fusion | flops 16777216 | bytes 458752 | tf_op jit(solution)/shard_map/fsc,fcg->fsg/dot_general | solution.py:73
  26.4 1.8 %fusion.28 = f32[2,64,256]{2,1,0:T(8,128)} fusion(bf16[2,64,256]{2,1,0:T(8,128)(2,1)S(1)} %reshape.364, bf16[2,1024,256]{2,1,0:T(8,128)(2,1)} %get-tuple-element.9), kind=kOutput, calls=%fused_computation.54 | convolution fusion | flops 16777216 | bytes 458752 | tf_op jit(solution)/shard_map/fsc,fcg->fsg/dot_general | solution.py:74
  28.1 0.0 collective-permute-done.3
  28.1 0.1 copy.24
  28.3 1.1 %fusion.42 = f32[2,64,256]{2,1,0:T(8,128)S(1)} fusion(bf16[2,64,256]{2,1,0:T(8,128)(2,1)S(1)} %reshape.368, bf16[2,1024,256]{2,1,0:T(8,128)(2,1)} %get-tuple-element.6), kind=kOutput, calls=%fused_computation.68 | convolution fusion | flops 16777216 | bytes 458752 | tf_op jit(solution)/shard_map/fsc,fcg->fsg/dot_general | solution.py:73
  29.4 0.2 fusion.36
  29.6 1.8 %fusion.30 = f32[2,64,256]{2,1,0:T(8,128)} fusion(bf16[2,64,256]{2,1,0:T(8,128)(2,1)S(1)} %reshape.368, bf16[2,1024,256]{2,1,0:T(8,128)(2,1)} %get-tuple-element.8), kind=kOutput, calls=%fused_computation.56 | convolution fusion | flops 16777216 | bytes 458752 | tf_op jit(solution)/shard_map/fsc,fcg->fsg/dot_general | solution.py:73
  31.3 1.8 %fusion.24 = f32[2,64,256]{2,1,0:T(8,128)} fusion(bf16[2,64,256]{2,1,0:T(8,128)(2,1)S(1)} %reshape.368, bf16[2,1024,256]{2,1,0:T(8,128)(2,1)} %get-tuple-element.9), kind=kOutput, calls=%fused_computation.50 | convolution fusion | flops 16777216 | bytes 458752 | tf_op jit(solution)/shard_map/fsc,fcg->fsg/dot_general | solution.py:74
  33.1 0.0 collective-permute-done.1
  33.1 0.1 copy.22
  33.2 0.0 collective-permute-done.2
  33.3 1.5 %copy.23 = bf16[128,2,128]{2,1,0:T(2,128)(2,1)} copy(bf16[128,2,128]{2,0,1:T(8,128)(2,1)} %collective-permute-done.2) | data formatting | bytes 131072 | tf_op jit(solution)/shard_map/ppermute | solution.py:32
  34.8 0.9 %reshape.367 = bf16[2,64,256]{2,1,0:T(8,128)(2,1)S(1)} reshape(bf16[128,2,128]{2,1,0:T(2,128)(2,1)} %copy.23) | data formatting | bytes 131072 | tf_op jit(solution)/shard_map/reshape | solution.py:71
  35.7 0.0 copy-start.2
  35.7 0.0 copy-start.1
  35.7 1.2 %convolution_add_fusion.7 = f32[2,64,256]{2,1,0:T(8,128)S(1)} fusion(f32[2,64,256]{2,1,0:T(8,128)} %fusion.46, bf16[2,64,256]{2,1,0:T(8,128)(2,1)S(1)} %reshape.366, bf16[2,1024,256]{2,1,0:T(8,128)(2,1)} %get-tuple-element.6), kind=kOutput, calls=%fused_computation.46 | convolution fusion | flops 16809984 | bytes 589824 | tf_op jit(solution)/shard_map/fsc,fcg->fsg/dot_general | solution.py:73
  36.9 1.1 %convolution_add_fusion.5 = f32[2,64,256]{2,1,0:T(8,128)S(1)} fusion(f32[2,64,256]{2,1,0:T(8,128)} %fusion.40, bf16[2,64,256]{2,1,0:T(8,128)(2,1)S(1)} %reshape.366, bf16[2,1024,256]{2,1,0:T(8,128)(2,1)S(1)} %get-tuple-element.7), kind=kOutput, calls=%fused_computation.43 | convolution fusion | flops 16809984 | bytes 589824 | tf_op jit(solution)/shard_map/fsc,fcg->fsg/dot_general | solution.py:74
  38.0 1.2 %convolution_add_fusion.3 = f32[2,64,256]{2,1,0:T(8,128)S(1)} fusion(f32[2,64,256]{2,1,0:T(8,128)} %fusion.34, bf16[2,64,256]{2,1,0:T(8,128)(2,1)S(1)} %reshape.366, bf16[2,1024,256]{2,1,0:T(8,128)(2,1)} %get-tuple-element.8), kind=kOutput, calls=%fused_computation.40 | convolution fusion | flops 16809984 | bytes 589824 | tf_op jit(solution)/shard_map/fsc,fcg->fsg/dot_general | solution.py:73
  39.1 1.2 %convolution_add_fusion.1 = f32[2,64,256]{2,1,0:T(8,128)S(1)} fusion(f32[2,64,256]{2,1,0:T(8,128)} %fusion.28, bf16[2,64,256]{2,1,0:T(8,128)(2,1)S(1)} %reshape.366, bf16[2,1024,256]{2,1,0:T(8,128)(2,1)} %get-tuple-element.9), kind=kOutput, calls=%fused_computation.37 | convolution fusion | flops 16809984 | bytes 589824 | tf_op jit(solution)/shard_map/fsc,fcg->fsg/dot_general | solution.py:74
  40.3 0.0 copy-done.2
  40.3 1.1 %fusion.21 = f32[2,64,256]{2,1,0:T(8,128)S(1)} fusion(f32[2,64,256]{2,1,0:T(8,128)S(1)} %copy-done.2, f32[2,64,256]{2,1,0:T(8,128)S(1)} %convolution_add_fusion.3, bf16[2,64,256]{2,1,0:T(8,128)(2,1)S(1)} %reshape.367, bf16[2,1024,256]{2,1,0:T(8,128)(2,1)} %get-tuple-element.8), kind=kOutput, calls=%fused_computation.39 | convolution fusion | flops 16842752 | bytes 720896 | tf_op jit(solution)/shard_map/fsc,fcg->fsg/dot_general | solution.py:73
  41.4 0.0 copy-done.1
  41.4 1.1 %fusion.20 = f32[2,64,256]{2,1,0:T(8,128)S(1)} fusion(f32[2,64,256]{2,1,0:T(8,128)S(1)} %copy-done.1, f32[2,64,256]{2,1,0:T(8,128)S(1)} %convolution_add_fusion.1, bf16[2,64,256]{2,1,0:T(8,128)(2,1)S(1)} %reshape.367, bf16[2,1024,256]{2,1,0:T(8,128)(2,1)} %get-tuple-element.9), kind=kOutput, calls=%fused_computation.36 | convolution fusion | flops 16842752 | bytes 720896 | tf_op jit(solution)/shard_map/fsc,fcg->fsg/dot_general | solution.py:74
  42.6 1.4 %collective-permute-start.4 = (f32[2,256]{1,0:T(2,128)S(1)}, f32[2,256]{1,0:T(2,128)S(1)}, u32[]{:S(2)}, u32[]{:S(2)}) collective-permute-start(f32[2,256]{1,0:T(2,128)S(1)} %fusion.50), channel_id=1, source_target_pairs={{0,1},{1,0},{2,3},{3,2},{4,5},{5,4},{6,7},{7,6},{8,9},{9,8},{10,11... | collective-permute-start | bytes 6152 | tf_op jit(solution)/shard_map/ppermute | solution.py:32
  44.0 1.1 %fusion.23 = f32[2,64,256]{2,1,0:T(8,128)S(1)} fusion(f32[2,64,256]{2,1,0:T(8,128)S(1)} %fusion.42, f32[2,64,256]{2,1,0:T(8,128)S(1)} %convolution_add_fusion.7, bf16[2,64,256]{2,1,0:T(8,128)(2,1)S(1)} %reshape.367, bf16[2,1024,256]{2,1,0:T(8,128)(2,1)} %get-tuple-element.6), kind=kOutput, calls=%fused_computation.45 | convolution fusion | flops 16842752 | bytes 720896 | tf_op jit(solution)/shard_map/fsc,fcg->fsg/dot_general | solution.py:73
  45.1 0.2 fusion.22
  45.3 1.0 %collective-permute-done.4 = f32[2,256]{1,0:T(2,128)S(1)} collective-permute-done((f32[2,256]{1,0:T(2,128)S(1)}, f32[2,256]{1,0:T(2,128)S(1)}, u32[]{:S(2)}, u32[]{:S(2)}) %collective-permute-start.4) | collective-permute-done | bytes 2080 | tf_op jit(solution)/shard_map/ppermute | solution.py:32
  46.3 1.5 %collective-permute-start.5 = (f32[4,256]{1,0:T(4,128)S(1)}, f32[4,256]{1,0:T(4,128)S(1)}, u32[]{:S(2)}, u32[]{:S(2)}) collective-permute-start(f32[4,256]{1,0:T(4,128)S(1)} %pad_maximum_fusion.3), channel_id=1, source_target_pairs={{0,16},{8,24},{16,0},{24,8},{1,17},{9,25},{17,1},{25,9},{2,18},{10... | collective-permute-start | bytes 12296 | tf_op jit(solution)/shard_map/ppermute | solution.py:32
  47.8 2.1 %collective-permute-done.5 = f32[4,256]{1,0:T(4,128)S(1)} collective-permute-done((f32[4,256]{1,0:T(4,128)S(1)}, f32[4,256]{1,0:T(4,128)S(1)}, u32[]{:S(2)}, u32[]{:S(2)}) %collective-permute-start.5) | collective-permute-done | bytes 4128 | tf_op jit(solution)/shard_map/ppermute | solution.py:32
  49.9 0.1 collective-permute-start.6
  50.0 1.1 %collective-permute-done.6 = f32[4,256]{1,0:T(4,128)S(1)} collective-permute-done((f32[4,256]{1,0:T(4,128)S(1)}, f32[4,256]{1,0:T(4,128)S(1)}, u32[]{:S(2)}, u32[]{:S(2)}) %collective-permute-start.6) | collective-permute-done | bytes 4128 | tf_op jit(solution)/shard_map/ppermute | solution.py:32
  51.1 0.6 %broadcast_multiply_fusion = f32[256]{0:T(256)} fusion(f32[256]{0:T(256)S(1)} %get-tuple-element.10), kind=kLoop, calls=%fused_computation.108 | loop fusion | flops 256 | bytes 2048 | tf_op jit(solution)/shard_map/div | solution.py:87
  51.7 0.6 %constant_dynamic-slice_fusion = f32[1,256]{1,0:T(1,128)} fusion(f32[4,256]{1,0:T(4,128)S(1)} %get-tuple-element.11, s32[]{:T(128)S(6)} %select_n.55), kind=kLoop, calls=%fused_computation.110 | loop fusion | bytes 2052 | tf_op jit(solution)/shard_map/dynamic_slice | solution.py:86
  (25 shorter events, 0.4 us)
Async XLA Ops:
  0.6 1.8 %copy-start = (bf16[32,128,256]{2,1,0:T(8,128)(2,1)S(1)}, bf16[32,128,256]{2,1,0:T(8,128)(2,1)}, u32[]{:S(2)}) copy-start(bf16[32,128,256]{2,1,0:T(8,128)(2,1)} %param.4) | copy-start | bytes 6291460
  0.6 2.5 %copy-start.3 = (s32[3,256]{1,0:T(4,128)S(1)}, s32[3,256]{1,0:T(4,128)}, u32[]{:S(2)}) copy-start(s32[3,256]{1,0:T(4,128)} %param.7) | copy-start | bytes 9220
  0.7 5.4 %copy-start.4 = (s32[3,1024]{1,0:T(4,128)S(1)}, s32[3,1024]{1,0:T(4,128)}, u32[]{:S(2)}) copy-start(s32[3,1024]{1,0:T(4,128)} %param.6) | copy-start | bytes 36868
  3.2 4.8 %collective-permute-start = (bf16[134,128]{1,0:T(8,128)(2,1)S(1)}, bf16[134,128]{1,0:T(8,128)(2,1)S(1)}, u32[]{:S(2)}, u32[]{:S(2)}) collective-permute-start(bf16[134,128]{1,0:T(8,128)(2,1)S(1)} %pad_maximum_fusion.1), channel_id=1, source_target_pairs={{0,1},{1,0},{2,3},{3,2},{4,5},{5,4},{6,7},{7,6},{8,9},{9,8},{10,11... | collective-permute-start | bytes 102920 | tf_op jit(solution)/shard_map/ppermute | solution.py:32
  9.5 23.6 %collective-permute-start.1 = (bf16[128,2,128]{2,0,1:T(8,128)(2,1)}, bf16[128,2,128]{2,0,1:T(8,128)(2,1)S(1)}, u32[]{:S(2)}, u32[]{:S(2)}) collective-permute-start(bf16[128,2,128]{2,0,1:T(8,128)(2,1)} %pad_maximum_fusion), channel_id=1, source_target_pairs={{0,2},{1,3},{2,0},{3,1},{4,6},{5,7},{6,4},{7,5},{8,10},{9,11},{10,... | collective-permute-start | bytes 196616 | tf_op jit(solution)/shard_map/ppermute | solution.py:32
  11.9 16.2 %collective-permute-start.3 = (bf16[128,2,128]{2,0,1:T(8,128)(2,1)}, bf16[128,2,128]{2,0,1:T(8,128)(2,1)S(1)}, u32[]{:S(2)}, u32[]{:S(2)}) collective-permute-start(bf16[128,2,128]{2,0,1:T(8,128)(2,1)} %pad_maximum_fusion), channel_id=1, source_target_pairs={{0,6},{1,7},{2,4},{3,5},{4,2},{5,3},{6,0},{7,1},{8,14},{9,15},{10,... | collective-permute-start | bytes 196616 | tf_op jit(solution)/shard_map/ppermute | solution.py:32
  14.4 18.9 %collective-permute-start.2 = (bf16[128,2,128]{2,0,1:T(8,128)(2,1)}, bf16[128,2,128]{2,0,1:T(8,128)(2,1)}, u32[]{:S(2)}, u32[]{:S(2)}) collective-permute-start(bf16[128,2,128]{2,0,1:T(8,128)(2,1)} %pad_maximum_fusion), channel_id=1, source_target_pairs={{0,4},{1,5},{2,6},{3,7},{4,0},{5,1},{6,2},{7,3},{8,12},{9,13},{10,... | collective-permute-start | bytes 196616 | tf_op jit(solution)/shard_map/ppermute | solution.py:32
  35.7 4.6 %copy-start.2 = (f32[2,64,256]{2,1,0:T(8,128)S(1)}, f32[2,64,256]{2,1,0:T(8,128)}, u32[]{:S(2)}) copy-start(f32[2,64,256]{2,1,0:T(8,128)} %fusion.30) | copy-start | bytes 393220
  35.7 5.7 %copy-start.1 = (f32[2,64,256]{2,1,0:T(8,128)S(1)}, f32[2,64,256]{2,1,0:T(8,128)}, u32[]{:S(2)}) copy-start(f32[2,64,256]{2,1,0:T(8,128)} %fusion.24) | copy-start | bytes 393220
  42.6 3.7 %collective-permute-start.4 = (f32[2,256]{1,0:T(2,128)S(1)}, f32[2,256]{1,0:T(2,128)S(1)}, u32[]{:S(2)}, u32[]{:S(2)}) collective-permute-start(f32[2,256]{1,0:T(2,128)S(1)} %fusion.50), channel_id=1, source_target_pairs={{0,1},{1,0},{2,3},{3,2},{4,5},{5,4},{6,7},{7,6},{8,9},{9,8},{10,11... | collective-permute-start | bytes 6152 | tf_op jit(solution)/shard_map/ppermute | solution.py:32
  46.3 3.6 %collective-permute-start.5 = (f32[4,256]{1,0:T(4,128)S(1)}, f32[4,256]{1,0:T(4,128)S(1)}, u32[]{:S(2)}, u32[]{:S(2)}) collective-permute-start(f32[4,256]{1,0:T(4,128)S(1)} %pad_maximum_fusion.3), channel_id=1, source_target_pairs={{0,16},{8,24},{16,0},{24,8},{1,17},{9,25},{17,1},{25,9},{2,18},{10... | collective-permute-start | bytes 12296 | tf_op jit(solution)/shard_map/ppermute | solution.py:32
  49.9 1.2 %collective-permute-start.6 = (f32[4,256]{1,0:T(4,128)S(1)}, f32[4,256]{1,0:T(4,128)S(1)}, u32[]{:S(2)}, u32[]{:S(2)}) collective-permute-start(f32[4,256]{1,0:T(4,128)S(1)} %fusion.60), channel_id=1, source_target_pairs={{0,8},{8,0},{16,24},{24,16},{1,9},{9,1},{17,25},{25,17},{2,10},{10... | collective-permute-start | bytes 12296 | tf_op jit(solution)/shard_map/ppermute | solution.py:32

commit v2 on v0

v2 whole, which is shorter than its diff:
```python
import functools
import math

import jax
import jax.numpy as jnp
from jax import lax
from jax.experimental import pallas as pl
from jax.experimental.pallas import tpu as pltpu
from jax.sharding import PartitionSpec as P


def fit(function, degree):
    import numpy as np

    nodes = 0.125 + 0.125 * np.cos(math.pi * (np.arange(degree + 1) + 0.5) / (degree + 1))
    matrix = np.vander(nodes, degree + 1, increasing=True)
    return [float(v) for v in np.linalg.solve(matrix, function(np.sqrt(nodes)))]


def fits():
    import numpy as np

    return fit(lambda x: np.sin(math.pi * x) / x, 5), fit(lambda x: np.cos(math.pi * x), 5)


def horner(u, coefficients):
    total = coefficients[-1]
    for value in coefficients[-2::-1]:
        total = total * u + value
    return total


def scaled_cos_sin(turns, scale):
    whole = (turns + 12582912.0) - 12582912.0
    x = turns - whole
    u = x * x
    sine, cosine = fits()
    root = math.sqrt(2.0 * scale)
    s = x * horner(u, [v * root for v in sine])
    c = horner(u, [-v * root for v in cosine])
    return scale - s * s, s * c


def transform_kernel(half, bins_far, points_far, series_ref, keep_ref, send_ref, bins_ref, points_ref, held, tall, sems, small_sems):
    side = lax.axis_index("grid") % 2
    snaps, channels, samples = held.shape
    rows = tall.shape[0] // snaps
    all_bins = rows // 2
    chunks = sems.shape[0]
    step = snaps // chunks
    copies = [
        pltpu.make_async_copy(series_ref.at[pl.ds(i * step, step)], held.at[pl.ds(i * step, step)], sems.at[i])
        for i in range(chunks)
    ]
    small = [
        pltpu.make_async_copy(bins_far, bins_ref, small_sems.at[0]),
        pltpu.make_async_copy(points_far, points_ref, small_sems.at[1]),
    ]
    for copy in small + copies:
        copy.start()
    for copy in small:
        copy.wait()
    row = lax.broadcasted_iota(jnp.int32, (rows, samples), 0)
    sample = lax.broadcasted_iota(jnp.int32, (rows, samples), 1)
    number = jnp.zeros((rows, samples), jnp.int32)
    for f in range(all_bins):
        number = jnp.where(row // 2 == f, bins_ref[(f + side * half) % all_bins], number)
    turns = (number * sample).astype(jnp.float32) * (1.0 / samples)
    cosine, sine = scaled_cos_sin(turns, (samples / 2.0) ** (-0.5))
    table = jnp.where(row % 2 == 0, cosine, sine).astype(jnp.bfloat16)
    group = 2 if channels % 128 == 0 and step % 2 == 0 else 1
    for i, copy in enumerate(copies):
        copy.wait()
        for s in range(i * step, (i + 1) * step, group):
            block = held[s : s + group].reshape(group * channels, samples)
            out = lax.dot_general(table, block, (((1,), (1,)), ((), ())), preferred_element_type=jnp.float32)
            for p in range(group):
                tall[pl.ds((s + p) * rows, rows), :] = out[:, p * channels : (p + 1) * channels]
    for k in range(rows):
        picked = tall[pl.ds(k, snaps, stride=rows), :].astype(jnp.bfloat16)
        target, base = (keep_ref, k) if k < rows // 2 else (send_ref, k - rows // 2)
        target[pl.ds(base * snaps, snaps), :] = picked
    extra = send_ref.shape[0] - rows // 2 * snaps
    pieces = [
        points_ref[pl.ds(a, 1), pl.ds(p, channels)].astype(jnp.float32)
        for a in range(points_ref.shape[0])
        for p in range(0, points_ref.shape[1], channels)
    ]
    pieces.append(jnp.zeros((extra - len(pieces), channels), jnp.float32))
    send_ref[pl.ds(rows // 2 * snaps, extra), :] = jnp.concatenate(pieces, 0).astype(jnp.bfloat16)


def pair_kernel(keep_ref, received_ref, pair_ref):
    side = lax.axis_index("grid") % 2
    rows, channels = keep_ref.shape

    @pl.when(side == 0)
    def _():
        pair_ref[:, :channels] = keep_ref[...]
        pair_ref[:, channels:] = received_ref[:rows, :]

    @pl.when(side == 1)
    def _():
        pair_ref[:, channels:] = keep_ref[...]
        pair_ref[:, :channels] = received_ref[:rows, :]


def split(value):
    high = jnp.floor(value * (1.0 / 64.0))
    return high, value - 64.0 * high


def replica_kernel(half, samples, packed, bins_ref, sensors_ref, points_ref, beam_ref, squares):
    side = lax.axis_index("grid") % 2
    channels = sensors_ref.shape[1]
    points = beam_ref.shape[3]
    sensors = [sensors_ref[pl.ds(a, 1), :].astype(jnp.float32) for a in range(3)]
    if packed:
        width = points_ref.shape[1]
        base = points_ref.shape[0] - packed
        tail = points_ref[pl.ds(base, packed), :].astype(jnp.float32)
        per = points // width
        places = [jnp.concatenate([tail[a * per + p : a * per + p + 1] for p in range(per)], 1) for a in range(3)]
    else:
        places = [points_ref[pl.ds(a, 1), :].astype(jnp.float32) for a in range(3)]
    s_high, s_low = split(sum(v * v for v in sensors))
    g_high, g_low = split(sum(v * v for v in places))
    one = jnp.ones((1, channels), jnp.float32)
    left = jnp.concatenate([-2.0 * v for v in sensors] + [s_high, s_low, 64.0 * one, one, 0.0 * one], 0)
    one = jnp.ones((1, points), jnp.float32)
    right = jnp.concatenate(places + [64.0 * one, one, g_high, g_low, 0.0 * one], 0)
    squares[...] = lax.dot_general(
        left.T.astype(jnp.bfloat16), right.astype(jnp.bfloat16), (((1,), (0,)), ((), ())),
        preferred_element_type=jnp.float32,
    )
    step = 32
    rates = [
        bins_ref[f + side * half].astype(jnp.float32) * (2.0 / samples) for f in range(half)
    ]

    @pl.loop(0, channels // step)
    def _(i):
        span = pl.ds(pl.multiple_of(i * step, step), step)
        square = squares[span, :]
        distance = square * lax.rsqrt(jnp.maximum(square, 1.0))
        for f in range(half):
            real, imag = scaled_cos_sin(distance * rates[f], channels ** (-0.5))
            beam_ref[f, 0, span, :] = real.astype(jnp.bfloat16)
            beam_ref[f, 1, span, :] = imag.astype(jnp.bfloat16)


def product_kernel(masks, first, last, *refs):
    blocks, rest = refs[: len(masks)], refs[len(masks) :]
    beams, rest = rest[:2], rest[2:]
    sums_in = None if first else rest[0]
    out = rest[-1]
    place = lax.axis_index("grid") // 2
    half = beams[0].shape[0]
    rows = blocks[0].shape[0] // half
    depth = blocks[0].shape[1]
    points = beams[0].shape[3]
    snaps = rows // 2
    for f in range(half):
        for b, beam in enumerate(beams):
            totals = [None, None]
            for part in range(2):
                total = None if first else sums_in[f, b, part]
                for mask, block in zip(masks, blocks):
                    start = pl.multiple_of((place ^ mask) * depth, depth)
                    term = jnp.dot(
                        block[pl.ds(f * rows, rows), :], beam[f, part, pl.ds(start, depth), :],
                        preferred_element_type=jnp.float32,
                    )
                    total = term if total is None else total + term
                totals[part] = total
            if last:
                real = totals[0][:snaps] + totals[1][snaps:]
                imag = totals[0][snaps:] - totals[1][:snaps]
                out[b, pl.ds(f, 1), :] = jnp.sum(real * real + imag * imag, 0, keepdims=True)
            else:
                for part in range(2):
                    out[f, b, part] = totals[part]


def vmem(n):
    return [pl.BlockSpec(memory_space=pltpu.VMEM)] * n


def grant(mib):
    return pltpu.CompilerParams(vmem_limit_bytes=mib << 20)


def near(*values):
    return [pltpu.with_memory_space_constraint(v, pltpu.VMEM) for v in values]


def on_device(series, bins, sensor_coords, grid_coords):
    snap_local, channel_local, samples = series.shape
    all_bins = bins.shape[0]
    channels = sensor_coords.shape[1]
    grid_local = grid_coords.shape[1]
    freq_size = lax.axis_size("freq")
    grid_size = lax.axis_size("grid")
    snap_total = snap_local * freq_size
    half = all_bins // 2
    rows = all_bins * snap_local
    side = lax.axis_index("grid") % 2

    def swap(value, axis, mask):
        size = lax.axis_size(axis)
        return lax.ppermute(value, axis, [(i, i ^ mask) for i in range(size)])

    packed = -(-3 * grid_local // channel_local // 16) * 16
    chunks = 4
    keep, send = pl.pallas_call(
        functools.partial(transform_kernel, half),
        out_shape=[
            pltpu.VMEM((rows, channel_local), jnp.bfloat16),
            pltpu.VMEM((rows + packed, channel_local), jnp.bfloat16),
        ],
        in_specs=[pl.BlockSpec(memory_space=pl.ANY)] * 3,
        out_specs=vmem(2),
        scratch_shapes=[
            pltpu.SMEM(bins.shape, jnp.int32),
            pltpu.VMEM(grid_coords.shape, jnp.int32),
            pltpu.VMEM(series.shape, jnp.bfloat16),
            pltpu.VMEM((snap_local * 2 * all_bins, channel_local), jnp.float32),
            pltpu.SemaphoreType.DMA((chunks,)),
            pltpu.SemaphoreType.DMA((2,)),
        ],
        compiler_params=grant(12),
    )(*[pltpu.with_memory_space_constraint(v, pltpu.HBM) for v in (bins, grid_coords, series)])
    received = swap(send, "grid", 1)

    def replicas(points, packed):
        return pl.pallas_call(
            functools.partial(replica_kernel, half, samples, packed),
            out_shape=pltpu.VMEM((half, 2, channels, grid_local), jnp.bfloat16),
            in_specs=[pl.BlockSpec(memory_space=pltpu.SMEM), *vmem(2)],
            out_specs=vmem(1)[0],
            scratch_shapes=[pltpu.VMEM((channels, grid_local), jnp.float32)],
            compiler_params=grant(12),
        )(bins, sensor_coords, points)

    pair = pl.pallas_call(
        pair_kernel,
        out_shape=pltpu.VMEM((rows, 2 * channel_local), jnp.bfloat16),
        in_specs=vmem(2),
        out_specs=vmem(1)[0],
        compiler_params=grant(12),
    )(*near(keep, received))
    far = {k: swap(pair, "grid", 2 * k) for k in range(1, grid_size // 2)}
    beams = (replicas(grid_coords, 0), replicas(*near(received), packed))
    sums = pl.pallas_call(
        functools.partial(product_kernel, (0,), True, False),
        out_shape=pltpu.VMEM((half, 2, 2, 2 * snap_local, grid_local), jnp.float32),
        in_specs=vmem(3),
        out_specs=vmem(1)[0],
        compiler_params=grant(12),
    )(*near(pair, *beams))
    masks = tuple(far)
    powers = pl.pallas_call(
        functools.partial(product_kernel, masks, False, True),
        out_shape=pltpu.VMEM((2, half, grid_local), jnp.float32),
        in_specs=vmem(len(masks) + 3),
        out_specs=vmem(1)[0],
        compiler_params=grant(12),
    )(*near(*[far[k] for k in masks], *beams, sums))
    total = jnp.concatenate([powers[0], swap(powers[1], "grid", 1)], 0)
    step = freq_size // 2
    while step:
        total = total + swap(total, "freq", step)
        step //= 2
    total = total / snap_total
    bin_count = all_bins // freq_size
    mine = (lax.axis_index("freq") * bin_count + side * half) % all_bins
    bin_power = lax.dynamic_slice_in_dim(total, mine, bin_count)
    power = jnp.sum(total, 0) / all_bins
    return (bin_power, power)


def solution(mesh):
    return jax.shard_map(
        on_device,
        mesh=mesh,
        in_specs=(P("freq", "grid", None), P(), P(), P(None, "grid")),
        out_specs=(P("freq", "grid"), P("grid")),
        check_vma=False,
    )
```

time: 64.5 us -> 30.5 us (0.47)
  blocking collectives: 34.5 us -> 0 us
  matrix products: 17.7 us -> 0 us
  Pallas kernels: 0 us -> 10.2 us
  starting transfers between devices: 4.24 us -> 11.4 us
  waiting for transfers between devices: 2.83 us -> 6.84 us
  local copies, waits for them, and re-layouts: 1.93 us -> 0.58 us
  other arithmetic: 1.51 us -> 0.6 us
    all_gather x1 -> x0, blocking collectives: 28.8 us -> none  [on_device(): gathered = lax.all_gather(regrouped, 'grid', axis=2, tiled=True)]
    dot_general x5 -> x0, matrix products: 17.7 us -> none  [the longest x4 17.1 us: product(): jnp.einsum('fgc,fcs->fgs', left, right, preferred_element_type=jnp.float32)]
    ppermute x0 -> x7, starting transfers between devices: none -> 11.4 us  [swap(): return lax.ppermute(value, axis, [(i, i ^ mask) for i in range(size)])]
    pallas_call x0 -> x6, Pallas kernels: none -> 10.2 us  [the longest x2 6.81 us: replicas(): pl.pallas_call(functools.partial(replica_kernel, half, samples, packed),...]
    ppermute x0 -> x7, waiting for transfers between devices: none -> 6.84 us  [swap(): return lax.ppermute(value, axis, [(i, i ^ mask) for i in range(size)])]
    psum x1 -> x0, blocking collectives: 5.76 us -> none  [on_device(): summed = lax.psum(jnp.sum(bin_power, 0), 'freq')]
    all_to_all x1 -> x0, starting transfers between devices: 4.24 us -> none  [on_device(): lax.all_to_all(spectra, 'freq', split_axis=0, concat_axis=3, tiled=True)]
    all_to_all x1 -> x0, waiting for transfers between devices: 2.83 us -> none  [on_device(): lax.all_to_all(spectra, 'freq', split_axis=0, concat_axis=3, tiled=True)]
  transfers between devices with their start and end apart: 1 -> 7, of which waited for: 1 -> 4; matrix products, arithmetic and copies ran while one was open for 1% -> 0% of each run, Pallas kernels for 0% -> 23%
where the time goes in v2:
time: 30.5 us; the launch traced here: 30.4 us
  starting transfers between devices  11.4 us (37%)
  Pallas kernels  10.2 us (33%)
  waiting for transfers between devices  6.84 us (22%)
  between operations  0.79 us (3%)
  other arithmetic  0.6 us (2%)
  local copies, waits for them, and re-layouts  0.58 us (2%)
    ppermute x7, starting transfers between devices, swap(): return lax.ppermute(value, axis, [(i, i ^ mask) for i in range(size)])  11.4 us
    ppermute x7, waiting for transfers between devices, swap(): return lax.ppermute(value, axis, [(i, i ^ mask) for i in range(size)])  6.84 us
    pallas_call x2, Pallas kernels, replicas(): pl.pallas_call(functools.partial(replica_kernel, half, samples, packed),...  6.81 us
    pallas_call x1, Pallas kernels, on_device(): pl.pallas_call(functools.partial(transform_kernel, half), out_shape=[pltp...  2.37 us
    pallas_call x1, Pallas kernels, on_device(): pl.pallas_call(functools.partial(product_kernel, masks, False, True), out...  0.71 us
  transfers between devices with their start and end apart: 7, of which 4 were waited for; matrix products, arithmetic and copies ran while one was open for 0% of the time, Pallas kernels for 23%

profile of v2, /device:TPU:0, one launch (start us, length us, event | category | flops | bytes accessed | tf_op | source)
XLA Modules:
  0.0 30.4 jit_solution(1540458343560857149)
XLA Ops:
  0.6 0.0 copy-start.2
  0.6 0.0 copy-start.1
  0.7 0.0 copy-start
  0.7 2.4 %shard_map.59 = (bf16[128,128]{1,0:T(8,128)(2,1)S(1)}, bf16[144,128]{1,0:T(8,128)(2,1)S(1)}) custom-call(s32[4]{0:T(128)} %bins_ref.3, s32[3,256]{1,0:T(4,128)} %points_ref.1, bf16[32,128,256]{2,1,0:T(8,128)(2,1)} %series_ref.1), custom_call_target="tpu_custom_call" | custom-call | tf_op jit(solution)/shard_map/pallas_call | solution.py:215
  3.0 3.1 %collective-permute-start = (bf16[144,128]{1,0:T(8,128)(2,1)S(1)}, bf16[144,128]{1,0:T(8,128)(2,1)S(1)}, u32[]{:S(2)}, u32[]{:S(2)}) collective-permute-start(bf16[144,128]{1,0:T(8,128)(2,1)S(1)} %get-tuple-element.5), channel_id=1, source_target_pairs={{0,1},{1,0},{2,3},{3,2},{4,5},{5,4},{6,7},{7,6},{8,9},{9,8},{10,11... | collective-permute-start | bytes 110600 | tf_op jit(solution)/shard_map/ppermute | solution.py:211
  6.1 1.9 %collective-permute-done.received_ref.points_ref = bf16[144,128]{1,0:T(8,128)(2,1)S(1)} collective-permute-done((bf16[144,128]{1,0:T(8,128)(2,1)S(1)}, bf16[144,128]{1,0:T(8,128)(2,1)S(1)}, u32[]{:S(2)}, u32[]{:S(2)}) %collective-permute-start) | collective-permute-done | bytes 36896 | tf_op jit(solution)/shard_map/ppermute | solution.py:211
  8.1 2.1 %collective-permute-start.1 = (bf16[128,256]{1,0:T(8,128)(2,1)S(1)}, bf16[128,256]{1,0:T(8,128)(2,1)S(1)}, u32[]{:S(2)}, u32[]{:S(2)}) collective-permute-start(bf16[128,256]{1,0:T(8,128)(2,1)S(1)} %shard_map.60.refs_0_), channel_id=1, source_target_pairs={{0,2},{1,3},{2,0},{3,1},{4,6},{5,7},{6,4},{7,5},{8,10},{9,11},{10,... | collective-permute-start | bytes 196616 | tf_op jit(solution)/shard_map/ppermute | solution.py:211
  10.2 2.6 %collective-permute-start.2 = (bf16[128,256]{1,0:T(8,128)(2,1)S(1)}, bf16[128,256]{1,0:T(8,128)(2,1)S(1)}, u32[]{:S(2)}, u32[]{:S(2)}) collective-permute-start(bf16[128,256]{1,0:T(8,128)(2,1)S(1)} %shard_map.60.refs_0_), channel_id=1, source_target_pairs={{0,4},{1,5},{2,6},{3,7},{4,0},{5,1},{6,2},{7,3},{8,12},{9,13},{10,... | collective-permute-start | bytes 196616 | tf_op jit(solution)/shard_map/ppermute | solution.py:211
  12.8 0.0 collective-permute-start.3
  12.8 0.0 copy-done.2
  12.8 0.0 copy-done.1
  12.8 0.0 copy-done
  12.8 3.4 %shard_map.61.refs_1_.refs_3_ = bf16[2,2,1024,256]{3,2,1,0:T(8,128)(2,1)S(1)} custom-call(s32[4]{0:T(128)S(1)} %copy-done.2, s32[3,1024]{1,0:T(4,128)S(1)} %copy-done, s32[3,256]{1,0:T(4,128)S(1)} %copy-done.1), custom_call_target="tpu_custom_call" | custom-call | tf_op jit(solution)/shard_map/pallas_call | solution.py:236
  16.2 3.4 %shard_map.62.refs_2_.refs_4_ = bf16[2,2,1024,256]{3,2,1,0:T(8,128)(2,1)S(1)} custom-call(s32[4]{0:T(128)S(1)} %copy-done.2, s32[3,1024]{1,0:T(4,128)S(1)} %copy-done, bf16[144,128]{1,0:T(8,128)(2,1)S(1)} %collective-permute-done.received_ref.points_ref), custom_call_target="tpu_custom_call" | custom-call | tf_op jit(solution)/shard_map/pallas_call | solution.py:236
  19.6 0.3 %shard_map.63.refs_5_ = f32[2,2,2,64,256]{4,3,2,1,0:T(8,128)S(1)} custom-call(bf16[128,256]{1,0:T(8,128)(2,1)S(1)} %shard_map.60.refs_0_, bf16[2,2,1024,256]{3,2,1,0:T(8,128)(2,1)S(1)} %shard_map.61.refs_1_.refs_3_, bf16[2,2,1024,256]{3,2,1,0:T(8,128)(2,1)S(1)} %shard_map.62.refs_2_.refs_4_), custom_call_target="tpu_custom_call" | custom-call | tf_op jit(solution)/shard_map/pallas_call | solution.py:254
  20.0 0.0 collective-permute-done.1.refs_0_
  20.0 0.0 collective-permute-done.2.refs_1_
  20.0 0.0 collective-permute-done.3.refs_2_
  20.0 0.7 %shard_map.64 = f32[2,2,256]{2,1,0:T(2,128)S(1)} custom-call(bf16[128,256]{1,0:T(8,128)(2,1)S(1)} %collective-permute-done.1.refs_0_, bf16[128,256]{1,0:T(8,128)(2,1)S(1)} %collective-permute-done.2.refs_1_, bf16[128,256]{1,0:T(8,128)(2,1)S(1)} %collective-permute-done.3.refs_2_, bf16[2,2,1024,256]{3,2,1,0:T(8,128)(2,1)S(1)} %shard_map.61.refs_1_.refs_3_, ...), custom_call_target="tpu_custom_call" | custom-call | tf_op jit(solution)/shard_map/pallas_call | solution.py:262
  20.7 1.8 %collective-permute-start.4 = (f32[2,256]{1,0:T(2,128)S(1)}, f32[2,256]{1,0:T(2,128)S(1)}, u32[]{:S(2)}, u32[]{:S(2)}) collective-permute-start(f32[2,256]{1,0:T(2,128)S(1)} %get-tuple-element.9), channel_id=1, source_target_pairs={{0,1},{1,0},{2,3},{3,2},{4,5},{5,4},{6,7},{7,6},{8,9},{9,8},{10,11... | collective-permute-start | bytes 6152 | tf_op jit(solution)/shard_map/ppermute | solution.py:211
  22.5 1.9 %collective-permute-done.4 = f32[2,256]{1,0:T(2,128)S(1)} collective-permute-done((f32[2,256]{1,0:T(2,128)S(1)}, f32[2,256]{1,0:T(2,128)S(1)}, u32[]{:S(2)}, u32[]{:S(2)}) %collective-permute-start.4) | collective-permute-done | bytes 2080 | tf_op jit(solution)/shard_map/ppermute | solution.py:211
  24.4 1.7 %collective-permute-start.5 = (f32[4,256]{1,0:T(4,128)S(1)}, f32[4,256]{1,0:T(4,128)S(1)}, u32[]{:S(2)}, u32[]{:S(2)}) collective-permute-start(f32[4,256]{1,0:T(4,128)S(1)} %pad_maximum_fusion), channel_id=1, source_target_pairs={{0,16},{8,24},{16,0},{24,8},{1,17},{9,25},{17,1},{25,9},{2,18},{10... | collective-permute-start | bytes 12296 | tf_op jit(solution)/shard_map/ppermute | solution.py:211
  26.1 1.9 %collective-permute-done.5 = f32[4,256]{1,0:T(4,128)S(1)} collective-permute-done((f32[4,256]{1,0:T(4,128)S(1)}, f32[4,256]{1,0:T(4,128)S(1)}, u32[]{:S(2)}, u32[]{:S(2)}) %collective-permute-start.5) | collective-permute-done | bytes 4128 | tf_op jit(solution)/shard_map/ppermute | solution.py:211
  28.0 0.1 collective-permute-start.6
  28.1 1.1 %collective-permute-done.6 = f32[4,256]{1,0:T(4,128)S(1)} collective-permute-done((f32[4,256]{1,0:T(4,128)S(1)}, f32[4,256]{1,0:T(4,128)S(1)}, u32[]{:S(2)}, u32[]{:S(2)}) %collective-permute-start.6) | collective-permute-done | bytes 4128 | tf_op jit(solution)/shard_map/ppermute | solution.py:211
  29.3 0.6 %broadcast_multiply_fusion = f32[256]{0:T(256)} fusion(f32[256]{0:T(256)S(1)} %get-tuple-element.6), kind=kLoop, calls=%fused_computation.4 | loop fusion | flops 256 | bytes 2048 | tf_op jit(solution)/shard_map/div | solution.py:278
  29.8 0.6 %constant_dynamic-slice_fusion = f32[1,256]{1,0:T(1,128)} fusion(f32[4,256]{1,0:T(4,128)S(1)} %get-tuple-element.7, s32[]{:T(128)S(6)} %select_n.16), kind=kLoop, calls=%fused_computation.5 | loop fusion | bytes 2052 | tf_op jit(solution)/shard_map/dynamic_slice | solution.py:277
  (5 shorter events, 0.1 us)
Async XLA Ops:
  0.6 12.2 %copy-start.2 = (s32[4]{0:T(128)S(1)}, s32[4]{0:T(128)}, u32[]{:S(2)}) copy-start(s32[4]{0:T(128)} %bins_ref.3) | copy-start | bytes 52
  0.6 12.2 %copy-start.1 = (s32[3,256]{1,0:T(4,128)S(1)}, s32[3,256]{1,0:T(4,128)}, u32[]{:S(2)}) copy-start(s32[3,256]{1,0:T(4,128)} %points_ref.1) | copy-start | bytes 9220
  0.7 12.2 %copy-start = (s32[3,1024]{1,0:T(4,128)S(1)}, s32[3,1024]{1,0:T(4,128)}, u32[]{:S(2)}) copy-start(s32[3,1024]{1,0:T(4,128)} %sensors_ref.3) | copy-start | bytes 36868
  3.0 5.0 %collective-permute-start = (bf16[144,128]{1,0:T(8,128)(2,1)S(1)}, bf16[144,128]{1,0:T(8,128)(2,1)S(1)}, u32[]{:S(2)}, u32[]{:S(2)}) collective-permute-start(bf16[144,128]{1,0:T(8,128)(2,1)S(1)} %get-tuple-element.5), channel_id=1, source_target_pairs={{0,1},{1,0},{2,3},{3,2},{4,5},{5,4},{6,7},{7,6},{8,9},{9,8},{10,11... | collective-permute-start | bytes 110600 | tf_op jit(solution)/shard_map/ppermute | solution.py:211
  8.1 11.9 %collective-permute-start.1 = (bf16[128,256]{1,0:T(8,128)(2,1)S(1)}, bf16[128,256]{1,0:T(8,128)(2,1)S(1)}, u32[]{:S(2)}, u32[]{:S(2)}) collective-permute-start(bf16[128,256]{1,0:T(8,128)(2,1)S(1)} %shard_map.60.refs_0_), channel_id=1, source_target_pairs={{0,2},{1,3},{2,0},{3,1},{4,6},{5,7},{6,4},{7,5},{8,10},{9,11},{10,... | collective-permute-start | bytes 196616 | tf_op jit(solution)/shard_map/ppermute | solution.py:211
  10.2 9.8 %collective-permute-start.2 = (bf16[128,256]{1,0:T(8,128)(2,1)S(1)}, bf16[128,256]{1,0:T(8,128)(2,1)S(1)}, u32[]{:S(2)}, u32[]{:S(2)}) collective-permute-start(bf16[128,256]{1,0:T(8,128)(2,1)S(1)} %shard_map.60.refs_0_), channel_id=1, source_target_pairs={{0,4},{1,5},{2,6},{3,7},{4,0},{5,1},{6,2},{7,3},{8,12},{9,13},{10,... | collective-permute-start | bytes 196616 | tf_op jit(solution)/shard_map/ppermute | solution.py:211
  12.8 7.2 %collective-permute-start.3 = (bf16[128,256]{1,0:T(8,128)(2,1)S(1)}, bf16[128,256]{1,0:T(8,128)(2,1)S(1)}, u32[]{:S(2)}, u32[]{:S(2)}) collective-permute-start(bf16[128,256]{1,0:T(8,128)(2,1)S(1)} %shard_map.60.refs_0_), channel_id=1, source_target_pairs={{0,6},{1,7},{2,4},{3,5},{4,2},{5,3},{6,0},{7,1},{8,14},{9,15},{10,... | collective-permute-start | bytes 196616 | tf_op jit(solution)/shard_map/ppermute | solution.py:211
  20.7 3.7 %collective-permute-start.4 = (f32[2,256]{1,0:T(2,128)S(1)}, f32[2,256]{1,0:T(2,128)S(1)}, u32[]{:S(2)}, u32[]{:S(2)}) collective-permute-start(f32[2,256]{1,0:T(2,128)S(1)} %get-tuple-element.9), channel_id=1, source_target_pairs={{0,1},{1,0},{2,3},{3,2},{4,5},{5,4},{6,7},{7,6},{8,9},{9,8},{10,11... | collective-permute-start | bytes 6152 | tf_op jit(solution)/shard_map/ppermute | solution.py:211
  24.4 3.6 %collective-permute-start.5 = (f32[4,256]{1,0:T(4,128)S(1)}, f32[4,256]{1,0:T(4,128)S(1)}, u32[]{:S(2)}, u32[]{:S(2)}) collective-permute-start(f32[4,256]{1,0:T(4,128)S(1)} %pad_maximum_fusion), channel_id=1, source_target_pairs={{0,16},{8,24},{16,0},{24,8},{1,17},{9,25},{17,1},{25,9},{2,18},{10... | collective-permute-start | bytes 12296 | tf_op jit(solution)/shard_map/ppermute | solution.py:211
  28.0 1.2 %collective-permute-start.6 = (f32[4,256]{1,0:T(4,128)S(1)}, f32[4,256]{1,0:T(4,128)S(1)}, u32[]{:S(2)}, u32[]{:S(2)}) collective-permute-start(f32[4,256]{1,0:T(4,128)S(1)} %fusion), channel_id=1, source_target_pairs={{0,8},{8,0},{16,24},{24,16},{1,9},{9,1},{17,25},{25,17},{2,10},{10... | collective-permute-start | bytes 12296 | tf_op jit(solution)/shard_map/ppermute | solution.py:211

commit v3 on v2

--- a/solution.py
+++ b/solution.py
@@ -20,7 +20,7 @@
 def fits():
     import numpy as np
 
-    return fit(lambda x: np.sin(math.pi * x) / x, 5), fit(lambda x: np.cos(math.pi * x), 5)
+    return fit(lambda x: np.sin(math.pi * x) / x, 4), fit(lambda x: np.cos(math.pi * x), 4)
 
 
 def horner(u, coefficients):
@@ -41,7 +41,46 @@
     return scale - s * s, s * c
 
 
-def transform_kernel(half, bins_far, points_far, series_ref, keep_ref, send_ref, bins_ref, points_ref, held, tall, sems, small_sems):
+def features(sensors_ref, places):
+    channels, points = sensors_ref.shape[1], places[0].shape[1]
+    sensors = [sensors_ref[pl.ds(a, 1), :].astype(jnp.float32) for a in range(3)]
+    s_high, s_low = split(sum(v * v for v in sensors))
+    g_high, g_low = split(sum(v * v for v in places))
+    one = jnp.ones((1, channels), jnp.float32)
+    left = jnp.concatenate([-2.0 * v for v in sensors] + [s_high, s_low, 64.0 * one, one, 0.0 * one], 0)
+    one = jnp.ones((1, points), jnp.float32)
+    right = jnp.concatenate(places + [64.0 * one, one, g_high, g_low, 0.0 * one], 0)
+    return left.T.astype(jnp.bfloat16), right.astype(jnp.bfloat16)
+
+
+def squared(left, right):
+    return lax.dot_general(left, right, (((1,), (0,)), ((), ())), preferred_element_type=jnp.float32)
+
+
+STEP = 32
+
+
+def fill(beam_ref, squares, rates):
+    scale = beam_ref.shape[2] ** (-0.5)
+
+    @pl.loop(0, squares.shape[0] // STEP)
+    def _(i):
+        span = pl.ds(pl.multiple_of(i * STEP, STEP), STEP)
+        square = squares[span, :]
+        distance = square * lax.rsqrt(jnp.maximum(square, 1.0))
+        for f, rate in rates.items():
+            real, imag = scaled_cos_sin(distance * rate, scale)
+            beam_ref[f, 0, span, :] = real.astype(jnp.bfloat16)
+            beam_ref[f, 1, span, :] = imag.astype(jnp.bfloat16)
+
+
+def rate_of(bins_ref, f, side, half, samples):
+    return bins_ref[f + side * half].astype(jnp.float32) * (2.0 / samples)
+
+
+def transform_kernel(
+    half, bins_far, points_far, series_ref, keep_ref, send_ref, bins_ref, points_ref, held, tall, sems, small_sems,
+):
     side = lax.axis_index("grid") % 2
     snaps, channels, samples = held.shape
     rows = tall.shape[0] // snaps
@@ -56,8 +95,10 @@
         pltpu.make_async_copy(bins_far, bins_ref, small_sems.at[0]),
         pltpu.make_async_copy(points_far, points_ref, small_sems.at[1]),
     ]
-    for copy in small + copies:
+    for copy in small:
         copy.start()
+    for copy in copies:
+        copy.start(priority=1)
     for copy in small:
         copy.wait()
     row = lax.broadcasted_iota(jnp.int32, (rows, samples), 0)
@@ -68,6 +109,11 @@
     turns = (number * sample).astype(jnp.float32) * (1.0 / samples)
     cosine, sine = scaled_cos_sin(turns, (samples / 2.0) ** (-0.5))
     table = jnp.where(row % 2 == 0, cosine, sine).astype(jnp.bfloat16)
+    places = [points_ref[pl.ds(a, 1), :].astype(jnp.float32) for a in range(3)]
+    extra = send_ref.shape[0] - rows // 2 * snaps
+    pieces = [v[:, p : p + channels] for v in places for p in range(0, points_ref.shape[1], channels)]
+    pieces.append(jnp.zeros((extra - len(pieces), channels), jnp.float32))
+    send_ref[pl.ds(rows // 2 * snaps, extra), :] = jnp.concatenate(pieces, 0).astype(jnp.bfloat16)
     group = 2 if channels % 128 == 0 and step % 2 == 0 else 1
     for i, copy in enumerate(copies):
         copy.wait()
@@ -80,14 +126,6 @@
         picked = tall[pl.ds(k, snaps, stride=rows), :].astype(jnp.bfloat16)
         target, base = (keep_ref, k) if k < rows // 2 else (send_ref, k - rows // 2)
         target[pl.ds(base * snaps, snaps), :] = picked
-    extra = send_ref.shape[0] - rows // 2 * snaps
-    pieces = [
-        points_ref[pl.ds(a, 1), pl.ds(p, channels)].astype(jnp.float32)
-        for a in range(points_ref.shape[0])
-        for p in range(0, points_ref.shape[1], channels)
-    ]
-    pieces.append(jnp.zeros((extra - len(pieces), channels), jnp.float32))
-    send_ref[pl.ds(rows // 2 * snaps, extra), :] = jnp.concatenate(pieces, 0).astype(jnp.bfloat16)
 
 
 def pair_kernel(keep_ref, received_ref, pair_ref):
@@ -112,41 +150,15 @@
 
 def replica_kernel(half, samples, packed, bins_ref, sensors_ref, points_ref, beam_ref, squares):
     side = lax.axis_index("grid") % 2
-    channels = sensors_ref.shape[1]
-    points = beam_ref.shape[3]
-    sensors = [sensors_ref[pl.ds(a, 1), :].astype(jnp.float32) for a in range(3)]
     if packed:
-        width = points_ref.shape[1]
-        base = points_ref.shape[0] - packed
-        tail = points_ref[pl.ds(base, packed), :].astype(jnp.float32)
-        per = points // width
+        per = beam_ref.shape[3] // points_ref.shape[1]
+        tail = points_ref[pl.ds(points_ref.shape[0] - packed, packed), :].astype(jnp.float32)
         places = [jnp.concatenate([tail[a * per + p : a * per + p + 1] for p in range(per)], 1) for a in range(3)]
     else:
         places = [points_ref[pl.ds(a, 1), :].astype(jnp.float32) for a in range(3)]
-    s_high, s_low = split(sum(v * v for v in sensors))
-    g_high, g_low = split(sum(v * v for v in places))
-    one = jnp.ones((1, channels), jnp.float32)
-    left = jnp.concatenate([-2.0 * v for v in sensors] + [s_high, s_low, 64.0 * one, one, 0.0 * one], 0)
-    one = jnp.ones((1, points), jnp.float32)
-    right = jnp.concatenate(places + [64.0 * one, one, g_high, g_low, 0.0 * one], 0)
-    squares[...] = lax.dot_general(
-        left.T.astype(jnp.bfloat16), right.astype(jnp.bfloat16), (((1,), (0,)), ((), ())),
-        preferred_element_type=jnp.float32,
-    )
-    step = 32
-    rates = [
-        bins_ref[f + side * half].astype(jnp.float32) * (2.0 / samples) for f in range(half)
-    ]
-
-    @pl.loop(0, channels // step)
-    def _(i):
-        span = pl.ds(pl.multiple_of(i * step, step), step)
-        square = squares[span, :]
-        distance = square * lax.rsqrt(jnp.maximum(square, 1.0))
-        for f in range(half):
-            real, imag = scaled_cos_sin(distance * rates[f], channels ** (-0.5))
-            beam_ref[f, 0, span, :] = real.astype(jnp.bfloat16)
-            beam_ref[f, 1, span, :] = imag.astype(jnp.bfloat16)
+    squares[...] = squared(*features(sensors_ref, places))
+    rates = {f: rate_of(bins_ref, f, side, half, samples) for f in range(half)}
+    fill(beam_ref, squares, rates)
 
 
 def product_kernel(masks, first, last, *refs):
@@ -194,6 +206,15 @@
     return [pltpu.with_memory_space_constraint(v, pltpu.VMEM) for v in values]
 
 
+def finish_kernel(snap_total, mine_ref, theirs_ref, bin_power_ref, power_ref, total_ref):
+    bin_count = bin_power_ref.shape[0]
+    half = mine_ref.shape[0] // 2
+    first = (lax.axis_index("freq") * bin_count + lax.axis_index("grid") % 2 * half) % mine_ref.shape[0]
+    total_ref[...] = (mine_ref[...] + theirs_ref[...]) / snap_total
+    bin_power_ref[...] = total_ref[pl.ds(first, bin_count), :]
+    power_ref[...] = jnp.sum(total_ref[...], 0, keepdims=True) / mine_ref.shape[0]
+
+
 def on_device(series, bins, sensor_coords, grid_coords):
     snap_local, channel_local, samples = series.shape
     all_bins = bins.shape[0]
@@ -204,14 +225,14 @@
     snap_total = snap_local * freq_size
     half = all_bins // 2
     rows = all_bins * snap_local
-    side = lax.axis_index("grid") % 2
-
-    def swap(value, axis, mask):
-        size = lax.axis_size(axis)
-        return lax.ppermute(value, axis, [(i, i ^ mask) for i in range(size)])
+
+    def swap(value, mask):
+        return lax.ppermute(value, "grid", [(i, i ^ mask) for i in range(grid_size)])
 
     packed = -(-3 * grid_local // channel_local // 16) * 16
-    chunks = 4
+    chunks = 2
+    beam_type = pltpu.VMEM((half, 2, channels, grid_local), jnp.bfloat16)
+    squares_type = pltpu.VMEM((channels, grid_local), jnp.float32)
     keep, send = pl.pallas_call(
         functools.partial(transform_kernel, half),
         out_shape=[
@@ -230,18 +251,20 @@
         ],
         compiler_params=grant(12),
     )(*[pltpu.with_memory_space_constraint(v, pltpu.HBM) for v in (bins, grid_coords, series)])
-    received = swap(send, "grid", 1)
+    received = swap(send, 1)
 
     def replicas(points, packed):
         return pl.pallas_call(
             functools.partial(replica_kernel, half, samples, packed),
-            out_shape=pltpu.VMEM((half, 2, channels, grid_local), jnp.bfloat16),
+            out_shape=beam_type,
             in_specs=[pl.BlockSpec(memory_space=pltpu.SMEM), *vmem(2)],
             out_specs=vmem(1)[0],
-            scratch_shapes=[pltpu.VMEM((channels, grid_local), jnp.float32)],
+            scratch_shapes=[squares_type],
             compiler_params=grant(12),
         )(bins, sensor_coords, points)
 
+    own_beam = replicas(grid_coords, 0)
+    received, own_beam = lax.optimization_barrier((received, own_beam))
     pair = pl.pallas_call(
         pair_kernel,
         out_shape=pltpu.VMEM((rows, 2 * channel_local), jnp.bfloat16),
@@ -249,8 +272,9 @@
         out_specs=vmem(1)[0],
         compiler_params=grant(12),
     )(*near(keep, received))
-    far = {k: swap(pair, "grid", 2 * k) for k in range(1, grid_size // 2)}
-    beams = (replicas(grid_coords, 0), replicas(*near(received), packed))
+    far = {k: swap(pair, 2 * k) for k in range(1, grid_size // 2)}
+    other_beam = replicas(*near(received), packed)
+    beams = (own_beam, other_beam)
     sums = pl.pallas_call(
         functools.partial(product_kernel, (0,), True, False),
         out_shape=pltpu.VMEM((half, 2, 2, 2 * snap_local, grid_local), jnp.float32),
@@ -266,17 +290,31 @@
         out_specs=vmem(1)[0],
         compiler_params=grant(12),
     )(*near(*[far[k] for k in masks], *beams, sums))
-    total = jnp.concatenate([powers[0], swap(powers[1], "grid", 1)], 0)
-    step = freq_size // 2
-    while step:
-        total = total + swap(total, "freq", step)
-        step //= 2
-    total = total / snap_total
-    bin_count = all_bins // freq_size
-    mine = (lax.axis_index("freq") * bin_count + side * half) % all_bins
-    bin_power = lax.dynamic_slice_in_dim(total, mine, bin_count)
-    power = jnp.sum(total, 0) / all_bins
-    return (bin_power, power)
+    def across(value, freq_mask, grid_mask):
+        every = [(f, g) for f in range(freq_size) for g in range(grid_size)]
+        index = lambda f, g: f * grid_size + g
+        pairs = [(index(f, g), index(f ^ freq_mask, g ^ grid_mask)) for f, g in every]
+        return lax.ppermute(value, ("freq", "grid"), pairs)
+
+    mine, theirs = powers[0], powers[1]
+    masks = list(range(2, freq_size, 2))
+    apart = [across(theirs, m, 1) for m in masks]
+    beside = [across(mine, m, 0) for m in masks]
+    crossed = across(theirs, 0, 1)
+    total = jnp.concatenate([sum(beside, mine), sum(apart, crossed)], 0)
+    returned = across(total, 1, 0)
+    bin_power, power = pl.pallas_call(
+        functools.partial(finish_kernel, snap_total),
+        out_shape=[
+            jax.ShapeDtypeStruct((all_bins // freq_size, grid_local), jnp.float32),
+            jax.ShapeDtypeStruct((1, grid_local), jnp.float32),
+        ],
+        in_specs=vmem(2),
+        out_specs=vmem(2),
+        scratch_shapes=[pltpu.VMEM((all_bins, grid_local), jnp.float32)],
+        compiler_params=grant(12),
+    )(*near(total, returned))
+    return (bin_power, power.reshape(grid_local))
 
 
 def solution(mesh):

time: 30.5 us -> 26.9 us (0.88)
  waiting for transfers between devices: 6.84 us -> 4.83 us
  other arithmetic: 0.6 us -> 0.02 us
  local copies, waits for them, and re-layouts: 0.58 us -> 0.02 us
    ppermute x7 -> x8, waiting for transfers between devices: 6.84 us -> 4.83 us  [the longest x4 3.64 us: across(): return lax.ppermute(value, ('freq', 'grid'), pairs)]
    pallas_call x0 -> x1, Pallas kernels: none -> 0.58 us  [on_device(): pl.pallas_call(functools.partial(finish_kernel, snap_total), out_shape=[j...]
    div x1 -> x0, other arithmetic: 0.57 us -> none  [on_device(): power = jnp.sum(total, 0) / all_bins]
    dynamic_slice x1 -> x0, local copies, waits for them, and re-layouts: 0.57 us -> none  [on_device(): bin_power = lax.dynamic_slice_in_dim(total, mine, bin_count)]
    pallas_call x2, Pallas kernels: 6.81 us -> 6.27 us  [replicas(): pl.pallas_call(functools.partial(replica_kernel, half, samples, packed),...]
    ppermute x7 -> x8, starting transfers between devices: 11.4 us -> 11.1 us  [the longest x4 7.51 us: swap(): lax.ppermute(value, 'grid', [(i, i ^ mask) for i in range(grid_size)])]
  transfers between devices with their start and end apart: 7 -> 8, of which waited for: 4 -> 4; matrix products, arithmetic and copies ran while one was open for 0% -> 0% of each run, Pallas kernels for 23% -> 25%
where the time goes in v3:
time: 26.9 us; the launch traced here: 26.7 us
  starting transfers between devices  11.1 us (41%)
  Pallas kernels  9.98 us (37%)
  waiting for transfers between devices  4.83 us (18%)
  between operations  0.74 us (3%)
    ppermute x4, starting transfers between devices, swap(): lax.ppermute(value, 'grid', [(i, i ^ mask) for i in range(grid_size)])  7.51 us
    pallas_call x2, Pallas kernels, replicas(): pl.pallas_call(functools.partial(replica_kernel, half, samples, packed),...  6.27 us
    ppermute x4, waiting for transfers between devices, across(): return lax.ppermute(value, ('freq', 'grid'), pairs)  3.64 us
    ppermute x4, starting transfers between devices, across(): return lax.ppermute(value, ('freq', 'grid'), pairs)  3.62 us
    pallas_call x1, Pallas kernels, on_device(): pl.pallas_call(functools.partial(transform_kernel, half), out_shape=[pltp...  2.09 us
    ppermute x4, waiting for transfers between devices, swap(): lax.ppermute(value, 'grid', [(i, i ^ mask) for i in range(grid_size)])  1.19 us
    pallas_call x1, Pallas kernels, on_device(): pl.pallas_call(functools.partial(product_kernel, masks, False, True), out...  0.69 us
    pallas_call x1, Pallas kernels, on_device(): pl.pallas_call(functools.partial(finish_kernel, snap_total), out_shape=[j...  0.58 us
  transfers between devices with their start and end apart: 8, of which 4 were waited for; matrix products, arithmetic and copies ran while one was open for 0% of the time, Pallas kernels for 25%

profile of v3, /device:TPU:0, one launch (start us, length us, event | category | flops | bytes accessed | tf_op | source)
XLA Modules:
  0.0 26.7 jit_solution(4372649252149380131)
XLA Ops:
  0.6 0.0 copy-start.2
  0.6 0.0 copy-start.1
  0.7 0.0 copy-start
  0.7 2.1 %shard_map.59 = (bf16[128,128]{1,0:T(8,128)(2,1)S(1)}, bf16[144,128]{1,0:T(8,128)(2,1)S(1)}) custom-call(s32[4]{0:T(128)} %bins_ref.3, s32[3,256]{1,0:T(4,128)} %points_ref.1, bf16[32,128,256]{2,1,0:T(8,128)(2,1)} %series_ref.1), custom_call_target="tpu_custom_call" | custom-call | tf_op jit(solution)/shard_map/pallas_call | solution.py:236
  2.8 3.1 %collective-permute-start = (bf16[144,128]{1,0:T(8,128)(2,1)S(1)}, bf16[144,128]{1,0:T(8,128)(2,1)S(1)}, u32[]{:S(2)}, u32[]{:S(2)}) collective-permute-start(bf16[144,128]{1,0:T(8,128)(2,1)S(1)} %get-tuple-element.9), channel_id=1, source_target_pairs={{0,1},{1,0},{2,3},{3,2},{4,5},{5,4},{6,7},{7,6},{8,9},{9,8},{10,11... | collective-permute-start | bytes 110600 | tf_op jit(solution)/shard_map/ppermute | solution.py:230
  5.8 0.0 copy-done.2
  5.8 0.0 copy-done.1
  5.8 0.0 copy-done
  5.8 3.1 %shard_map.60.refs_1_.refs_3_ = bf16[2,2,1024,256]{3,2,1,0:T(8,128)(2,1)S(1)} custom-call(s32[4]{0:T(128)S(1)} %copy-done.2, s32[3,1024]{1,0:T(4,128)S(1)} %copy-done, s32[3,256]{1,0:T(4,128)S(1)} %copy-done.1), custom_call_target="tpu_custom_call" | custom-call | tf_op jit(solution)/shard_map/pallas_call | solution.py:257
  9.0 0.0 collective-permute-done.received_ref.points_ref
  9.0 3.7 %collective-permute-start.3 = (bf16[128,256]{1,0:T(8,128)(2,1)S(1)}, bf16[128,256]{1,0:T(8,128)(2,1)S(1)}, u32[]{:S(2)}, u32[]{:S(2)}) collective-permute-start(bf16[128,256]{1,0:T(8,128)(2,1)S(1)} %shard_map.61.refs_0_), channel_id=1, source_target_pairs={{0,6},{1,7},{2,4},{3,5},{4,2},{5,3},{6,0},{7,1},{8,14},{9,15},{10,... | collective-permute-start | bytes 196616 | tf_op jit(solution)/shard_map/ppermute | solution.py:230
  12.7 0.0 collective-permute-start.2
  12.7 0.8 %collective-permute-start.1 = (bf16[128,256]{1,0:T(8,128)(2,1)S(1)}, bf16[128,256]{1,0:T(8,128)(2,1)S(1)}, u32[]{:S(2)}, u32[]{:S(2)}) collective-permute-start(bf16[128,256]{1,0:T(8,128)(2,1)S(1)} %shard_map.61.refs_0_), channel_id=1, source_target_pairs={{0,2},{1,3},{2,0},{3,1},{4,6},{5,7},{6,4},{7,5},{8,10},{9,11},{10,... | collective-permute-start | bytes 196616 | tf_op jit(solution)/shard_map/ppermute | solution.py:230
  13.5 3.1 %shard_map.62.refs_2_.refs_4_ = bf16[2,2,1024,256]{3,2,1,0:T(8,128)(2,1)S(1)} custom-call(s32[4]{0:T(128)S(1)} %copy-done.2, s32[3,1024]{1,0:T(4,128)S(1)} %copy-done, bf16[144,128]{1,0:T(8,128)(2,1)S(1)} %collective-permute-done.received_ref.points_ref), custom_call_target="tpu_custom_call" | custom-call | tf_op jit(solution)/shard_map/pallas_call | solution.py:257
  16.6 0.3 %shard_map.63.refs_5_ = f32[2,2,2,64,256]{4,3,2,1,0:T(8,128)S(1)} custom-call(bf16[128,256]{1,0:T(8,128)(2,1)S(1)} %shard_map.61.refs_0_, bf16[2,2,1024,256]{3,2,1,0:T(8,128)(2,1)S(1)} %shard_map.60.refs_1_.refs_3_, bf16[2,2,1024,256]{3,2,1,0:T(8,128)(2,1)S(1)} %shard_map.62.refs_2_.refs_4_), custom_call_target="tpu_custom_call" | custom-call | tf_op jit(solution)/shard_map/pallas_call | solution.py:278
  16.9 0.0 collective-permute-done.3.refs_2_
  16.9 1.2 %collective-permute-done.2.refs_1_ = bf16[128,256]{1,0:T(8,128)(2,1)S(1)} collective-permute-done((bf16[128,256]{1,0:T(8,128)(2,1)S(1)}, bf16[128,256]{1,0:T(8,128)(2,1)S(1)}, u32[]{:S(2)}, u32[]{:S(2)}) %collective-permute-start.2) | collective-permute-done | bytes 65568 | tf_op jit(solution)/shard_map/ppermute | solution.py:230
  18.1 0.0 collective-permute-done.1.refs_0_
  18.1 0.7 %shard_map.64 = f32[2,2,256]{2,1,0:T(2,128)S(1)} custom-call(bf16[128,256]{1,0:T(8,128)(2,1)S(1)} %collective-permute-done.1.refs_0_, bf16[128,256]{1,0:T(8,128)(2,1)S(1)} %collective-permute-done.2.refs_1_, bf16[128,256]{1,0:T(8,128)(2,1)S(1)} %collective-permute-done.3.refs_2_, bf16[2,2,1024,256]{3,2,1,0:T(8,128)(2,1)S(1)} %shard_map.60.refs_1_.refs_3_, ...), custom_call_target="tpu_custom_call" | custom-call | tf_op jit(solution)/shard_map/pallas_call | solution.py:286
  18.8 1.6 %collective-permute-start.4 = (f32[2,256]{1,0:T(2,128)S(1)}, f32[2,256]{1,0:T(2,128)S(1)}, u32[]{:S(2)}, u32[]{:S(2)}) collective-permute-start(f32[2,256]{1,0:T(2,128)S(1)} %get-tuple-element.14), channel_id=1, source_target_pairs={{0,16},{1,17},{2,18},{3,19},{4,20},{5,21},{6,22},{7,23},{8,24},{9,... | collective-permute-start | bytes 6152 | tf_op jit(solution)/shard_map/ppermute | solution.py:297
  20.4 0.6 %collective-permute-start.6 = (f32[2,256]{1,0:T(2,128)S(1)}, f32[2,256]{1,0:T(2,128)S(1)}, u32[]{:S(2)}, u32[]{:S(2)}) collective-permute-start(f32[2,256]{1,0:T(2,128)S(1)} %get-tuple-element.15), channel_id=1, source_target_pairs={{0,17},{1,16},{2,19},{3,18},{4,21},{5,20},{6,23},{7,22},{8,25},{9,... | collective-permute-start | bytes 6152 | tf_op jit(solution)/shard_map/ppermute | solution.py:297
  21.0 1.4 %collective-permute-start.5 = (f32[2,256]{1,0:T(2,128)S(1)}, f32[2,256]{1,0:T(2,128)S(1)}, u32[]{:S(2)}, u32[]{:S(2)}) collective-permute-start(f32[2,256]{1,0:T(2,128)S(1)} %get-tuple-element.15), channel_id=1, source_target_pairs={{0,1},{1,0},{2,3},{3,2},{4,5},{5,4},{6,7},{7,6},{8,9},{9,8},{10,11... | collective-permute-start | bytes 6152 | tf_op jit(solution)/shard_map/ppermute | solution.py:297
  22.4 0.1 collective-permute-done.4
  22.5 2.4 %collective-permute-done.6 = f32[2,256]{1,0:T(2,128)S(1)} collective-permute-done((f32[2,256]{1,0:T(2,128)S(1)}, f32[2,256]{1,0:T(2,128)S(1)}, u32[]{:S(2)}, u32[]{:S(2)}) %collective-permute-start.6) | collective-permute-done | bytes 2080 | tf_op jit(solution)/shard_map/ppermute | solution.py:297
  24.9 0.0 collective-permute-done.5
  24.9 0.1 collective-permute-start.7
  25.0 1.2 %collective-permute-done.7.theirs_ref = f32[4,256]{1,0:T(4,128)S(1)} collective-permute-done((f32[4,256]{1,0:T(4,128)S(1)}, f32[4,256]{1,0:T(4,128)S(1)}, u32[]{:S(2)}, u32[]{:S(2)}) %collective-permute-start.7) | collective-permute-done | bytes 4128 | tf_op jit(solution)/shard_map/ppermute | solution.py:297
  26.1 0.6 %shard_map.65 = (f32[1,256]{1,0:T(1,128)}, f32[1,256]{1,0:T(1,128)}) custom-call(f32[4,256]{1,0:T(4,128)S(1)} %pad_maximum_fusion.mine_ref, f32[4,256]{1,0:T(4,128)S(1)} %collective-permute-done.7.theirs_ref), custom_call_target="tpu_custom_call" | custom-call | tf_op jit(solution)/shard_map/pallas_call | solution.py:306
  (5 shorter events, 0.1 us)
Async XLA Ops:
  0.6 5.2 %copy-start.2 = (s32[4]{0:T(128)S(1)}, s32[4]{0:T(128)}, u32[]{:S(2)}) copy-start(s32[4]{0:T(128)} %bins_ref.3) | copy-start | bytes 52
  0.6 5.2 %copy-start.1 = (s32[3,256]{1,0:T(4,128)S(1)}, s32[3,256]{1,0:T(4,128)}, u32[]{:S(2)}) copy-start(s32[3,256]{1,0:T(4,128)} %points_ref.1) | copy-start | bytes 9220
  0.7 5.2 %copy-start = (s32[3,1024]{1,0:T(4,128)S(1)}, s32[3,1024]{1,0:T(4,128)}, u32[]{:S(2)}) copy-start(s32[3,1024]{1,0:T(4,128)} %sensors_ref.3) | copy-start | bytes 36868
  2.8 6.2 %collective-permute-start = (bf16[144,128]{1,0:T(8,128)(2,1)S(1)}, bf16[144,128]{1,0:T(8,128)(2,1)S(1)}, u32[]{:S(2)}, u32[]{:S(2)}) collective-permute-start(bf16[144,128]{1,0:T(8,128)(2,1)S(1)} %get-tuple-element.9), channel_id=1, source_target_pairs={{0,1},{1,0},{2,3},{3,2},{4,5},{5,4},{6,7},{7,6},{8,9},{9,8},{10,11... | collective-permute-start | bytes 110600 | tf_op jit(solution)/shard_map/ppermute | solution.py:230
  9.0 7.9 %collective-permute-start.3 = (bf16[128,256]{1,0:T(8,128)(2,1)S(1)}, bf16[128,256]{1,0:T(8,128)(2,1)S(1)}, u32[]{:S(2)}, u32[]{:S(2)}) collective-permute-start(bf16[128,256]{1,0:T(8,128)(2,1)S(1)} %shard_map.61.refs_0_), channel_id=1, source_target_pairs={{0,6},{1,7},{2,4},{3,5},{4,2},{5,3},{6,0},{7,1},{8,14},{9,15},{10,... | collective-permute-start | bytes 196616 | tf_op jit(solution)/shard_map/ppermute | solution.py:230
  12.7 5.4 %collective-permute-start.2 = (bf16[128,256]{1,0:T(8,128)(2,1)S(1)}, bf16[128,256]{1,0:T(8,128)(2,1)S(1)}, u32[]{:S(2)}, u32[]{:S(2)}) collective-permute-start(bf16[128,256]{1,0:T(8,128)(2,1)S(1)} %shard_map.61.refs_0_), channel_id=1, source_target_pairs={{0,4},{1,5},{2,6},{3,7},{4,0},{5,1},{6,2},{7,3},{8,12},{9,13},{10,... | collective-permute-start | bytes 196616 | tf_op jit(solution)/shard_map/ppermute | solution.py:230
  12.7 5.4 %collective-permute-start.1 = (bf16[128,256]{1,0:T(8,128)(2,1)S(1)}, bf16[128,256]{1,0:T(8,128)(2,1)S(1)}, u32[]{:S(2)}, u32[]{:S(2)}) collective-permute-start(bf16[128,256]{1,0:T(8,128)(2,1)S(1)} %shard_map.61.refs_0_), channel_id=1, source_target_pairs={{0,2},{1,3},{2,0},{3,1},{4,6},{5,7},{6,4},{7,5},{8,10},{9,11},{10,... | collective-permute-start | bytes 196616 | tf_op jit(solution)/shard_map/ppermute | solution.py:230
  18.8 3.7 %collective-permute-start.4 = (f32[2,256]{1,0:T(2,128)S(1)}, f32[2,256]{1,0:T(2,128)S(1)}, u32[]{:S(2)}, u32[]{:S(2)}) collective-permute-start(f32[2,256]{1,0:T(2,128)S(1)} %get-tuple-element.14), channel_id=1, source_target_pairs={{0,16},{1,17},{2,18},{3,19},{4,20},{5,21},{6,22},{7,23},{8,24},{9,... | collective-permute-start | bytes 6152 | tf_op jit(solution)/shard_map/ppermute | solution.py:297
  20.4 4.5 %collective-permute-start.6 = (f32[2,256]{1,0:T(2,128)S(1)}, f32[2,256]{1,0:T(2,128)S(1)}, u32[]{:S(2)}, u32[]{:S(2)}) collective-permute-start(f32[2,256]{1,0:T(2,128)S(1)} %get-tuple-element.15), channel_id=1, source_target_pairs={{0,17},{1,16},{2,19},{3,18},{4,21},{5,20},{6,23},{7,22},{8,25},{9,... | collective-permute-start | bytes 6152 | tf_op jit(solution)/shard_map/ppermute | solution.py:297
  21.0 3.9 %collective-permute-start.5 = (f32[2,256]{1,0:T(2,128)S(1)}, f32[2,256]{1,0:T(2,128)S(1)}, u32[]{:S(2)}, u32[]{:S(2)}) collective-permute-start(f32[2,256]{1,0:T(2,128)S(1)} %get-tuple-element.15), channel_id=1, source_target_pairs={{0,1},{1,0},{2,3},{3,2},{4,5},{5,4},{6,7},{7,6},{8,9},{9,8},{10,11... | collective-permute-start | bytes 6152 | tf_op jit(solution)/shard_map/ppermute | solution.py:297
  24.9 1.2 %collective-permute-start.7 = (f32[4,256]{1,0:T(4,128)S(1)}, f32[4,256]{1,0:T(4,128)S(1)}, u32[]{:S(2)}, u32[]{:S(2)}) collective-permute-start(f32[4,256]{1,0:T(4,128)S(1)} %pad_maximum_fusion.mine_ref), channel_id=1, source_target_pairs={{0,8},{1,9},{2,10},{3,11},{4,12},{5,13},{6,14},{7,15},{8,0},{9,1},... | collective-permute-start | bytes 12296 | tf_op jit(solution)/shard_map/ppermute | solution.py:297

commit v4 on v0

v4 whole, which is shorter than its diff:
```python
import functools
import math

import jax
import jax.numpy as jnp
from jax import lax
from jax.experimental import pallas as pl
from jax.experimental.pallas import tpu as pltpu
from jax.sharding import PartitionSpec as P


def fit(function, degree):
    import numpy as np

    nodes = 0.125 + 0.125 * np.cos(math.pi * (np.arange(degree + 1) + 0.5) / (degree + 1))
    matrix = np.vander(nodes, degree + 1, increasing=True)
    return [float(v) for v in np.linalg.solve(matrix, function(np.sqrt(nodes)))]


def fits():
    import numpy as np

    return fit(lambda x: np.sin(math.pi * x) / x, 4), fit(lambda x: np.cos(math.pi * x), 4)


def horner(u, coefficients):
    total = coefficients[-1]
    for value in coefficients[-2::-1]:
        total = total * u + value
    return total


def scaled_cos_sin(turns, scale):
    whole = (turns + 12582912.0) - 12582912.0
    x = turns - whole
    u = x * x
    sine, cosine = fits()
    root = math.sqrt(2.0 * scale)
    s = x * horner(u, [v * root for v in sine])
    c = horner(u, [-v * root for v in cosine])
    return scale - s * s, s * c


def features(sensors_ref, places):
    channels, points = sensors_ref.shape[1], places[0].shape[1]
    sensors = [sensors_ref[pl.ds(a, 1), :].astype(jnp.float32) for a in range(3)]
    s_high, s_low = split(sum(v * v for v in sensors))
    g_high, g_low = split(sum(v * v for v in places))
    one = jnp.ones((1, channels), jnp.float32)
    left = jnp.concatenate([-2.0 * v for v in sensors] + [s_high, s_low, 64.0 * one, one, 0.0 * one], 0)
    one = jnp.ones((1, points), jnp.float32)
    right = jnp.concatenate(places + [64.0 * one, one, g_high, g_low, 0.0 * one], 0)
    return left.T.astype(jnp.bfloat16), right.astype(jnp.bfloat16)


def squared(left, right):
    return lax.dot_general(left, right, (((1,), (0,)), ((), ())), preferred_element_type=jnp.float32)


STEP = 32


def fill(beam_ref, squares, rates):
    scale = beam_ref.shape[2] ** (-0.5)

    @pl.loop(0, squares.shape[0] // STEP)
    def _(i):
        span = pl.ds(pl.multiple_of(i * STEP, STEP), STEP)
        square = squares[span, :]
        distance = square * lax.rsqrt(jnp.maximum(square, 1.0))
        for f in range(beam_ref.shape[0]):
            real, imag = scaled_cos_sin(distance * rates[f], scale)
            beam_ref[f, 0, span, :] = real.astype(jnp.bfloat16)
            beam_ref[f, 1, span, :] = imag.astype(jnp.bfloat16)


def bin_at(bins_ref, f):
    return bins_ref[:, f : f + 1].astype(jnp.float32)


def transform_kernel(bins_far, series_ref, spectra_ref, bins_ref, held, tall, sems, small_sem):
    snaps, channels, samples = held.shape
    rows = tall.shape[0] // snaps
    all_bins = rows // 2
    chunks = sems.shape[0]
    step = snaps // chunks
    copies = [
        pltpu.make_async_copy(series_ref.at[pl.ds(i * step, step)], held.at[pl.ds(i * step, step)], sems.at[i])
        for i in range(chunks)
    ]
    small = pltpu.make_async_copy(bins_far, bins_ref, small_sem)
    small.start()
    for copy in copies:
        copy.start(priority=1)
    small.wait()
    row = lax.broadcasted_iota(jnp.int32, (rows, samples), 0)
    sample = lax.broadcasted_iota(jnp.int32, (rows, samples), 1)
    number = jnp.zeros((rows, samples), jnp.float32)
    for f in range(all_bins):
        number = jnp.where(row // 2 == f, bin_at(bins_ref, f), number)
    turns = number * sample.astype(jnp.float32) * (1.0 / samples)
    cosine, sine = scaled_cos_sin(turns, (samples / 2.0) ** (-0.5))
    table = jnp.where(row % 2 == 0, cosine, sine).astype(jnp.bfloat16)
    group = 2 if channels % 128 == 0 and step % 2 == 0 else 1
    for i, copy in enumerate(copies):
        copy.wait()
        for s in range(i * step, (i + 1) * step, group):
            block = held[s : s + group].reshape(group * channels, samples)
            out = lax.dot_general(table, block, (((1,), (1,)), ((), ())), preferred_element_type=jnp.float32)
            for p in range(group):
                tall[pl.ds((s + p) * rows, rows), :] = out[:, p * channels : (p + 1) * channels]
    for k in range(rows):
        picked = tall[pl.ds(k, snaps, stride=rows), :].astype(jnp.bfloat16)
        spectra_ref[pl.ds(k * snaps, snaps), :] = picked


def stack_kernel(*refs):
    out = refs[-1]
    for k, ref in enumerate(refs[:-1]):
        out[pl.ds(k * ref.shape[0], ref.shape[0]), :] = ref[...]


def split(value):
    high = jnp.floor(value * (1.0 / 64.0))
    return high, value - 64.0 * high


def replica_kernel(bins, samples, first, bins_ref, sensors_ref, points_ref, *refs):
    if first:
        beam_ref, squares, rates = refs
        places = [points_ref[pl.ds(a, 1), :].astype(jnp.float32) for a in range(3)]
        squares[...] = squared(*features(sensors_ref, places))
    else:
        squares, beam_ref, rates = refs
    for i, f in enumerate(bins):
        rates[i] = jnp.broadcast_to(bin_at(bins_ref, f) * (2.0 / samples), rates.shape[1:])
    fill(beam_ref, squares, rates)


def product_kernel(masks, last, *refs):
    blocks, beams, rest = refs[: len(masks)], refs[len(masks) : len(masks) + 2], refs[len(masks) + 2 :]
    out = rest[-1]
    sums = rest[0] if last else out
    place = lax.axis_index("grid")
    half = beams[0].shape[0]
    depth = blocks[0].shape[1]
    rows = sums.shape[2]
    snaps = rows // 2
    for f in range(2 * half):
        beam = beams[f // half]
        totals = []
        for part in range(2):
            total = rest[0][f, part] if last else None
            for block, inside in zip(blocks, masks):
                for i, mask in enumerate(inside):
                    start = pl.multiple_of((place ^ mask) * depth, depth)
                    term = jnp.dot(
                        block[pl.ds((i * 2 * half + f) * rows, rows), :], beam[f % half, part, pl.ds(start, depth), :],
                        preferred_element_type=jnp.float32,
                    )
                    total = term if total is None else total + term
            totals.append(total)
        if last:
            real = totals[0][:snaps] + totals[1][snaps:]
            imag = totals[0][snaps:] - totals[1][:snaps]
            out[pl.ds(f, 1), :] = jnp.sum(real * real + imag * imag, 0, keepdims=True)
        else:
            for part in range(2):
                out[f, part] = totals[part]


def vmem(n):
    return [pl.BlockSpec(memory_space=pltpu.VMEM)] * n


def grant(mib):
    return pltpu.CompilerParams(vmem_limit_bytes=mib << 20)


def near(*values):
    return [pltpu.with_memory_space_constraint(v, pltpu.VMEM) for v in values]


def finish_kernel(snap_total, mine_ref, theirs_ref, bin_power_ref, power_ref, total_ref):
    bin_count = bin_power_ref.shape[0]
    total_ref[...] = (mine_ref[...] + theirs_ref[...]) / snap_total
    bin_power_ref[...] = total_ref[pl.ds(lax.axis_index("freq") * bin_count, bin_count), :]
    power_ref[...] = jnp.sum(total_ref[...], 0, keepdims=True) / mine_ref.shape[0]


def on_device(series, bins, sensor_coords, grid_coords):
    snap_local, channel_local, samples = series.shape
    all_bins = bins.shape[0]
    channels = sensor_coords.shape[1]
    grid_local = grid_coords.shape[1]
    freq_size = lax.axis_size("freq")
    grid_size = lax.axis_size("grid")
    snap_total = snap_local * freq_size
    half = all_bins // 2
    rows = 2 * all_bins * snap_local

    def swap(value, axis, mask):
        size = lax.axis_size(axis)
        return lax.ppermute(value, axis, [(i, i ^ mask) for i in range(size)])

    def call(kernel, out_shape, inputs, scratch=(), near_inputs=True):
        outs = out_shape if isinstance(out_shape, list) else [out_shape]
        result = pl.pallas_call(
            kernel,
            out_shape=outs,
            in_specs=vmem(len(inputs)) if near_inputs else [pl.BlockSpec(memory_space=pl.ANY)] * len(inputs),
            out_specs=vmem(len(outs)),
            scratch_shapes=scratch,
            compiler_params=grant(12),
        )(*inputs)
        return result if isinstance(out_shape, list) else result[0]

    chunks = 2
    bins_row = bins.reshape(1, all_bins)
    spectra = call(
        transform_kernel,
        pltpu.VMEM((rows, channel_local), jnp.bfloat16),
        [pltpu.with_memory_space_constraint(v, pltpu.HBM) for v in (bins_row, series)],
        [
            pltpu.VMEM((1, all_bins), jnp.int32),
            pltpu.VMEM(series.shape, jnp.bfloat16),
            pltpu.VMEM((rows, channel_local), jnp.float32),
            pltpu.SemaphoreType.DMA((chunks,)),
            pltpu.SemaphoreType.DMA,
        ],
        near_inputs=False,
    )
    far = []
    for k in range(1, grid_size // 2):
        far.append(swap(spectra, "grid", 2 * k))
    near_spectra = swap(spectra, "grid", 1)
    beam_type = pltpu.VMEM((half, 2, channels, grid_local), jnp.bfloat16)
    squares_type = pltpu.VMEM((channels, grid_local), jnp.float32)
    rates_type = pltpu.VMEM((half, STEP, grid_local), jnp.float32)
    beam0, squares = call(
        functools.partial(replica_kernel, range(half), samples, True),
        [beam_type, squares_type], [bins_row, sensor_coords, grid_coords], [rates_type],
    )
    stacked = call(stack_kernel, pltpu.VMEM((len(far) * rows, channel_local), jnp.bfloat16), near(*far))
    rest = swap(stacked, "grid", 1)
    beam1 = call(
        functools.partial(replica_kernel, range(half, all_bins), samples, False),
        beam_type, [bins_row, sensor_coords, grid_coords, *near(squares)], [rates_type],
    )
    masks = [2 * k for k in range(1, grid_size // 2)]
    sums = call(
        functools.partial(product_kernel, [[0], *[[m] for m in masks], [1]], False),
        pltpu.VMEM((all_bins, 2, 2 * snap_local, grid_local), jnp.float32),
        near(spectra, *far, near_spectra, beam0, beam1),
    )
    total = call(
        functools.partial(product_kernel, [[m + 1 for m in masks]], True),
        pltpu.VMEM((all_bins, grid_local), jnp.float32),
        near(rest, beam0, beam1, sums),
    )
    step = freq_size // 2
    while step > 1:
        total += swap(total, "freq", step)
        step //= 2
    bin_power, power = call(
        functools.partial(finish_kernel, snap_total),
        [
            jax.ShapeDtypeStruct((all_bins // freq_size, grid_local), jnp.float32),
            jax.ShapeDtypeStruct((1, grid_local), jnp.float32),
        ],
        near(total, swap(total, "freq", 1)),
        [pltpu.VMEM((all_bins, grid_local), jnp.float32)],
    )
    return (bin_power, power.reshape(grid_local))


def solution(mesh):
    return jax.shard_map(
        on_device,
        mesh=mesh,
        in_specs=(P("freq", "grid", None), P(), P(), P(None, "grid")),
        out_specs=(P("freq", "grid"), P("grid")),
        check_vma=False,
    )
```

time: 64.5 us -> 28.2 us (0.44)
  blocking collectives: 34.5 us -> 0 us
  matrix products: 17.7 us -> 0 us
  Pallas kernels: 0 us -> 8.56 us
  waiting for transfers between devices: 2.83 us -> 9.36 us
  starting transfers between devices: 4.24 us -> 9.36 us
  local copies, waits for them, and re-layouts: 1.93 us -> 0.01 us
  other arithmetic: 1.51 us -> 0.01 us
  between operations: 1.41 us -> 0.72 us
    all_gather x1 -> x0, blocking collectives: 28.8 us -> none  [on_device(): gathered = lax.all_gather(regrouped, 'grid', axis=2, tiled=True)]
    dot_general x5 -> x0, matrix products: 17.7 us -> none  [the longest x4 17.1 us: product(): jnp.einsum('fgc,fcs->fgs', left, right, preferred_element_type=jnp.float32)]
    ppermute x0 -> x7, starting transfers between devices: none -> 9.36 us  [swap(): return lax.ppermute(value, axis, [(i, i ^ mask) for i in range(size)])]
    ppermute x0 -> x7, waiting for transfers between devices: none -> 9.36 us  [swap(): return lax.ppermute(value, axis, [(i, i ^ mask) for i in range(size)])]
    pallas_call x0 -> x7, Pallas kernels: none -> 8.56 us  [call(): pl.pallas_call(kernel, out_shape=outs, in_specs=vmem(len(inputs)) if near...]
    psum x1 -> x0, blocking collectives: 5.76 us -> none  [on_device(): summed = lax.psum(jnp.sum(bin_power, 0), 'freq')]
    all_to_all x1 -> x0, starting transfers between devices: 4.24 us -> none  [on_device(): lax.all_to_all(spectra, 'freq', split_axis=0, concat_axis=3, tiled=True)]
    all_to_all x1 -> x0, waiting for transfers between devices: 2.83 us -> none  [on_device(): lax.all_to_all(spectra, 'freq', split_axis=0, concat_axis=3, tiled=True)]
  transfers between devices with their start and end apart: 1 -> 7, of which waited for: 1 -> 4; matrix products, arithmetic and copies ran while one was open for 1% -> 0% of each run, Pallas kernels for 0% -> 20%
where the time goes in v4:
time: 28.2 us; the launch traced here: 28 us
  starting transfers between devices  9.36 us (33%)
  waiting for transfers between devices  9.36 us (33%)
  Pallas kernels  8.56 us (30%)
  between operations  0.72 us (3%)
    ppermute x7, starting transfers between devices, swap(): return lax.ppermute(value, axis, [(i, i ^ mask) for i in range(size)])  9.36 us
    ppermute x7, waiting for transfers between devices, swap(): return lax.ppermute(value, axis, [(i, i ^ mask) for i in range(size)])  9.36 us
    pallas_call x7, Pallas kernels, call(): pl.pallas_call(kernel, out_shape=outs, in_specs=vmem(len(inputs)) if near...  8.56 us
  transfers between devices with their start and end apart: 7, of which 4 were waited for; matrix products, arithmetic and copies ran while one was open for 0% of the time, Pallas kernels for 20%

profile of v4, /device:TPU:0, one launch (start us, length us, event | category | flops | bytes accessed | tf_op | source)
XLA Modules:
  0.0 28.0 jit_solution(13974451540514134964)
XLA Ops:
  0.6 0.0 copy-start.2
  0.6 0.0 copy-start
  0.7 0.0 copy-start.1
  0.7 2.1 %shard_map.59.refs_0_ = bf16[256,128]{1,0:T(8,128)(2,1)S(1)} custom-call(s32[1,4]{1,0:T(1,128)} %bitcast.2, bf16[32,128,256]{2,1,0:T(8,128)(2,1)} %series_ref.1), custom_call_target="tpu_custom_call" | custom-call | tf_op jit(solution)/shard_map/pallas_call | solution.py:208
  2.7 3.1 %collective-permute-start = (bf16[256,128]{1,0:T(8,128)(2,1)S(1)}, bf16[256,128]{1,0:T(8,128)(2,1)S(1)}, u32[]{:S(2)}, u32[]{:S(2)}) collective-permute-start(bf16[256,128]{1,0:T(8,128)(2,1)S(1)} %shard_map.59.refs_0_), channel_id=1, source_target_pairs={{0,2},{1,3},{2,0},{3,1},{4,6},{5,7},{6,4},{7,5},{8,10},{9,11},{10,... | collective-permute-start | bytes 196616 | tf_op jit(solution)/shard_map/ppermute | solution.py:204
  5.9 2.6 %collective-permute-start.1 = (bf16[256,128]{1,0:T(8,128)(2,1)S(1)}, bf16[256,128]{1,0:T(8,128)(2,1)S(1)}, u32[]{:S(2)}, u32[]{:S(2)}) collective-permute-start(bf16[256,128]{1,0:T(8,128)(2,1)S(1)} %shard_map.59.refs_0_), channel_id=1, source_target_pairs={{0,4},{1,5},{2,6},{3,7},{4,0},{5,1},{6,2},{7,3},{8,12},{9,13},{10,... | collective-permute-start | bytes 196616 | tf_op jit(solution)/shard_map/ppermute | solution.py:204
  8.5 0.0 collective-permute-start.2
  8.5 0.0 collective-permute-done.refs_0_.refs_1_
  8.5 4.7 %collective-permute-done.1.refs_1_.refs_2_ = bf16[256,128]{1,0:T(8,128)(2,1)S(1)} collective-permute-done((bf16[256,128]{1,0:T(8,128)(2,1)S(1)}, bf16[256,128]{1,0:T(8,128)(2,1)S(1)}, u32[]{:S(2)}, u32[]{:S(2)}) %collective-permute-start.1) | collective-permute-done | bytes 65568 | tf_op jit(solution)/shard_map/ppermute | solution.py:204
  13.1 1.4 %collective-permute-done.2.refs_2_.refs_3_ = bf16[256,128]{1,0:T(8,128)(2,1)S(1)} collective-permute-done((bf16[256,128]{1,0:T(8,128)(2,1)S(1)}, bf16[256,128]{1,0:T(8,128)(2,1)S(1)}, u32[]{:S(2)}, u32[]{:S(2)}) %collective-permute-start.2) | collective-permute-done | bytes 65568 | tf_op jit(solution)/shard_map/ppermute | solution.py:204
  14.5 1.6 %collective-permute-start.3 = (bf16[768,128]{1,0:T(8,128)(2,1)S(1)}, bf16[768,128]{1,0:T(8,128)(2,1)S(1)}, u32[]{:S(2)}, u32[]{:S(2)}) collective-permute-start(bf16[768,128]{1,0:T(8,128)(2,1)S(1)} %shard_map.60), channel_id=1, source_target_pairs={{0,1},{1,0},{2,3},{3,2},{4,5},{5,4},{6,7},{7,6},{8,9},{9,8},{10,11... | collective-permute-start | bytes 589832 | tf_op jit(solution)/shard_map/ppermute | solution.py:204
  16.1 0.5 %collective-permute-start.4 = (bf16[256,128]{1,0:T(8,128)(2,1)S(1)}, bf16[256,128]{1,0:T(8,128)(2,1)S(1)}, u32[]{:S(2)}, u32[]{:S(2)}) collective-permute-start(bf16[256,128]{1,0:T(8,128)(2,1)S(1)} %shard_map.59.refs_0_), channel_id=1, source_target_pairs={{0,1},{1,0},{2,3},{3,2},{4,5},{5,4},{6,7},{7,6},{8,9},{9,8},{10,11... | collective-permute-start | bytes 196616 | tf_op jit(solution)/shard_map/ppermute | solution.py:204
  16.6 0.0 copy-done.2
  16.6 0.0 copy-done
  16.6 0.0 copy-done.1
  16.6 2.7 %shard_map.61 = (bf16[2,2,1024,256]{3,2,1,0:T(8,128)(2,1)S(1)}, f32[1024,256]{1,0:T(8,128)S(1)}) custom-call(s32[1,4]{1,0:T(1,128)S(1)} %bitcast.3, s32[3,1024]{1,0:T(4,128)S(1)} %copy-done, s32[3,256]{1,0:T(4,128)S(1)} %copy-done.1), custom_call_target="tpu_custom_call" | custom-call | tf_op jit(solution)/shard_map/pallas_call | solution.py:208
  19.3 2.4 %shard_map.62.refs_6_.refs_2_ = bf16[2,2,1024,256]{3,2,1,0:T(8,128)(2,1)S(1)} custom-call(s32[1,4]{1,0:T(1,128)S(1)} %bitcast.4, s32[3,1024]{1,0:T(4,128)S(1)} %copy-done, s32[3,256]{1,0:T(4,128)S(1)} %copy-done.1, f32[1024,256]{1,0:T(8,128)S(1)} %get-tuple-element.7.refs_0_), custom_call_target="tpu_custom_call" | custom-call | tf_op jit(solution)/shard_map/pallas_call | solution.py:208
  21.7 0.0 collective-permute-done.4.refs_4_
  21.7 0.5 %shard_map.63.refs_3_ = f32[4,2,64,256]{3,2,1,0:T(8,128)S(1)} custom-call(bf16[256,128]{1,0:T(8,128)(2,1)S(1)} %shard_map.59.refs_0_, bf16[256,128]{1,0:T(8,128)(2,1)S(1)} %collective-permute-done.refs_0_.refs_1_, bf16[256,128]{1,0:T(8,128)(2,1)S(1)} %collective-permute-done.1.refs_1_.refs_2_, bf16[256,128]{1,0:T(8,128)(2,1)S(1)} %collective-permute-done.2.refs_2_.refs_3_, ...), custom_call_target="tpu_custom_call" | custom-call | tf_op jit(solution)/shard_map/pallas_call | solution.py:208
  22.2 0.0 collective-permute-done.3.refs_0_
  22.2 0.4 %shard_map.64 = f32[4,256]{1,0:T(4,128)S(1)} custom-call(bf16[768,128]{1,0:T(8,128)(2,1)S(1)} %collective-permute-done.3.refs_0_, bf16[2,2,1024,256]{3,2,1,0:T(8,128)(2,1)S(1)} %get-tuple-element.6.refs_5_.refs_1_, bf16[2,2,1024,256]{3,2,1,0:T(8,128)(2,1)S(1)} %shard_map.62.refs_6_.refs_2_, f32[4,2,64,256]{3,2,1,0:T(8,128)S(1)} %shard_map.63.refs_3_), custom_call_target="tpu_custom_call" | custom-call | tf_op jit(solution)/shard_map/pallas_call | solution.py:208
  22.6 1.6 %collective-permute-start.5 = (f32[4,256]{1,0:T(4,128)S(1)}, f32[4,256]{1,0:T(4,128)S(1)}, u32[]{:S(2)}, u32[]{:S(2)}) collective-permute-start(f32[4,256]{1,0:T(4,128)S(1)} %shard_map.64), channel_id=1, source_target_pairs={{0,16},{8,24},{16,0},{24,8},{1,17},{9,25},{17,1},{25,9},{2,18},{10... | collective-permute-start | bytes 12296 | tf_op jit(solution)/shard_map/ppermute | solution.py:204
  24.1 2.1 %collective-permute-done.5 = f32[4,256]{1,0:T(4,128)S(1)} collective-permute-done((f32[4,256]{1,0:T(4,128)S(1)}, f32[4,256]{1,0:T(4,128)S(1)}, u32[]{:S(2)}, u32[]{:S(2)}) %collective-permute-start.5) | collective-permute-done | bytes 4128 | tf_op jit(solution)/shard_map/ppermute | solution.py:204
  26.3 0.0 collective-permute-start.6
  26.3 1.2 %collective-permute-done.6.theirs_ref = f32[4,256]{1,0:T(4,128)S(1)} collective-permute-done((f32[4,256]{1,0:T(4,128)S(1)}, f32[4,256]{1,0:T(4,128)S(1)}, u32[]{:S(2)}, u32[]{:S(2)}) %collective-permute-start.6) | collective-permute-done | bytes 4128 | tf_op jit(solution)/shard_map/ppermute | solution.py:204
  27.4 0.6 %shard_map.65 = (f32[1,256]{1,0:T(1,128)}, f32[1,256]{1,0:T(1,128)}) custom-call(f32[4,256]{1,0:T(4,128)S(1)} %add.3.mine_ref, f32[4,256]{1,0:T(4,128)S(1)} %collective-permute-done.6.theirs_ref), custom_call_target="tpu_custom_call" | custom-call | tf_op jit(solution)/shard_map/pallas_call | solution.py:208
  (2 shorter events, 0.0 us)
Async XLA Ops:
  0.6 16.0 %copy-start.2 = (s32[4]{0:T(128)S(1)}, s32[4]{0:T(128)}, u32[]{:S(2)}) copy-start(s32[4]{0:T(128)} %param.5) | copy-start | bytes 52
  0.6 16.0 %copy-start = (s32[3,1024]{1,0:T(4,128)S(1)}, s32[3,1024]{1,0:T(4,128)}, u32[]{:S(2)}) copy-start(s32[3,1024]{1,0:T(4,128)} %sensors_ref.3) | copy-start | bytes 36868
  0.7 16.0 %copy-start.1 = (s32[3,256]{1,0:T(4,128)S(1)}, s32[3,256]{1,0:T(4,128)}, u32[]{:S(2)}) copy-start(s32[3,256]{1,0:T(4,128)} %points_ref.3) | copy-start | bytes 9220
  2.7 5.7 %collective-permute-start = (bf16[256,128]{1,0:T(8,128)(2,1)S(1)}, bf16[256,128]{1,0:T(8,128)(2,1)S(1)}, u32[]{:S(2)}, u32[]{:S(2)}) collective-permute-start(bf16[256,128]{1,0:T(8,128)(2,1)S(1)} %shard_map.59.refs_0_), channel_id=1, source_target_pairs={{0,2},{1,3},{2,0},{3,1},{4,6},{5,7},{6,4},{7,5},{8,10},{9,11},{10,... | collective-permute-start | bytes 196616 | tf_op jit(solution)/shard_map/ppermute | solution.py:204
  5.9 7.3 %collective-permute-start.1 = (bf16[256,128]{1,0:T(8,128)(2,1)S(1)}, bf16[256,128]{1,0:T(8,128)(2,1)S(1)}, u32[]{:S(2)}, u32[]{:S(2)}) collective-permute-start(bf16[256,128]{1,0:T(8,128)(2,1)S(1)} %shard_map.59.refs_0_), channel_id=1, source_target_pairs={{0,4},{1,5},{2,6},{3,7},{4,0},{5,1},{6,2},{7,3},{8,12},{9,13},{10,... | collective-permute-start | bytes 196616 | tf_op jit(solution)/shard_map/ppermute | solution.py:204
  8.5 6.1 %collective-permute-start.2 = (bf16[256,128]{1,0:T(8,128)(2,1)S(1)}, bf16[256,128]{1,0:T(8,128)(2,1)S(1)}, u32[]{:S(2)}, u32[]{:S(2)}) collective-permute-start(bf16[256,128]{1,0:T(8,128)(2,1)S(1)} %shard_map.59.refs_0_), channel_id=1, source_target_pairs={{0,6},{1,7},{2,4},{3,5},{4,2},{5,3},{6,0},{7,1},{8,14},{9,15},{10,... | collective-permute-start | bytes 196616 | tf_op jit(solution)/shard_map/ppermute | solution.py:204
  14.5 7.6 %collective-permute-start.3 = (bf16[768,128]{1,0:T(8,128)(2,1)S(1)}, bf16[768,128]{1,0:T(8,128)(2,1)S(1)}, u32[]{:S(2)}, u32[]{:S(2)}) collective-permute-start(bf16[768,128]{1,0:T(8,128)(2,1)S(1)} %shard_map.60), channel_id=1, source_target_pairs={{0,1},{1,0},{2,3},{3,2},{4,5},{5,4},{6,7},{7,6},{8,9},{9,8},{10,11... | collective-permute-start | bytes 589832 | tf_op jit(solution)/shard_map/ppermute | solution.py:204
  16.1 5.5 %collective-permute-start.4 = (bf16[256,128]{1,0:T(8,128)(2,1)S(1)}, bf16[256,128]{1,0:T(8,128)(2,1)S(1)}, u32[]{:S(2)}, u32[]{:S(2)}) collective-permute-start(bf16[256,128]{1,0:T(8,128)(2,1)S(1)} %shard_map.59.refs_0_), channel_id=1, source_target_pairs={{0,1},{1,0},{2,3},{3,2},{4,5},{5,4},{6,7},{7,6},{8,9},{9,8},{10,11... | collective-permute-start | bytes 196616 | tf_op jit(solution)/shard_map/ppermute | solution.py:204
  22.6 3.7 %collective-permute-start.5 = (f32[4,256]{1,0:T(4,128)S(1)}, f32[4,256]{1,0:T(4,128)S(1)}, u32[]{:S(2)}, u32[]{:S(2)}) collective-permute-start(f32[4,256]{1,0:T(4,128)S(1)} %shard_map.64), channel_id=1, source_target_pairs={{0,16},{8,24},{16,0},{24,8},{1,17},{9,25},{17,1},{25,9},{2,18},{10... | collective-permute-start | bytes 12296 | tf_op jit(solution)/shard_map/ppermute | solution.py:204
  26.3 1.2 %collective-permute-start.6 = (f32[4,256]{1,0:T(4,128)S(1)}, f32[4,256]{1,0:T(4,128)S(1)}, u32[]{:S(2)}, u32[]{:S(2)}) collective-permute-start(f32[4,256]{1,0:T(4,128)S(1)} %add.3.mine_ref), channel_id=1, source_target_pairs={{0,8},{8,0},{16,24},{24,16},{1,9},{9,1},{17,25},{25,17},{2,10},{10... | collective-permute-start | bytes 12296 | tf_op jit(solution)/shard_map/ppermute | solution.py:204

commit v5 on v4

--- a/solution.py
+++ b/solution.py
@@ -181,9 +181,9 @@
     return [pltpu.with_memory_space_constraint(v, pltpu.VMEM) for v in values]
 
 
-def finish_kernel(snap_total, mine_ref, theirs_ref, bin_power_ref, power_ref, total_ref):
+def finish_kernel(snap_total, mine_ref, second_ref, third_ref, fourth_ref, bin_power_ref, power_ref, total_ref):
     bin_count = bin_power_ref.shape[0]
-    total_ref[...] = (mine_ref[...] + theirs_ref[...]) / snap_total
+    total_ref[...] = ((mine_ref[...] + second_ref[...]) + (third_ref[...] + fourth_ref[...])) / snap_total
     bin_power_ref[...] = total_ref[pl.ds(lax.axis_index("freq") * bin_count, bin_count), :]
     power_ref[...] = jnp.sum(total_ref[...], 0, keepdims=True) / mine_ref.shape[0]
 
@@ -230,9 +230,13 @@
         ],
         near_inputs=False,
     )
-    far = []
+    far = {}
     for k in range(1, grid_size // 2):
-        far.append(swap(spectra, "grid", 2 * k))
+        far[k] = swap(spectra, "grid", 2 * k)
+
+    def stack(*values):
+        return call(stack_kernel, pltpu.VMEM((len(values) * rows, channel_local), jnp.bfloat16), near(*values))
+
     near_spectra = swap(spectra, "grid", 1)
     beam_type = pltpu.VMEM((half, 2, channels, grid_local), jnp.bfloat16)
     squares_type = pltpu.VMEM((channels, grid_local), jnp.float32)
@@ -241,34 +245,35 @@
         functools.partial(replica_kernel, range(half), samples, True),
         [beam_type, squares_type], [bins_row, sensor_coords, grid_coords], [rates_type],
     )
-    stacked = call(stack_kernel, pltpu.VMEM((len(far) * rows, channel_local), jnp.bfloat16), near(*far))
-    rest = swap(stacked, "grid", 1)
+    rest = swap(stack(*far.values()), "grid", 1)
     beam1 = call(
         functools.partial(replica_kernel, range(half, all_bins), samples, False),
         beam_type, [bins_row, sensor_coords, grid_coords, *near(squares)], [rates_type],
     )
-    masks = [2 * k for k in range(1, grid_size // 2)]
     sums = call(
-        functools.partial(product_kernel, [[0], *[[m] for m in masks], [1]], False),
+        functools.partial(product_kernel, [[0], *[[2 * k] for k in far], [1]], False),
         pltpu.VMEM((all_bins, 2, 2 * snap_local, grid_local), jnp.float32),
-        near(spectra, *far, near_spectra, beam0, beam1),
+        near(spectra, *far.values(), near_spectra, beam0, beam1),
     )
     total = call(
-        functools.partial(product_kernel, [[m + 1 for m in masks]], True),
+        functools.partial(product_kernel, [[2 * k + 1 for k in far]], True),
         pltpu.VMEM((all_bins, grid_local), jnp.float32),
         near(rest, beam0, beam1, sums),
     )
     step = freq_size // 2
-    while step > 1:
+    while step > 2:
         total += swap(total, "freq", step)
         step //= 2
+    others = []
+    for mask in (2, 3, 1):
+        others.append(swap(total, "freq", mask))
     bin_power, power = call(
         functools.partial(finish_kernel, snap_total),
         [
             jax.ShapeDtypeStruct((all_bins // freq_size, grid_local), jnp.float32),
             jax.ShapeDtypeStruct((1, grid_local), jnp.float32),
         ],
-        near(total, swap(total, "freq", 1)),
+        near(total, *others),
         [pltpu.VMEM((all_bins, grid_local), jnp.float32)],
     )
     return (bin_power, power.reshape(grid_local))

time: 28.2 us -> 27.9 us (0.989)
  waiting for transfers between devices: 9.36 us -> 8.46 us
  starting transfers between devices: 9.36 us -> 10 us
    ppermute x7 -> x8, waiting for transfers between devices: 9.36 us -> 8.46 us  [swap(): return lax.ppermute(value, axis, [(i, i ^ mask) for i in range(size)])]
    ppermute x7 -> x8, starting transfers between devices: 9.36 us -> 10 us  [swap(): return lax.ppermute(value, axis, [(i, i ^ mask) for i in range(size)])]
  transfers between devices with their start and end apart: 7 -> 8, of which waited for: 4 -> 4; matrix products, arithmetic and copies ran while one was open for 0% -> 0% of each run, Pallas kernels for 20% -> 20%
where the time goes in v5:
time: 27.9 us; the launch traced here: 27.8 us
  starting transfers between devices  10 us (36%)
  Pallas kernels  8.56 us (31%)
  waiting for transfers between devices  8.46 us (30%)
  between operations  0.72 us (3%)
    ppermute x8, starting transfers between devices, swap(): return lax.ppermute(value, axis, [(i, i ^ mask) for i in range(size)])  10 us
    pallas_call x7, Pallas kernels, call(): pl.pallas_call(kernel, out_shape=outs, in_specs=vmem(len(inputs)) if near...  8.56 us
    ppermute x8, waiting for transfers between devices, swap(): return lax.ppermute(value, axis, [(i, i ^ mask) for i in range(size)])  8.46 us
  transfers between devices with their start and end apart: 8, of which 4 were waited for; matrix products, arithmetic and copies ran while one was open for 0% of the time, Pallas kernels for 20%

profile of v5, /device:TPU:0, one launch (start us, length us, event | category | flops | bytes accessed | tf_op | source)
XLA Modules:
  0.0 27.8 jit_solution(16685812748862426278)
XLA Ops:
  0.6 0.0 copy-start.2
  0.6 0.0 copy-start
  0.7 0.0 copy-start.1
  0.7 2.1 %shard_map.59.refs_0_ = bf16[256,128]{1,0:T(8,128)(2,1)S(1)} custom-call(s32[1,4]{1,0:T(1,128)} %bitcast.2, bf16[32,128,256]{2,1,0:T(8,128)(2,1)} %series_ref.1), custom_call_target="tpu_custom_call" | custom-call | tf_op jit(solution)/shard_map/pallas_call | solution.py:208
  2.7 3.1 %collective-permute-start = (bf16[256,128]{1,0:T(8,128)(2,1)S(1)}, bf16[256,128]{1,0:T(8,128)(2,1)S(1)}, u32[]{:S(2)}, u32[]{:S(2)}) collective-permute-start(bf16[256,128]{1,0:T(8,128)(2,1)S(1)} %shard_map.59.refs_0_), channel_id=1, source_target_pairs={{0,2},{1,3},{2,0},{3,1},{4,6},{5,7},{6,4},{7,5},{8,10},{9,11},{10,... | collective-permute-start | bytes 196616 | tf_op jit(solution)/shard_map/ppermute | solution.py:204
  5.9 2.6 %collective-permute-start.1 = (bf16[256,128]{1,0:T(8,128)(2,1)S(1)}, bf16[256,128]{1,0:T(8,128)(2,1)S(1)}, u32[]{:S(2)}, u32[]{:S(2)}) collective-permute-start(bf16[256,128]{1,0:T(8,128)(2,1)S(1)} %shard_map.59.refs_0_), channel_id=1, source_target_pairs={{0,4},{1,5},{2,6},{3,7},{4,0},{5,1},{6,2},{7,3},{8,12},{9,13},{10,... | collective-permute-start | bytes 196616 | tf_op jit(solution)/shard_map/ppermute | solution.py:204
  8.5 0.0 collective-permute-start.2
  8.5 0.0 collective-permute-done.refs_0_.refs_1_
  8.5 4.7 %collective-permute-done.1.refs_1_.refs_2_ = bf16[256,128]{1,0:T(8,128)(2,1)S(1)} collective-permute-done((bf16[256,128]{1,0:T(8,128)(2,1)S(1)}, bf16[256,128]{1,0:T(8,128)(2,1)S(1)}, u32[]{:S(2)}, u32[]{:S(2)}) %collective-permute-start.1) | collective-permute-done | bytes 65568 | tf_op jit(solution)/shard_map/ppermute | solution.py:204
  13.1 1.4 %collective-permute-done.2.refs_2_.refs_3_ = bf16[256,128]{1,0:T(8,128)(2,1)S(1)} collective-permute-done((bf16[256,128]{1,0:T(8,128)(2,1)S(1)}, bf16[256,128]{1,0:T(8,128)(2,1)S(1)}, u32[]{:S(2)}, u32[]{:S(2)}) %collective-permute-start.2) | collective-permute-done | bytes 65568 | tf_op jit(solution)/shard_map/ppermute | solution.py:204
  14.5 1.6 %collective-permute-start.3 = (bf16[768,128]{1,0:T(8,128)(2,1)S(1)}, bf16[768,128]{1,0:T(8,128)(2,1)S(1)}, u32[]{:S(2)}, u32[]{:S(2)}) collective-permute-start(bf16[768,128]{1,0:T(8,128)(2,1)S(1)} %shard_map.60), channel_id=1, source_target_pairs={{0,1},{1,0},{2,3},{3,2},{4,5},{5,4},{6,7},{7,6},{8,9},{9,8},{10,11... | collective-permute-start | bytes 589832 | tf_op jit(solution)/shard_map/ppermute | solution.py:204
  16.1 0.5 %collective-permute-start.4 = (bf16[256,128]{1,0:T(8,128)(2,1)S(1)}, bf16[256,128]{1,0:T(8,128)(2,1)S(1)}, u32[]{:S(2)}, u32[]{:S(2)}) collective-permute-start(bf16[256,128]{1,0:T(8,128)(2,1)S(1)} %shard_map.59.refs_0_), channel_id=1, source_target_pairs={{0,1},{1,0},{2,3},{3,2},{4,5},{5,4},{6,7},{7,6},{8,9},{9,8},{10,11... | collective-permute-start | bytes 196616 | tf_op jit(solution)/shard_map/ppermute | solution.py:204
  16.6 0.0 copy-done.2
  16.6 0.0 copy-done
  16.6 0.0 copy-done.1
  16.6 2.7 %shard_map.61 = (bf16[2,2,1024,256]{3,2,1,0:T(8,128)(2,1)S(1)}, f32[1024,256]{1,0:T(8,128)S(1)}) custom-call(s32[1,4]{1,0:T(1,128)S(1)} %bitcast.3, s32[3,1024]{1,0:T(4,128)S(1)} %copy-done, s32[3,256]{1,0:T(4,128)S(1)} %copy-done.1), custom_call_target="tpu_custom_call" | custom-call | tf_op jit(solution)/shard_map/pallas_call | solution.py:208
  19.3 2.4 %shard_map.62.refs_6_.refs_2_ = bf16[2,2,1024,256]{3,2,1,0:T(8,128)(2,1)S(1)} custom-call(s32[1,4]{1,0:T(1,128)S(1)} %bitcast.4, s32[3,1024]{1,0:T(4,128)S(1)} %copy-done, s32[3,256]{1,0:T(4,128)S(1)} %copy-done.1, f32[1024,256]{1,0:T(8,128)S(1)} %get-tuple-element.7.refs_0_), custom_call_target="tpu_custom_call" | custom-call | tf_op jit(solution)/shard_map/pallas_call | solution.py:208
  21.7 0.0 collective-permute-done.4.refs_4_
  21.7 0.5 %shard_map.63.refs_3_ = f32[4,2,64,256]{3,2,1,0:T(8,128)S(1)} custom-call(bf16[256,128]{1,0:T(8,128)(2,1)S(1)} %shard_map.59.refs_0_, bf16[256,128]{1,0:T(8,128)(2,1)S(1)} %collective-permute-done.refs_0_.refs_1_, bf16[256,128]{1,0:T(8,128)(2,1)S(1)} %collective-permute-done.1.refs_1_.refs_2_, bf16[256,128]{1,0:T(8,128)(2,1)S(1)} %collective-permute-done.2.refs_2_.refs_3_, ...), custom_call_target="tpu_custom_call" | custom-call | tf_op jit(solution)/shard_map/pallas_call | solution.py:208
  22.2 0.0 collective-permute-done.3.refs_0_
  22.2 0.4 %shard_map.64.mine_ref = f32[4,256]{1,0:T(4,128)S(1)} custom-call(bf16[768,128]{1,0:T(8,128)(2,1)S(1)} %collective-permute-done.3.refs_0_, bf16[2,2,1024,256]{3,2,1,0:T(8,128)(2,1)S(1)} %get-tuple-element.6.refs_5_.refs_1_, bf16[2,2,1024,256]{3,2,1,0:T(8,128)(2,1)S(1)} %shard_map.62.refs_6_.refs_2_, f32[4,2,64,256]{3,2,1,0:T(8,128)S(1)} %shard_map.63.refs_3_), custom_call_target="tpu_custom_call" | custom-call | tf_op jit(solution)/shard_map/pallas_call | solution.py:208
  22.6 1.6 %collective-permute-start.5 = (f32[4,256]{1,0:T(4,128)S(1)}, f32[4,256]{1,0:T(4,128)S(1)}, u32[]{:S(2)}, u32[]{:S(2)}) collective-permute-start(f32[4,256]{1,0:T(4,128)S(1)} %shard_map.64.mine_ref), channel_id=1, source_target_pairs={{0,16},{8,24},{16,0},{24,8},{1,17},{9,25},{17,1},{25,9},{2,18},{10... | collective-permute-start | bytes 12296 | tf_op jit(solution)/shard_map/ppermute | solution.py:204
  24.1 0.0 collective-permute-start.6
  24.1 0.6 %collective-permute-start.7 = (f32[4,256]{1,0:T(4,128)S(1)}, f32[4,256]{1,0:T(4,128)S(1)}, u32[]{:S(2)}, u32[]{:S(2)}) collective-permute-start(f32[4,256]{1,0:T(4,128)S(1)} %shard_map.64.mine_ref), channel_id=1, source_target_pairs={{0,8},{8,0},{16,24},{24,16},{1,9},{9,1},{17,25},{25,17},{2,10},{10... | collective-permute-start | bytes 12296 | tf_op jit(solution)/shard_map/ppermute | solution.py:204
  24.8 1.5 %collective-permute-done.5.second_ref = f32[4,256]{1,0:T(4,128)S(1)} collective-permute-done((f32[4,256]{1,0:T(4,128)S(1)}, f32[4,256]{1,0:T(4,128)S(1)}, u32[]{:S(2)}, u32[]{:S(2)}) %collective-permute-start.5) | collective-permute-done | bytes 4128 | tf_op jit(solution)/shard_map/ppermute | solution.py:204
  26.3 0.9 %collective-permute-done.6.third_ref = f32[4,256]{1,0:T(4,128)S(1)} collective-permute-done((f32[4,256]{1,0:T(4,128)S(1)}, f32[4,256]{1,0:T(4,128)S(1)}, u32[]{:S(2)}, u32[]{:S(2)}) %collective-permute-start.6) | collective-permute-done | bytes 4128 | tf_op jit(solution)/shard_map/ppermute | solution.py:204
  27.2 0.0 collective-permute-done.7.fourth_ref
  27.2 0.6 %shard_map.65 = (f32[1,256]{1,0:T(1,128)}, f32[1,256]{1,0:T(1,128)}) custom-call(f32[4,256]{1,0:T(4,128)S(1)} %shard_map.64.mine_ref, f32[4,256]{1,0:T(4,128)S(1)} %collective-permute-done.5.second_ref, f32[4,256]{1,0:T(4,128)S(1)} %collective-permute-done.6.third_ref, f32[4,256]{1,0:T(4,128)S(1)} %collective-permute-done.7.fourth_ref), custom_call_target="tpu_custom_call" | custom-call | tf_op jit(solution)/shard_map/pallas_call | solution.py:208
  (1 shorter events, 0.0 us)
Async XLA Ops:
  0.6 16.0 %copy-start.2 = (s32[4]{0:T(128)S(1)}, s32[4]{0:T(128)}, u32[]{:S(2)}) copy-start(s32[4]{0:T(128)} %param.5) | copy-start | bytes 52
  0.6 16.0 %copy-start = (s32[3,1024]{1,0:T(4,128)S(1)}, s32[3,1024]{1,0:T(4,128)}, u32[]{:S(2)}) copy-start(s32[3,1024]{1,0:T(4,128)} %sensors_ref.3) | copy-start | bytes 36868
  0.7 16.0 %copy-start.1 = (s32[3,256]{1,0:T(4,128)S(1)}, s32[3,256]{1,0:T(4,128)}, u32[]{:S(2)}) copy-start(s32[3,256]{1,0:T(4,128)} %points_ref.3) | copy-start | bytes 9220
  2.7 5.7 %collective-permute-start = (bf16[256,128]{1,0:T(8,128)(2,1)S(1)}, bf16[256,128]{1,0:T(8,128)(2,1)S(1)}, u32[]{:S(2)}, u32[]{:S(2)}) collective-permute-start(bf16[256,128]{1,0:T(8,128)(2,1)S(1)} %shard_map.59.refs_0_), channel_id=1, source_target_pairs={{0,2},{1,3},{2,0},{3,1},{4,6},{5,7},{6,4},{7,5},{8,10},{9,11},{10,... | collective-permute-start | bytes 196616 | tf_op jit(solution)/shard_map/ppermute | solution.py:204
  5.9 7.3 %collective-permute-start.1 = (bf16[256,128]{1,0:T(8,128)(2,1)S(1)}, bf16[256,128]{1,0:T(8,128)(2,1)S(1)}, u32[]{:S(2)}, u32[]{:S(2)}) collective-permute-start(bf16[256,128]{1,0:T(8,128)(2,1)S(1)} %shard_map.59.refs_0_), channel_id=1, source_target_pairs={{0,4},{1,5},{2,6},{3,7},{4,0},{5,1},{6,2},{7,3},{8,12},{9,13},{10,... | collective-permute-start | bytes 196616 | tf_op jit(solution)/shard_map/ppermute | solution.py:204
  8.5 6.1 %collective-permute-start.2 = (bf16[256,128]{1,0:T(8,128)(2,1)S(1)}, bf16[256,128]{1,0:T(8,128)(2,1)S(1)}, u32[]{:S(2)}, u32[]{:S(2)}) collective-permute-start(bf16[256,128]{1,0:T(8,128)(2,1)S(1)} %shard_map.59.refs_0_), channel_id=1, source_target_pairs={{0,6},{1,7},{2,4},{3,5},{4,2},{5,3},{6,0},{7,1},{8,14},{9,15},{10,... | collective-permute-start | bytes 196616 | tf_op jit(solution)/shard_map/ppermute | solution.py:204
  14.5 7.6 %collective-permute-start.3 = (bf16[768,128]{1,0:T(8,128)(2,1)S(1)}, bf16[768,128]{1,0:T(8,128)(2,1)S(1)}, u32[]{:S(2)}, u32[]{:S(2)}) collective-permute-start(bf16[768,128]{1,0:T(8,128)(2,1)S(1)} %shard_map.60), channel_id=1, source_target_pairs={{0,1},{1,0},{2,3},{3,2},{4,5},{5,4},{6,7},{7,6},{8,9},{9,8},{10,11... | collective-permute-start | bytes 589832 | tf_op jit(solution)/shard_map/ppermute | solution.py:204
  16.1 5.5 %collective-permute-start.4 = (bf16[256,128]{1,0:T(8,128)(2,1)S(1)}, bf16[256,128]{1,0:T(8,128)(2,1)S(1)}, u32[]{:S(2)}, u32[]{:S(2)}) collective-permute-start(bf16[256,128]{1,0:T(8,128)(2,1)S(1)} %shard_map.59.refs_0_), channel_id=1, source_target_pairs={{0,1},{1,0},{2,3},{3,2},{4,5},{5,4},{6,7},{7,6},{8,9},{9,8},{10,11... | collective-permute-start | bytes 196616 | tf_op jit(solution)/shard_map/ppermute | solution.py:204
  22.6 3.7 %collective-permute-start.5 = (f32[4,256]{1,0:T(4,128)S(1)}, f32[4,256]{1,0:T(4,128)S(1)}, u32[]{:S(2)}, u32[]{:S(2)}) collective-permute-start(f32[4,256]{1,0:T(4,128)S(1)} %shard_map.64.mine_ref), channel_id=1, source_target_pairs={{0,16},{8,24},{16,0},{24,8},{1,17},{9,25},{17,1},{25,9},{2,18},{10... | collective-permute-start | bytes 12296 | tf_op jit(solution)/shard_map/ppermute | solution.py:204
  24.1 3.0 %collective-permute-start.6 = (f32[4,256]{1,0:T(4,128)S(1)}, f32[4,256]{1,0:T(4,128)S(1)}, u32[]{:S(2)}, u32[]{:S(2)}) collective-permute-start(f32[4,256]{1,0:T(4,128)S(1)} %shard_map.64.mine_ref), channel_id=1, source_target_pairs={{0,24},{8,16},{16,8},{24,0},{1,25},{9,17},{17,9},{25,1},{2,26},{10... | collective-permute-start | bytes 12296 | tf_op jit(solution)/shard_map/ppermute | solution.py:204
  24.1 3.0 %collective-permute-start.7 = (f32[4,256]{1,0:T(4,128)S(1)}, f32[4,256]{1,0:T(4,128)S(1)}, u32[]{:S(2)}, u32[]{:S(2)}) collective-permute-start(f32[4,256]{1,0:T(4,128)S(1)} %shard_map.64.mine_ref), channel_id=1, source_target_pairs={{0,8},{8,0},{16,24},{24,16},{1,9},{9,1},{17,25},{25,17},{2,10},{10... | collective-permute-start | bytes 12296 | tf_op jit(solution)/shard_map/ppermute | solution.py:204

commit v6 on v5

--- a/solution.py
+++ b/solution.py
@@ -17,10 +17,10 @@
     return [float(v) for v in np.linalg.solve(matrix, function(np.sqrt(nodes)))]
 
 
-def fits():
+def half_sine():
     import numpy as np
 
-    return fit(lambda x: np.sin(math.pi * x) / x, 4), fit(lambda x: np.cos(math.pi * x), 4)
+    return fit(lambda x: np.sin(math.pi * x) / x, 4)
 
 
 def horner(u, coefficients):
@@ -33,12 +33,11 @@
 def scaled_cos_sin(turns, scale):
     whole = (turns + 12582912.0) - 12582912.0
     x = turns - whole
-    u = x * x
-    sine, cosine = fits()
     root = math.sqrt(2.0 * scale)
-    s = x * horner(u, [v * root for v in sine])
-    c = horner(u, [-v * root for v in cosine])
-    return scale - s * s, s * c
+    s = x * horner(x * x, [-v * root for v in half_sine()])
+    real = scale - s * s
+    rest = jnp.maximum(real + scale, 1e-30)
+    return real, s * (rest * lax.rsqrt(rest))
 
 
 def features(sensors_ref, places):
@@ -57,28 +56,34 @@
     return lax.dot_general(left, right, (((1,), (0,)), ((), ())), preferred_element_type=jnp.float32)
 
 
-STEP = 32
+STEP = 64
+TOGETHER = 1
 
 
 def fill(beam_ref, squares, rates):
-    scale = beam_ref.shape[2] ** (-0.5)
-
-    @pl.loop(0, squares.shape[0] // STEP)
+    channels = squares.shape[0]
+    scale = channels ** (-0.5)
+    together = TOGETHER if channels % (STEP * TOGETHER) == 0 else 1
+
+    @pl.loop(0, channels // (STEP * together))
     def _(i):
-        span = pl.ds(pl.multiple_of(i * STEP, STEP), STEP)
-        square = squares[span, :]
-        distance = square * lax.rsqrt(jnp.maximum(square, 1.0))
-        for f in range(beam_ref.shape[0]):
-            real, imag = scaled_cos_sin(distance * rates[f], scale)
-            beam_ref[f, 0, span, :] = real.astype(jnp.bfloat16)
-            beam_ref[f, 1, span, :] = imag.astype(jnp.bfloat16)
+        for part in range(together):
+            span = pl.ds(pl.multiple_of((i * together + part) * STEP, STEP), STEP)
+            square = squares[span, :]
+            distance = square * lax.rsqrt(jnp.maximum(square, 1.0))
+            for f in range(beam_ref.shape[0]):
+                real, imag = scaled_cos_sin(distance * rates[f], scale)
+                beam_ref[f, 0, span, :] = real.astype(jnp.bfloat16)
+                beam_ref[f, 1, span, :] = imag.astype(jnp.bfloat16)
 
 
 def bin_at(bins_ref, f):
     return bins_ref[:, f : f + 1].astype(jnp.float32)
 
 
-def transform_kernel(bins_far, series_ref, spectra_ref, bins_ref, held, tall, sems, small_sem):
+def transform_kernel(
+    bins_far, sensors_far, points_far, series_ref, spectra_ref, bins_ref, sensors_ref, points_ref, held, tall, sems, small_sems
+):
     snaps, channels, samples = held.shape
     rows = tall.shape[0] // snaps
     all_bins = rows // 2
@@ -88,11 +93,16 @@
         pltpu.make_async_copy(series_ref.at[pl.ds(i * step, step)], held.at[pl.ds(i * step, step)], sems.at[i])
         for i in range(chunks)
     ]
-    small = pltpu.make_async_copy(bins_far, bins_ref, small_sem)
-    small.start()
+    small = [
+        pltpu.make_async_copy(a, b, small_sems.at[i])
+        for i, (a, b) in enumerate([(bins_far, bins_ref), (sensors_far, sensors_ref), (points_far, points_ref)])
+    ]
+    small[0].start()
     for copy in copies:
         copy.start(priority=1)
-    small.wait()
+    for copy in small[1:]:
+        copy.start()
+    small[0].wait()
     row = lax.broadcasted_iota(jnp.int32, (rows, samples), 0)
     sample = lax.broadcasted_iota(jnp.int32, (rows, samples), 1)
     number = jnp.zeros((rows, samples), jnp.float32)
@@ -109,6 +119,8 @@
             out = lax.dot_general(table, block, (((1,), (1,)), ((), ())), preferred_element_type=jnp.float32)
             for p in range(group):
                 tall[pl.ds((s + p) * rows, rows), :] = out[:, p * channels : (p + 1) * channels]
+    for copy in small[1:]:
+        copy.wait()
     for k in range(rows):
         picked = tall[pl.ds(k, snaps, stride=rows), :].astype(jnp.bfloat16)
         spectra_ref[pl.ds(k * snaps, snaps), :] = picked
@@ -142,12 +154,13 @@
     out = rest[-1]
     sums = rest[0] if last else out
     place = lax.axis_index("grid")
-    half = beams[0].shape[0]
+    counts = [beam.shape[0] for beam in beams]
+    bins = sum(counts)
     depth = blocks[0].shape[1]
     rows = sums.shape[2]
     snaps = rows // 2
-    for f in range(2 * half):
-        beam = beams[f // half]
+    for f in range(bins):
+        beam, at = (beams[0], f) if f < counts[0] else (beams[1], f - counts[0])
         totals = []
         for part in range(2):
             total = rest[0][f, part] if last else None
@@ -155,7 +168,7 @@
                 for i, mask in enumerate(inside):
                     start = pl.multiple_of((place ^ mask) * depth, depth)
                     term = jnp.dot(
-                        block[pl.ds((i * 2 * half + f) * rows, rows), :], beam[f % half, part, pl.ds(start, depth), :],
+                        block[pl.ds((i * bins + f) * rows, rows), :], beam[at, part, pl.ds(start, depth), :],
                         preferred_element_type=jnp.float32,
                     )
                     total = term if total is None else total + term
@@ -217,16 +230,16 @@
 
     chunks = 2
     bins_row = bins.reshape(1, all_bins)
-    spectra = call(
+    small = [pltpu.VMEM(v.shape, v.dtype) for v in (bins_row, sensor_coords, grid_coords)]
+    spectra, *tables = call(
         transform_kernel,
-        pltpu.VMEM((rows, channel_local), jnp.bfloat16),
-        [pltpu.with_memory_space_constraint(v, pltpu.HBM) for v in (bins_row, series)],
+        [pltpu.VMEM((rows, channel_local), jnp.bfloat16), *small],
+        [pltpu.with_memory_space_constraint(v, pltpu.HBM) for v in (bins_row, sensor_coords, grid_coords, series)],
         [
-            pltpu.VMEM((1, all_bins), jnp.int32),
             pltpu.VMEM(series.shape, jnp.bfloat16),
             pltpu.VMEM((rows, channel_local), jnp.float32),
             pltpu.SemaphoreType.DMA((chunks,)),
-            pltpu.SemaphoreType.DMA,
+            pltpu.SemaphoreType.DMA((3,)),
         ],
         near_inputs=False,
     )
@@ -238,25 +251,27 @@
         return call(stack_kernel, pltpu.VMEM((len(values) * rows, channel_local), jnp.bfloat16), near(*values))
 
     near_spectra = swap(spectra, "grid", 1)
+    corner = swap(spectra, "grid", 3)
+    late = [k for k in far if k != 1]
     beam_type = pltpu.VMEM((half, 2, channels, grid_local), jnp.bfloat16)
     squares_type = pltpu.VMEM((channels, grid_local), jnp.float32)
     rates_type = pltpu.VMEM((half, STEP, grid_local), jnp.float32)
     beam0, squares = call(
-        functools.partial(replica_kernel, range(half), samples, True),
-        [beam_type, squares_type], [bins_row, sensor_coords, grid_coords], [rates_type],
-    )
-    rest = swap(stack(*far.values()), "grid", 1)
+        functools.partial(replica_kernel, range(FIRST), samples, True),
+        [pltpu.VMEM((FIRST, 2, channels, grid_local), jnp.bfloat16), squares_type], near(*tables), [rates_type],
+    )
+    rest = swap(stack(*[far[k] for k in late]), "grid", 1)
     beam1 = call(
-        functools.partial(replica_kernel, range(half, all_bins), samples, False),
-        beam_type, [bins_row, sensor_coords, grid_coords, *near(squares)], [rates_type],
+        functools.partial(replica_kernel, range(FIRST, all_bins), samples, False),
+        pltpu.VMEM((all_bins - FIRST, 2, channels, grid_local), jnp.bfloat16), near(*tables, squares), [pltpu.VMEM((all_bins - FIRST, STEP, grid_local), jnp.float32)],
     )
     sums = call(
-        functools.partial(product_kernel, [[0], *[[2 * k] for k in far], [1]], False),
+        functools.partial(product_kernel, [[0], *[[2 * k] for k in far], [1], [3]], False),
         pltpu.VMEM((all_bins, 2, 2 * snap_local, grid_local), jnp.float32),
-        near(spectra, *far.values(), near_spectra, beam0, beam1),
+        near(spectra, *far.values(), near_spectra, corner, beam0, beam1),
     )
     total = call(
-        functools.partial(product_kernel, [[2 * k + 1 for k in far]], True),
+        functools.partial(product_kernel, [[2 * k + 1 for k in late]], True),
         pltpu.VMEM((all_bins, grid_local), jnp.float32),
         near(rest, beam0, beam1, sums),
     )
@@ -279,6 +294,9 @@
     return (bin_power, power.reshape(grid_local))
 
 
+FIRST = 1
+
+
 def solution(mesh):
     return jax.shard_map(
         on_device,

time: 27.9 us -> 28.6 us (1.025)
  starting transfers between devices: 10 us -> 12.8 us
  waiting for transfers between devices: 8.46 us -> 7.21 us
  Pallas kernels: 8.56 us -> 7.78 us
    ppermute x8 -> x9, starting transfers between devices: 10 us -> 12.8 us  [swap(): return lax.ppermute(value, axis, [(i, i ^ mask) for i in range(size)])]
    ppermute x8 -> x9, waiting for transfers between devices: 8.46 us -> 7.21 us  [swap(): return lax.ppermute(value, axis, [(i, i ^ mask) for i in range(size)])]
    pallas_call x7, Pallas kernels: 8.56 us -> 7.78 us  [call(): pl.pallas_call(kernel, out_shape=outs, in_specs=vmem(len(inputs)) if near...]
  transfers between devices with their start and end apart: 8 -> 9, of which waited for: 4 -> 4; matrix products, arithmetic and copies ran while one was open for 0% -> 0% of each run, Pallas kernels for 20% -> 17%
where the time goes in v6:
time: 28.6 us; the launch traced here: 28.5 us
  starting transfers between devices  12.8 us (45%)
  Pallas kernels  7.78 us (27%)
  waiting for transfers between devices  7.21 us (25%)
  between operations  0.71 us (2%)
    ppermute x9, starting transfers between devices, swap(): return lax.ppermute(value, axis, [(i, i ^ mask) for i in range(size)])  12.8 us
    pallas_call x7, Pallas kernels, call(): pl.pallas_call(kernel, out_shape=outs, in_specs=vmem(len(inputs)) if near...  7.78 us
    ppermute x9, waiting for transfers between devices, swap(): return lax.ppermute(value, axis, [(i, i ^ mask) for i in range(size)])  7.21 us
  transfers between devices with their start and end apart: 9, of which 4 were waited for; matrix products, arithmetic and copies ran while one was open for 0% of the time, Pallas kernels for 17%

profile of v6, /device:TPU:0, one launch (start us, length us, event | category | flops | bytes accessed | tf_op | source)
XLA Modules:
  0.0 28.5 jit_solution(17413673313521569823)
XLA Ops:
  0.6 2.1 %shard_map.59 = (bf16[256,128]{1,0:T(8,128)(2,1)S(1)}, s32[1,4]{1,0:T(1,128)S(1)}, s32[3,1024]{1,0:T(4,128)S(1)}, s32[3,256]{1,0:T(4,128)S(1)}) custom-call(s32[1,4]{1,0:T(1,128)} %bitcast.2, s32[3,1024]{1,0:T(4,128)} %sensors_far.1, s32[3,256]{1,0:T(4,128)} %points_far.1, bf16[32,128,256]{2,1,0:T(8,128)(2,1)} %series_ref.1), custom_call_target="tpu_custom_call" | custom-call | tf_op jit(solution)/shard_map/pallas_call | solution.py:221
  2.8 4.1 %collective-permute-start = (bf16[256,128]{1,0:T(8,128)(2,1)S(1)}, bf16[256,128]{1,0:T(8,128)(2,1)S(1)}, u32[]{:S(2)}, u32[]{:S(2)}) collective-permute-start(bf16[256,128]{1,0:T(8,128)(2,1)S(1)} %get-tuple-element.10.refs_0_), channel_id=1, source_target_pairs={{0,4},{1,5},{2,6},{3,7},{4,0},{5,1},{6,2},{7,3},{8,12},{9,13},{10,... | collective-permute-start | bytes 196616 | tf_op jit(solution)/shard_map/ppermute | solution.py:217
  6.9 1.3 %collective-permute-start.1 = (bf16[256,128]{1,0:T(8,128)(2,1)S(1)}, bf16[256,128]{1,0:T(8,128)(2,1)S(1)}, u32[]{:S(2)}, u32[]{:S(2)}) collective-permute-start(bf16[256,128]{1,0:T(8,128)(2,1)S(1)} %get-tuple-element.10.refs_0_), channel_id=1, source_target_pairs={{0,6},{1,7},{2,4},{3,5},{4,2},{5,3},{6,0},{7,1},{8,14},{9,15},{10,... | collective-permute-start | bytes 196616 | tf_op jit(solution)/shard_map/ppermute | solution.py:217
  8.2 2.4 %collective-permute-done.refs_0_.refs_2_ = bf16[256,128]{1,0:T(8,128)(2,1)S(1)} collective-permute-done((bf16[256,128]{1,0:T(8,128)(2,1)S(1)}, bf16[256,128]{1,0:T(8,128)(2,1)S(1)}, u32[]{:S(2)}, u32[]{:S(2)}) %collective-permute-start) | collective-permute-done | bytes 65568 | tf_op jit(solution)/shard_map/ppermute | solution.py:217
  10.6 2.5 %collective-permute-done.1.refs_1_.refs_3_ = bf16[256,128]{1,0:T(8,128)(2,1)S(1)} collective-permute-done((bf16[256,128]{1,0:T(8,128)(2,1)S(1)}, bf16[256,128]{1,0:T(8,128)(2,1)S(1)}, u32[]{:S(2)}, u32[]{:S(2)}) %collective-permute-start.1) | collective-permute-done | bytes 65568 | tf_op jit(solution)/shard_map/ppermute | solution.py:217
  13.1 1.6 %collective-permute-start.2 = (bf16[512,128]{1,0:T(8,128)(2,1)S(1)}, bf16[512,128]{1,0:T(8,128)(2,1)S(1)}, u32[]{:S(2)}, u32[]{:S(2)}) collective-permute-start(bf16[512,128]{1,0:T(8,128)(2,1)S(1)} %shard_map.60), channel_id=1, source_target_pairs={{0,1},{1,0},{2,3},{3,2},{4,5},{5,4},{6,7},{7,6},{8,9},{9,8},{10,11... | collective-permute-start | bytes 393224 | tf_op jit(solution)/shard_map/ppermute | solution.py:217
  14.7 1.1 %collective-permute-start.3 = (bf16[256,128]{1,0:T(8,128)(2,1)S(1)}, bf16[256,128]{1,0:T(8,128)(2,1)S(1)}, u32[]{:S(2)}, u32[]{:S(2)}) collective-permute-start(bf16[256,128]{1,0:T(8,128)(2,1)S(1)} %get-tuple-element.10.refs_0_), channel_id=1, source_target_pairs={{0,2},{1,3},{2,0},{3,1},{4,6},{5,7},{6,4},{7,5},{8,10},{9,11},{10,... | collective-permute-start | bytes 196616 | tf_op jit(solution)/shard_map/ppermute | solution.py:217
  15.7 0.3 %collective-permute-start.4 = (bf16[256,128]{1,0:T(8,128)(2,1)S(1)}, bf16[256,128]{1,0:T(8,128)(2,1)S(1)}, u32[]{:S(2)}, u32[]{:S(2)}) collective-permute-start(bf16[256,128]{1,0:T(8,128)(2,1)S(1)} %get-tuple-element.10.refs_0_), channel_id=1, source_target_pairs={{0,1},{1,0},{2,3},{3,2},{4,5},{5,4},{6,7},{7,6},{8,9},{9,8},{10,11... | collective-permute-start | bytes 196616 | tf_op jit(solution)/shard_map/ppermute | solution.py:217
  16.0 2.1 %collective-permute-start.5 = (bf16[256,128]{1,0:T(8,128)(2,1)S(1)}, bf16[256,128]{1,0:T(8,128)(2,1)S(1)}, u32[]{:S(2)}, u32[]{:S(2)}) collective-permute-start(bf16[256,128]{1,0:T(8,128)(2,1)S(1)} %get-tuple-element.10.refs_0_), channel_id=1, source_target_pairs={{0,3},{1,2},{2,1},{3,0},{4,7},{5,6},{6,5},{7,4},{8,11},{9,10},{10,... | collective-permute-start | bytes 196616 | tf_op jit(solution)/shard_map/ppermute | solution.py:217
  18.1 1.4 %shard_map.61 = (bf16[1,2,1024,256]{3,2,1,0:T(8,128)(2,1)S(1)}, f32[1024,256]{1,0:T(8,128)S(1)}) custom-call(s32[1,4]{1,0:T(1,128)S(1)} %get-tuple-element.11.bins_ref, s32[3,1024]{1,0:T(4,128)S(1)} %get-tuple-element.12.sensors_ref, s32[3,256]{1,0:T(4,128)S(1)} %get-tuple-element.13.points_ref), custom_call_target="tpu_custom_call" | custom-call | tf_op jit(solution)/shard_map/pallas_call | solution.py:221
  19.6 2.7 %shard_map.62.refs_7_.refs_2_ = bf16[3,2,1024,256]{3,2,1,0:T(8,128)(2,1)S(1)} custom-call(s32[1,4]{1,0:T(1,128)S(1)} %get-tuple-element.11.bins_ref, s32[3,1024]{1,0:T(4,128)S(1)} %get-tuple-element.12.sensors_ref, s32[3,256]{1,0:T(4,128)S(1)} %get-tuple-element.13.points_ref, f32[1024,256]{1,0:T(8,128)S(1)} %get-tuple-element.15.refs_0_), custom_call_target="tpu_custom_call" | custom-call | tf_op jit(solution)/shard_map/pallas_call | solution.py:221
  22.3 0.0 collective-permute-done.3.refs_1_
  22.3 0.0 collective-permute-done.4.refs_4_
  22.3 0.0 collective-permute-done.5.refs_5_
  22.4 0.6 %shard_map.63.refs_3_ = f32[4,2,64,256]{3,2,1,0:T(8,128)S(1)} custom-call(bf16[256,128]{1,0:T(8,128)(2,1)S(1)} %get-tuple-element.10.refs_0_, bf16[256,128]{1,0:T(8,128)(2,1)S(1)} %collective-permute-done.3.refs_1_, bf16[256,128]{1,0:T(8,128)(2,1)S(1)} %collective-permute-done.refs_0_.refs_2_, bf16[256,128]{1,0:T(8,128)(2,1)S(1)} %collective-permute-done.1.refs_1_.refs_3_, ...), custom_call_target="tpu_custom_call" | custom-call | tf_op jit(solution)/shard_map/pallas_call | solution.py:221
  22.9 0.0 collective-permute-done.2.refs_0_
  23.0 0.3 %shard_map.64.mine_ref = f32[4,256]{1,0:T(4,128)S(1)} custom-call(bf16[512,128]{1,0:T(8,128)(2,1)S(1)} %collective-permute-done.2.refs_0_, bf16[1,2,1024,256]{3,2,1,0:T(8,128)(2,1)S(1)} %get-tuple-element.14.refs_6_.refs_1_, bf16[3,2,1024,256]{3,2,1,0:T(8,128)(2,1)S(1)} %shard_map.62.refs_7_.refs_2_, f32[4,2,64,256]{3,2,1,0:T(8,128)S(1)} %shard_map.63.refs_3_), custom_call_target="tpu_custom_call" | custom-call | tf_op jit(solution)/shard_map/pallas_call | solution.py:221
  23.3 1.6 %collective-permute-start.6 = (f32[4,256]{1,0:T(4,128)S(1)}, f32[4,256]{1,0:T(4,128)S(1)}, u32[]{:S(2)}, u32[]{:S(2)}) collective-permute-start(f32[4,256]{1,0:T(4,128)S(1)} %shard_map.64.mine_ref), channel_id=1, source_target_pairs={{0,16},{8,24},{16,0},{24,8},{1,17},{9,25},{17,1},{25,9},{2,18},{10... | collective-permute-start | bytes 12296 | tf_op jit(solution)/shard_map/ppermute | solution.py:217
  24.8 0.0 collective-permute-start.7
  24.8 0.6 %collective-permute-start.8 = (f32[4,256]{1,0:T(4,128)S(1)}, f32[4,256]{1,0:T(4,128)S(1)}, u32[]{:S(2)}, u32[]{:S(2)}) collective-permute-start(f32[4,256]{1,0:T(4,128)S(1)} %shard_map.64.mine_ref), channel_id=1, source_target_pairs={{0,8},{8,0},{16,24},{24,16},{1,9},{9,1},{17,25},{25,17},{2,10},{10... | collective-permute-start | bytes 12296 | tf_op jit(solution)/shard_map/ppermute | solution.py:217
  25.5 1.5 %collective-permute-done.6.second_ref = f32[4,256]{1,0:T(4,128)S(1)} collective-permute-done((f32[4,256]{1,0:T(4,128)S(1)}, f32[4,256]{1,0:T(4,128)S(1)}, u32[]{:S(2)}, u32[]{:S(2)}) %collective-permute-start.6) | collective-permute-done | bytes 4128 | tf_op jit(solution)/shard_map/ppermute | solution.py:217
  27.0 0.9 %collective-permute-done.7.third_ref = f32[4,256]{1,0:T(4,128)S(1)} collective-permute-done((f32[4,256]{1,0:T(4,128)S(1)}, f32[4,256]{1,0:T(4,128)S(1)}, u32[]{:S(2)}, u32[]{:S(2)}) %collective-permute-start.7) | collective-permute-done | bytes 4128 | tf_op jit(solution)/shard_map/ppermute | solution.py:217
  27.9 0.0 collective-permute-done.8.fourth_ref
  27.9 0.6 %shard_map.65 = (f32[1,256]{1,0:T(1,128)}, f32[1,256]{1,0:T(1,128)}) custom-call(f32[4,256]{1,0:T(4,128)S(1)} %shard_map.64.mine_ref, f32[4,256]{1,0:T(4,128)S(1)} %collective-permute-done.6.second_ref, f32[4,256]{1,0:T(4,128)S(1)} %collective-permute-done.7.third_ref, f32[4,256]{1,0:T(4,128)S(1)} %collective-permute-done.8.fourth_ref), custom_call_target="tpu_custom_call" | custom-call | tf_op jit(solution)/shard_map/pallas_call | solution.py:221
  (1 shorter events, 0.0 us)
Async XLA Ops:
  2.8 7.8 %collective-permute-start = (bf16[256,128]{1,0:T(8,128)(2,1)S(1)}, bf16[256,128]{1,0:T(8,128)(2,1)S(1)}, u32[]{:S(2)}, u32[]{:S(2)}) collective-permute-start(bf16[256,128]{1,0:T(8,128)(2,1)S(1)} %get-tuple-element.10.refs_0_), channel_id=1, source_target_pairs={{0,4},{1,5},{2,6},{3,7},{4,0},{5,1},{6,2},{7,3},{8,12},{9,13},{10,... | collective-permute-start | bytes 196616 | tf_op jit(solution)/shard_map/ppermute | solution.py:217
  6.9 6.2 %collective-permute-start.1 = (bf16[256,128]{1,0:T(8,128)(2,1)S(1)}, bf16[256,128]{1,0:T(8,128)(2,1)S(1)}, u32[]{:S(2)}, u32[]{:S(2)}) collective-permute-start(bf16[256,128]{1,0:T(8,128)(2,1)S(1)} %get-tuple-element.10.refs_0_), channel_id=1, source_target_pairs={{0,6},{1,7},{2,4},{3,5},{4,2},{5,3},{6,0},{7,1},{8,14},{9,15},{10,... | collective-permute-start | bytes 196616 | tf_op jit(solution)/shard_map/ppermute | solution.py:217
  13.1 9.9 %collective-permute-start.2 = (bf16[512,128]{1,0:T(8,128)(2,1)S(1)}, bf16[512,128]{1,0:T(8,128)(2,1)S(1)}, u32[]{:S(2)}, u32[]{:S(2)}) collective-permute-start(bf16[512,128]{1,0:T(8,128)(2,1)S(1)} %shard_map.60), channel_id=1, source_target_pairs={{0,1},{1,0},{2,3},{3,2},{4,5},{5,4},{6,7},{7,6},{8,9},{9,8},{10,11... | collective-permute-start | bytes 393224 | tf_op jit(solution)/shard_map/ppermute | solution.py:217
  14.7 7.7 %collective-permute-start.3 = (bf16[256,128]{1,0:T(8,128)(2,1)S(1)}, bf16[256,128]{1,0:T(8,128)(2,1)S(1)}, u32[]{:S(2)}, u32[]{:S(2)}) collective-permute-start(bf16[256,128]{1,0:T(8,128)(2,1)S(1)} %get-tuple-element.10.refs_0_), channel_id=1, source_target_pairs={{0,2},{1,3},{2,0},{3,1},{4,6},{5,7},{6,4},{7,5},{8,10},{9,11},{10,... | collective-permute-start | bytes 196616 | tf_op jit(solution)/shard_map/ppermute | solution.py:217
  15.7 6.6 %collective-permute-start.4 = (bf16[256,128]{1,0:T(8,128)(2,1)S(1)}, bf16[256,128]{1,0:T(8,128)(2,1)S(1)}, u32[]{:S(2)}, u32[]{:S(2)}) collective-permute-start(bf16[256,128]{1,0:T(8,128)(2,1)S(1)} %get-tuple-element.10.refs_0_), channel_id=1, source_target_pairs={{0,1},{1,0},{2,3},{3,2},{4,5},{5,4},{6,7},{7,6},{8,9},{9,8},{10,11... | collective-permute-start | bytes 196616 | tf_op jit(solution)/shard_map/ppermute | solution.py:217
  16.0 6.3 %collective-permute-start.5 = (bf16[256,128]{1,0:T(8,128)(2,1)S(1)}, bf16[256,128]{1,0:T(8,128)(2,1)S(1)}, u32[]{:S(2)}, u32[]{:S(2)}) collective-permute-start(bf16[256,128]{1,0:T(8,128)(2,1)S(1)} %get-tuple-element.10.refs_0_), channel_id=1, source_target_pairs={{0,3},{1,2},{2,1},{3,0},{4,7},{5,6},{6,5},{7,4},{8,11},{9,10},{10,... | collective-permute-start | bytes 196616 | tf_op jit(solution)/shard_map/ppermute | solution.py:217
  23.3 3.7 %collective-permute-start.6 = (f32[4,256]{1,0:T(4,128)S(1)}, f32[4,256]{1,0:T(4,128)S(1)}, u32[]{:S(2)}, u32[]{:S(2)}) collective-permute-start(f32[4,256]{1,0:T(4,128)S(1)} %shard_map.64.mine_ref), channel_id=1, source_target_pairs={{0,16},{8,24},{16,0},{24,8},{1,17},{9,25},{17,1},{25,9},{2,18},{10... | collective-permute-start | bytes 12296 | tf_op jit(solution)/shard_map/ppermute | solution.py:217
  24.8 3.0 %collective-permute-start.7 = (f32[4,256]{1,0:T(4,128)S(1)}, f32[4,256]{1,0:T(4,128)S(1)}, u32[]{:S(2)}, u32[]{:S(2)}) collective-permute-start(f32[4,256]{1,0:T(4,128)S(1)} %shard_map.64.mine_ref), channel_id=1, source_target_pairs={{0,24},{8,16},{16,8},{24,0},{1,25},{9,17},{17,9},{25,1},{2,26},{10... | collective-permute-start | bytes 12296 | tf_op jit(solution)/shard_map/ppermute | solution.py:217
  24.8 3.0 %collective-permute-start.8 = (f32[4,256]{1,0:T(4,128)S(1)}, f32[4,256]{1,0:T(4,128)S(1)}, u32[]{:S(2)}, u32[]{:S(2)}) collective-permute-start(f32[4,256]{1,0:T(4,128)S(1)} %shard_map.64.mine_ref), channel_id=1, source_target_pairs={{0,8},{8,0},{16,24},{24,16},{1,9},{9,1},{17,25},{25,17},{2,10},{10... | collective-permute-start | bytes 12296 | tf_op jit(solution)/shard_map/ppermute | solution.py:217

commit v7 on v6

--- a/solution.py
+++ b/solution.py
@@ -56,7 +56,7 @@
     return lax.dot_general(left, right, (((1,), (0,)), ((), ())), preferred_element_type=jnp.float32)
 
 
-STEP = 64
+STEP = 128
 TOGETHER = 1
 
 
@@ -97,11 +97,10 @@
         pltpu.make_async_copy(a, b, small_sems.at[i])
         for i, (a, b) in enumerate([(bins_far, bins_ref), (sensors_far, sensors_ref), (points_far, points_ref)])
     ]
-    small[0].start()
+    for copy in small:
+        copy.start()
     for copy in copies:
         copy.start(priority=1)
-    for copy in small[1:]:
-        copy.start()
     small[0].wait()
     row = lax.broadcasted_iota(jnp.int32, (rows, samples), 0)
     sample = lax.broadcasted_iota(jnp.int32, (rows, samples), 1)

time: 28.6 us -> 28.4 us (level)
  transfers between devices with their start and end apart: 9 -> 9, of which waited for: 4 -> 4; matrix products, arithmetic and copies ran while one was open for 0% -> 0% of each run, Pallas kernels for 17% -> 16%
where the time goes in v7:
time: 28.4 us; the launch traced here: 28.3 us
  starting transfers between devices  12.8 us (45%)
  Pallas kernels  7.58 us (27%)
  waiting for transfers between devices  7.2 us (25%)
  between operations  0.71 us (2%)
    ppermute x9, starting transfers between devices, swap(): return lax.ppermute(value, axis, [(i, i ^ mask) for i in range(size)])  12.8 us
    pallas_call x7, Pallas kernels, call(): pl.pallas_call(kernel, out_shape=outs, in_specs=vmem(len(inputs)) if near...  7.58 us
    ppermute x9, waiting for transfers between devices, swap(): return lax.ppermute(value, axis, [(i, i ^ mask) for i in range(size)])  7.2 us
  transfers between devices with their start and end apart: 9, of which 4 were waited for; matrix products, arithmetic and copies ran while one was open for 0% of the time, Pallas kernels for 16%

profile of v7, /device:TPU:0, one launch (start us, length us, event | category | flops | bytes accessed | tf_op | source)
XLA Modules:
  0.0 28.3 jit_solution(3572341936767820284)
XLA Ops:
  0.6 2.1 %shard_map.59 = (bf16[256,128]{1,0:T(8,128)(2,1)S(1)}, s32[1,4]{1,0:T(1,128)S(1)}, s32[3,1024]{1,0:T(4,128)S(1)}, s32[3,256]{1,0:T(4,128)S(1)}) custom-call(s32[1,4]{1,0:T(1,128)} %bitcast.2, s32[3,1024]{1,0:T(4,128)} %sensors_far.1, s32[3,256]{1,0:T(4,128)} %points_far.1, bf16[32,128,256]{2,1,0:T(8,128)(2,1)} %series_ref.1), custom_call_target="tpu_custom_call" | custom-call | tf_op jit(solution)/shard_map/pallas_call | solution.py:220
  2.8 4.1 %collective-permute-start = (bf16[256,128]{1,0:T(8,128)(2,1)S(1)}, bf16[256,128]{1,0:T(8,128)(2,1)S(1)}, u32[]{:S(2)}, u32[]{:S(2)}) collective-permute-start(bf16[256,128]{1,0:T(8,128)(2,1)S(1)} %get-tuple-element.10.refs_0_), channel_id=1, source_target_pairs={{0,4},{1,5},{2,6},{3,7},{4,0},{5,1},{6,2},{7,3},{8,12},{9,13},{10,... | collective-permute-start | bytes 196616 | tf_op jit(solution)/shard_map/ppermute | solution.py:216
  6.9 1.3 %collective-permute-start.1 = (bf16[256,128]{1,0:T(8,128)(2,1)S(1)}, bf16[256,128]{1,0:T(8,128)(2,1)S(1)}, u32[]{:S(2)}, u32[]{:S(2)}) collective-permute-start(bf16[256,128]{1,0:T(8,128)(2,1)S(1)} %get-tuple-element.10.refs_0_), channel_id=1, source_target_pairs={{0,6},{1,7},{2,4},{3,5},{4,2},{5,3},{6,0},{7,1},{8,14},{9,15},{10,... | collective-permute-start | bytes 196616 | tf_op jit(solution)/shard_map/ppermute | solution.py:216
  8.2 2.4 %collective-permute-done.refs_0_.refs_2_ = bf16[256,128]{1,0:T(8,128)(2,1)S(1)} collective-permute-done((bf16[256,128]{1,0:T(8,128)(2,1)S(1)}, bf16[256,128]{1,0:T(8,128)(2,1)S(1)}, u32[]{:S(2)}, u32[]{:S(2)}) %collective-permute-start) | collective-permute-done | bytes 65568 | tf_op jit(solution)/shard_map/ppermute | solution.py:216
  10.6 2.5 %collective-permute-done.1.refs_1_.refs_3_ = bf16[256,128]{1,0:T(8,128)(2,1)S(1)} collective-permute-done((bf16[256,128]{1,0:T(8,128)(2,1)S(1)}, bf16[256,128]{1,0:T(8,128)(2,1)S(1)}, u32[]{:S(2)}, u32[]{:S(2)}) %collective-permute-start.1) | collective-permute-done | bytes 65568 | tf_op jit(solution)/shard_map/ppermute | solution.py:216
  13.1 1.6 %collective-permute-start.2 = (bf16[512,128]{1,0:T(8,128)(2,1)S(1)}, bf16[512,128]{1,0:T(8,128)(2,1)S(1)}, u32[]{:S(2)}, u32[]{:S(2)}) collective-permute-start(bf16[512,128]{1,0:T(8,128)(2,1)S(1)} %shard_map.60), channel_id=1, source_target_pairs={{0,1},{1,0},{2,3},{3,2},{4,5},{5,4},{6,7},{7,6},{8,9},{9,8},{10,11... | collective-permute-start | bytes 393224 | tf_op jit(solution)/shard_map/ppermute | solution.py:216
  14.7 1.1 %collective-permute-start.3 = (bf16[256,128]{1,0:T(8,128)(2,1)S(1)}, bf16[256,128]{1,0:T(8,128)(2,1)S(1)}, u32[]{:S(2)}, u32[]{:S(2)}) collective-permute-start(bf16[256,128]{1,0:T(8,128)(2,1)S(1)} %get-tuple-element.10.refs_0_), channel_id=1, source_target_pairs={{0,2},{1,3},{2,0},{3,1},{4,6},{5,7},{6,4},{7,5},{8,10},{9,11},{10,... | collective-permute-start | bytes 196616 | tf_op jit(solution)/shard_map/ppermute | solution.py:216
  15.7 0.3 %collective-permute-start.4 = (bf16[256,128]{1,0:T(8,128)(2,1)S(1)}, bf16[256,128]{1,0:T(8,128)(2,1)S(1)}, u32[]{:S(2)}, u32[]{:S(2)}) collective-permute-start(bf16[256,128]{1,0:T(8,128)(2,1)S(1)} %get-tuple-element.10.refs_0_), channel_id=1, source_target_pairs={{0,1},{1,0},{2,3},{3,2},{4,5},{5,4},{6,7},{7,6},{8,9},{9,8},{10,11... | collective-permute-start | bytes 196616 | tf_op jit(solution)/shard_map/ppermute | solution.py:216
  16.0 2.1 %collective-permute-start.5 = (bf16[256,128]{1,0:T(8,128)(2,1)S(1)}, bf16[256,128]{1,0:T(8,128)(2,1)S(1)}, u32[]{:S(2)}, u32[]{:S(2)}) collective-permute-start(bf16[256,128]{1,0:T(8,128)(2,1)S(1)} %get-tuple-element.10.refs_0_), channel_id=1, source_target_pairs={{0,3},{1,2},{2,1},{3,0},{4,7},{5,6},{6,5},{7,4},{8,11},{9,10},{10,... | collective-permute-start | bytes 196616 | tf_op jit(solution)/shard_map/ppermute | solution.py:216
  18.1 1.4 %shard_map.61 = (bf16[1,2,1024,256]{3,2,1,0:T(8,128)(2,1)S(1)}, f32[1024,256]{1,0:T(8,128)S(1)}) custom-call(s32[1,4]{1,0:T(1,128)S(1)} %get-tuple-element.11.bins_ref, s32[3,1024]{1,0:T(4,128)S(1)} %get-tuple-element.12.sensors_ref, s32[3,256]{1,0:T(4,128)S(1)} %get-tuple-element.13.points_ref), custom_call_target="tpu_custom_call" | custom-call | tf_op jit(solution)/shard_map/pallas_call | solution.py:220
  19.5 2.6 %shard_map.62.refs_7_.refs_2_ = bf16[3,2,1024,256]{3,2,1,0:T(8,128)(2,1)S(1)} custom-call(s32[1,4]{1,0:T(1,128)S(1)} %get-tuple-element.11.bins_ref, s32[3,1024]{1,0:T(4,128)S(1)} %get-tuple-element.12.sensors_ref, s32[3,256]{1,0:T(4,128)S(1)} %get-tuple-element.13.points_ref, f32[1024,256]{1,0:T(8,128)S(1)} %get-tuple-element.15.refs_0_), custom_call_target="tpu_custom_call" | custom-call | tf_op jit(solution)/shard_map/pallas_call | solution.py:220
  22.1 0.0 collective-permute-done.3.refs_1_
  22.1 0.0 collective-permute-done.4.refs_4_
  22.1 0.0 collective-permute-done.5.refs_5_
  22.2 0.6 %shard_map.63.refs_3_ = f32[4,2,64,256]{3,2,1,0:T(8,128)S(1)} custom-call(bf16[256,128]{1,0:T(8,128)(2,1)S(1)} %get-tuple-element.10.refs_0_, bf16[256,128]{1,0:T(8,128)(2,1)S(1)} %collective-permute-done.3.refs_1_, bf16[256,128]{1,0:T(8,128)(2,1)S(1)} %collective-permute-done.refs_0_.refs_2_, bf16[256,128]{1,0:T(8,128)(2,1)S(1)} %collective-permute-done.1.refs_1_.refs_3_, ...), custom_call_target="tpu_custom_call" | custom-call | tf_op jit(solution)/shard_map/pallas_call | solution.py:220
  22.7 0.0 collective-permute-done.2.refs_0_
  22.8 0.3 %shard_map.64.mine_ref = f32[4,256]{1,0:T(4,128)S(1)} custom-call(bf16[512,128]{1,0:T(8,128)(2,1)S(1)} %collective-permute-done.2.refs_0_, bf16[1,2,1024,256]{3,2,1,0:T(8,128)(2,1)S(1)} %get-tuple-element.14.refs_6_.refs_1_, bf16[3,2,1024,256]{3,2,1,0:T(8,128)(2,1)S(1)} %shard_map.62.refs_7_.refs_2_, f32[4,2,64,256]{3,2,1,0:T(8,128)S(1)} %shard_map.63.refs_3_), custom_call_target="tpu_custom_call" | custom-call | tf_op jit(solution)/shard_map/pallas_call | solution.py:220
  23.1 1.5 %collective-permute-start.6 = (f32[4,256]{1,0:T(4,128)S(1)}, f32[4,256]{1,0:T(4,128)S(1)}, u32[]{:S(2)}, u32[]{:S(2)}) collective-permute-start(f32[4,256]{1,0:T(4,128)S(1)} %shard_map.64.mine_ref), channel_id=1, source_target_pairs={{0,16},{8,24},{16,0},{24,8},{1,17},{9,25},{17,1},{25,9},{2,18},{10... | collective-permute-start | bytes 12296 | tf_op jit(solution)/shard_map/ppermute | solution.py:216
  24.6 0.0 collective-permute-start.7
  24.6 0.7 %collective-permute-start.8 = (f32[4,256]{1,0:T(4,128)S(1)}, f32[4,256]{1,0:T(4,128)S(1)}, u32[]{:S(2)}, u32[]{:S(2)}) collective-permute-start(f32[4,256]{1,0:T(4,128)S(1)} %shard_map.64.mine_ref), channel_id=1, source_target_pairs={{0,8},{8,0},{16,24},{24,16},{1,9},{9,1},{17,25},{25,17},{2,10},{10... | collective-permute-start | bytes 12296 | tf_op jit(solution)/shard_map/ppermute | solution.py:216
  25.3 1.5 %collective-permute-done.6.second_ref = f32[4,256]{1,0:T(4,128)S(1)} collective-permute-done((f32[4,256]{1,0:T(4,128)S(1)}, f32[4,256]{1,0:T(4,128)S(1)}, u32[]{:S(2)}, u32[]{:S(2)}) %collective-permute-start.6) | collective-permute-done | bytes 4128 | tf_op jit(solution)/shard_map/ppermute | solution.py:216
  26.8 0.9 %collective-permute-done.7.third_ref = f32[4,256]{1,0:T(4,128)S(1)} collective-permute-done((f32[4,256]{1,0:T(4,128)S(1)}, f32[4,256]{1,0:T(4,128)S(1)}, u32[]{:S(2)}, u32[]{:S(2)}) %collective-permute-start.7) | collective-permute-done | bytes 4128 | tf_op jit(solution)/shard_map/ppermute | solution.py:216
  27.7 0.0 collective-permute-done.8.fourth_ref
  27.7 0.6 %shard_map.65 = (f32[1,256]{1,0:T(1,128)}, f32[1,256]{1,0:T(1,128)}) custom-call(f32[4,256]{1,0:T(4,128)S(1)} %shard_map.64.mine_ref, f32[4,256]{1,0:T(4,128)S(1)} %collective-permute-done.6.second_ref, f32[4,256]{1,0:T(4,128)S(1)} %collective-permute-done.7.third_ref, f32[4,256]{1,0:T(4,128)S(1)} %collective-permute-done.8.fourth_ref), custom_call_target="tpu_custom_call" | custom-call | tf_op jit(solution)/shard_map/pallas_call | solution.py:220
  (1 shorter events, 0.0 us)
Async XLA Ops:
  2.8 7.8 %collective-permute-start = (bf16[256,128]{1,0:T(8,128)(2,1)S(1)}, bf16[256,128]{1,0:T(8,128)(2,1)S(1)}, u32[]{:S(2)}, u32[]{:S(2)}) collective-permute-start(bf16[256,128]{1,0:T(8,128)(2,1)S(1)} %get-tuple-element.10.refs_0_), channel_id=1, source_target_pairs={{0,4},{1,5},{2,6},{3,7},{4,0},{5,1},{6,2},{7,3},{8,12},{9,13},{10,... | collective-permute-start | bytes 196616 | tf_op jit(solution)/shard_map/ppermute | solution.py:216
  6.9 6.2 %collective-permute-start.1 = (bf16[256,128]{1,0:T(8,128)(2,1)S(1)}, bf16[256,128]{1,0:T(8,128)(2,1)S(1)}, u32[]{:S(2)}, u32[]{:S(2)}) collective-permute-start(bf16[256,128]{1,0:T(8,128)(2,1)S(1)} %get-tuple-element.10.refs_0_), channel_id=1, source_target_pairs={{0,6},{1,7},{2,4},{3,5},{4,2},{5,3},{6,0},{7,1},{8,14},{9,15},{10,... | collective-permute-start | bytes 196616 | tf_op jit(solution)/shard_map/ppermute | solution.py:216
  13.1 9.7 %collective-permute-start.2 = (bf16[512,128]{1,0:T(8,128)(2,1)S(1)}, bf16[512,128]{1,0:T(8,128)(2,1)S(1)}, u32[]{:S(2)}, u32[]{:S(2)}) collective-permute-start(bf16[512,128]{1,0:T(8,128)(2,1)S(1)} %shard_map.60), channel_id=1, source_target_pairs={{0,1},{1,0},{2,3},{3,2},{4,5},{5,4},{6,7},{7,6},{8,9},{9,8},{10,11... | collective-permute-start | bytes 393224 | tf_op jit(solution)/shard_map/ppermute | solution.py:216
  14.7 7.5 %collective-permute-start.3 = (bf16[256,128]{1,0:T(8,128)(2,1)S(1)}, bf16[256,128]{1,0:T(8,128)(2,1)S(1)}, u32[]{:S(2)}, u32[]{:S(2)}) collective-permute-start(bf16[256,128]{1,0:T(8,128)(2,1)S(1)} %get-tuple-element.10.refs_0_), channel_id=1, source_target_pairs={{0,2},{1,3},{2,0},{3,1},{4,6},{5,7},{6,4},{7,5},{8,10},{9,11},{10,... | collective-permute-start | bytes 196616 | tf_op jit(solution)/shard_map/ppermute | solution.py:216
  15.7 6.4 %collective-permute-start.4 = (bf16[256,128]{1,0:T(8,128)(2,1)S(1)}, bf16[256,128]{1,0:T(8,128)(2,1)S(1)}, u32[]{:S(2)}, u32[]{:S(2)}) collective-permute-start(bf16[256,128]{1,0:T(8,128)(2,1)S(1)} %get-tuple-element.10.refs_0_), channel_id=1, source_target_pairs={{0,1},{1,0},{2,3},{3,2},{4,5},{5,4},{6,7},{7,6},{8,9},{9,8},{10,11... | collective-permute-start | bytes 196616 | tf_op jit(solution)/shard_map/ppermute | solution.py:216
  16.0 6.1 %collective-permute-start.5 = (bf16[256,128]{1,0:T(8,128)(2,1)S(1)}, bf16[256,128]{1,0:T(8,128)(2,1)S(1)}, u32[]{:S(2)}, u32[]{:S(2)}) collective-permute-start(bf16[256,128]{1,0:T(8,128)(2,1)S(1)} %get-tuple-element.10.refs_0_), channel_id=1, source_target_pairs={{0,3},{1,2},{2,1},{3,0},{4,7},{5,6},{6,5},{7,4},{8,11},{9,10},{10,... | collective-permute-start | bytes 196616 | tf_op jit(solution)/shard_map/ppermute | solution.py:216
  23.1 3.7 %collective-permute-start.6 = (f32[4,256]{1,0:T(4,128)S(1)}, f32[4,256]{1,0:T(4,128)S(1)}, u32[]{:S(2)}, u32[]{:S(2)}) collective-permute-start(f32[4,256]{1,0:T(4,128)S(1)} %shard_map.64.mine_ref), channel_id=1, source_target_pairs={{0,16},{8,24},{16,0},{24,8},{1,17},{9,25},{17,1},{25,9},{2,18},{10... | collective-permute-start | bytes 12296 | tf_op jit(solution)/shard_map/ppermute | solution.py:216
  24.6 3.0 %collective-permute-start.7 = (f32[4,256]{1,0:T(4,128)S(1)}, f32[4,256]{1,0:T(4,128)S(1)}, u32[]{:S(2)}, u32[]{:S(2)}) collective-permute-start(f32[4,256]{1,0:T(4,128)S(1)} %shard_map.64.mine_ref), channel_id=1, source_target_pairs={{0,24},{8,16},{16,8},{24,0},{1,25},{9,17},{17,9},{25,1},{2,26},{10... | collective-permute-start | bytes 12296 | tf_op jit(solution)/shard_map/ppermute | solution.py:216
  24.6 3.0 %collective-permute-start.8 = (f32[4,256]{1,0:T(4,128)S(1)}, f32[4,256]{1,0:T(4,128)S(1)}, u32[]{:S(2)}, u32[]{:S(2)}) collective-permute-start(f32[4,256]{1,0:T(4,128)S(1)} %shard_map.64.mine_ref), channel_id=1, source_target_pairs={{0,8},{8,0},{16,24},{24,16},{1,9},{9,1},{17,25},{25,17},{2,10},{10... | collective-permute-start | bytes 12296 | tf_op jit(solution)/shard_map/ppermute | solution.py:216
